TPU v7x, 32 devices: a whole 2x2x4 slice. The times are simulated.
32 devices in a mesh: grp: 4 (over z), tile: 8 (over y, x, core).
Axes of the slice: x: 2, y: 2, z: 4, core: 2. Of those that a mesh axis runs over, the one named last changes fastest.
Arguments:
- cotangent: bfloat16 [1, 32, 48, 128, 128], P(None, None, 'grp', 'tile'), may hold values from -6 to 6
- deriv_two: bfloat16 [1, 32, 48, 128, 128], P(None, None, 'grp', 'tile'), may hold values from -0.099609375 to 1.09375
- deriv_one: bfloat16 [1, 32, 48, 128, 128], P(None, None, 'grp', 'tile'), may hold values from -0.099609375 to 1.09375
- point_two: bfloat16 [32, 32], replicated, may hold values from -1 to 1
- point_one: bfloat16 [32, 32], replicated, may hold values from -1 to 1
- modes_two: float32 [1728, 32, 32], P('grp', 'tile'), may hold values from -6 to 6
- modes_one: float32 [1728, 32, 32], P('grp', 'tile'), may hold values from -6 to 6
- saved_two: float32 [1, 1728, 32], P(None, 'grp'), may hold values from -6 to 6
- saved_one: float32 [1, 1728, 32], P(None, 'grp'), may hold values from -6 to 6
Outputs:
- input_grad: bfloat16 [1, 32, 48, 128, 128], P(None, None, 'grp', 'tile')
- grad_one: float32 [1728, 32, 32], P('grp', 'tile')
- grad_two: float32 [1728, 32, 32], P('grp', 'tile')
All inputs are finite; a program needn't handle non-finite values.
Results may differ from a plain program's by a relative error of at most 0.01.
Values sent between devices are 32-bit elements; how exact they have to be, the bound alone decides.
No kernel may reach another device: no remote copies, remote signals or barrier semaphores. Data moves between devices by JAX's collectives and lax.ppermute only.
A program may use at most 64 MiB of HBM per device.

v0:
```python
import functools
import math

import jax
import jax.numpy as jnp
import numpy as np
from jax import lax
from jax.experimental import pallas as pl
from jax.experimental.pallas import tpu as pltpu
from jax.sharding import PartitionSpec as P


K = 12
LANES = 128
SUB = 8
COST = 1 << 31
HIGH = lax.Precision.HIGHEST
BOTH = ("grp", "tile")
VMEM = pl.BlockSpec(memory_space=pltpu.VMEM)
HBM = pl.BlockSpec(memory_space=pltpu.HBM)
SMEM = pl.BlockSpec(memory_space=pltpu.SMEM)
F32 = jnp.float32
BF16 = jnp.bfloat16


def basis(length):
    position = np.arange(length)
    orders = np.arange(K)
    frequency = (orders + 1) // 2
    phase = frequency[:, None] * position[None, :] % length
    angle = 2.0 * math.pi / length * phase
    factor = math.sqrt(2.0 / length)
    values = np.where(orders[:, None] % 2 == 1, factor * np.cos(angle), factor * np.sin(angle))
    values[0] = 1.0 / math.sqrt(length)
    return values.astype(np.float32)


class Plan:
    def __init__(self, mesh, cells, channels):
        self.groups, self.tiles = mesh.shape["grp"], mesh.shape["tile"]
        self.devices = self.groups * self.tiles
        self.x, self.y, self.z = cells
        self.c = channels
        self.per_row = LANES // channels
        self.blocks = K // self.per_row
        self.width = K * channels
        self.pairs = K * K // self.groups
        self.run = -(-self.pairs // self.tiles)
        self.slot = -(-self.run * self.blocks // SUB) * SUB
        self.packed = self.slot + SUB
        self.half = self.devices // 2
        self.lanes = self.per_row * self.slot
        self.fold = LANES // self.lanes
        self.rows = self.devices * self.run
        self.own = channels // self.tiles
        self.step = 8

    def valid(self, tile):
        return max(0, min(self.run, self.pairs - self.run * tile))


def call(body, plan, outs, scratch=(), specs=None, out_specs=None, count=None, limit=8, grid=()):
    return pl.pallas_call(
        functools.partial(body, plan),
        grid=grid,
        out_shape=tuple(
            pltpu.HBM(s, d) if spec is not VMEM else jax.ShapeDtypeStruct(s, d)
            for (s, d), spec in zip(outs, out_specs or [VMEM] * len(outs))
        ),
        in_specs=specs or [VMEM] * count,
        out_specs=tuple(out_specs or [VMEM] * len(outs)),
        scratch_shapes=list(scratch),
        compiler_params=pltpu.CompilerParams(vmem_limit_bytes=limit << 20),
        cost_estimate=pl.CostEstimate(flops=COST, bytes_accessed=COST // 1000, transcendentals=0),
    )


def forward_weights(plan, tz_ref, mask_ref, first):
    table = tz_ref[...]
    parts = []
    for u in range(plan.step):
        parts.append(table * mask_ref[first + u])
    return jnp.concatenate(parts, axis=0)


def emit_slots(plan, acc, table, keep_ref, send_ref, s_ref):
    p = plan
    s_ref[...] = jnp.dot(table, acc, precision=HIGH, preferred_element_type=F32)
    for d in range(p.devices):
        slots_ref, n = (keep_ref, d) if d < p.half else (send_ref, d - p.half)
        for j in range(p.blocks):
            slots_ref[n, j * p.run : (j + 1) * p.run, :] = s_ref[
                d * p.run : (d + 1) * p.run, j * LANES : (j + 1) * LANES
            ]
        if p.blocks * p.run < p.slot:
            slots_ref[n, p.blocks * p.run :, :] = jnp.zeros((p.slot - p.blocks * p.run, LANES), F32)


def product(up, der):
    return (up.astype(F32) * der.astype(F32)).astype(BF16)


def spread_rows(rows, cells):
    return lax.dot_general(
        rows, cells, (((0,), (0,)), ((), ())), precision=HIGH, preferred_element_type=F32
    )


def analyse_body(
    plan, place_ref, up_ref, der_hbm, tz_ref, mask_ref, rx_ref, ry_ref, ex_ref, ey_ref,
    keep_ref, send_ref, table_ref, acc_ref, s_ref, der_ref, sems,
):
    p = plan
    step = pl.program_id(0)

    def fetch(n):
        part = pl.ds(n * p.step, p.step)
        return pltpu.make_async_copy(der_hbm.at[part], der_ref.at[part], sems.at[n])

    @pl.when(step == 0)
    def _():
        for n in range(p.c // p.step):
            fetch(n).start()
        table_ref[...] = spread_rows(rx_ref[place_ref[2]], ex_ref[...]) * spread_rows(
            ry_ref[place_ref[3]], ey_ref[...]
        )
        acc_ref[...] = jnp.zeros_like(acc_ref)

    first = step * p.step
    weights = forward_weights(p, tz_ref, mask_ref, first)
    fetch(step).wait()
    parts = []
    for u in range(p.step):
        parts.append(product(up_ref[first + u], der_ref[first + u]))
    acc_ref[...] += jnp.dot(jnp.concatenate(parts, axis=1), weights, preferred_element_type=F32)

    @pl.when(step == pl.num_programs(0) - 1)
    def _():
        emit_slots(p, acc_ref[...], table_ref[...], keep_ref, send_ref, s_ref)


def gather_modes(plan, got_ref, more_ref, table_ref, d_ref):
    p = plan
    for d in range(p.devices):
        from_ref, n = (got_ref, d) if d < p.half else (more_ref, d - p.half)
        for j in range(p.blocks):
            d_ref[d * p.run : (d + 1) * p.run, j * LANES : (j + 1) * LANES] = from_ref[
                n, j * p.run : (j + 1) * p.run, :
            ]
    return lax.dot_general(
        table_ref[...], d_ref[...], (((0,), (0,)), ((), ())), precision=HIGH, preferred_element_type=F32
    ).astype(BF16)


def synth_analyse_body(
    plan, got_ref, more_ref, point_ref, der_ref, tz_ref, mask_ref, table_ref, gated_ref, keep_ref, send_ref,
    acc_ref, s_ref, d_ref, modes_ref, field_ref, sems,
):
    p = plan
    step = pl.program_id(0)

    def store(n):
        part = pl.ds(n * p.step, p.step)
        return pltpu.make_async_copy(field_ref.at[part], gated_ref.at[part], sems.at[n])

    @pl.when(step == 0)
    def _():
        modes_ref[...] = gather_modes(p, got_ref, more_ref, table_ref, d_ref)
        acc_ref[...] = jnp.zeros_like(acc_ref)

    first = step * p.step
    weights = forward_weights(p, tz_ref, mask_ref, first)
    synth = lax.dot_general(modes_ref[...], weights, (((1,), (1,)), ((), ())), preferred_element_type=F32)
    parts = []
    for u in range(p.step):
        middle = (point_ref[first + u] + synth[:, u * p.z : (u + 1) * p.z]).astype(BF16)
        gated = product(middle, der_ref[first + u])
        field_ref[first + u] = gated
        parts.append(gated)
    store(step).start()
    acc_ref[...] += jnp.dot(jnp.concatenate(parts, axis=1), weights, preferred_element_type=F32)

    @pl.when(step == pl.num_programs(0) - 1)
    def _():
        emit_slots(p, acc_ref[...], table_ref[...], keep_ref, send_ref, s_ref)
        for n in range(p.c // p.step):
            store(n).wait()


def synth_body(
    plan, place_ref, got_ref, more_ref, point_ref, tz_ref, mask_ref, table_ref, saved_ref, out_ref, grad_ref,
    d_ref, modes_ref,
):
    p = plan

    @pl.when(pl.program_id(0) == 0)
    def _():
        modes_ref[...] = gather_modes(p, got_ref, more_ref, table_ref, d_ref)
        grad_body(p, place_ref, got_ref, more_ref, saved_ref, grad_ref)

    first = pl.program_id(0) * p.step
    weights = forward_weights(p, tz_ref, mask_ref, first)
    synth = lax.dot_general(modes_ref[...], weights, (((1,), (1,)), ((), ())), preferred_element_type=F32)
    for u in range(p.step):
        out_ref[u] = (point_ref[first + u] + synth[:, u * p.z : (u + 1) * p.z]).astype(BF16)


def pointwise_body(plan, *refs):
    p = plan
    *field_refs, w_ref, spread_ref, out_ref, big_ref = refs
    n = p.c * p.y
    spread = spread_ref[...]
    rows = lax.dot_general(spread, w_ref[...], (((1,), (1,)), ((), ())), preferred_element_type=F32).astype(BF16)
    both = lax.dot_general(rows, spread, (((1,), (1,)), ((), ())), preferred_element_type=F32)
    same = (
        lax.broadcasted_iota(jnp.int32, (n, n), 0) % p.y == lax.broadcasted_iota(jnp.int32, (n, n), 1) % p.y
    )
    big_ref[...] = jnp.where(same, both, 0.0).astype(BF16)
    for x in range(0, p.x, 2):
        pair = []
        for h in range(2):
            cells = [ref[:, (x + h) * p.y : (x + h + 1) * p.y, :] for ref in field_refs]
            pair.append((product(*cells) if len(cells) == 2 else cells[0]).reshape(n, p.z))
        out = jnp.dot(big_ref[...], jnp.concatenate(pair, axis=1), preferred_element_type=F32)
        for h in range(2):
            out_ref[:, (x + h) * p.y : (x + h + 1) * p.y, :] = out[:, h * p.z : (h + 1) * p.z].reshape(
                p.c, p.y, p.z
            )


def pack_body(plan, two_hbm, one_hbm, order_hbm, out_ref, two_ref, one_ref, order_ref, sems):
    p = plan
    n = p.own * p.c
    rows = p.c // p.fold
    copies = [
        pltpu.make_async_copy(source, target, sems.at[n])
        for n, (source, target) in enumerate(((order_hbm, order_ref), (two_hbm, two_ref), (one_hbm, one_ref)))
    ]
    for copy in copies:
        copy.start()
    copies[0].wait()
    for layer, w_ref in enumerate((two_ref, one_ref)):
        copies[1 + layer].wait()
        rest = w_ref[...].reshape(n, p.pairs * K)
        parts = []
        for _ in range(3):
            parts.append(rest.astype(BF16))
            rest = rest - parts[-1].astype(F32)
        moved = jnp.dot(jnp.concatenate(parts, axis=0), order_ref[...], preferred_element_type=F32)
        moved = moved[:n] + moved[n : 2 * n] + moved[2 * n :]
        for o in range(p.own):
            mine = moved[o * p.c : (o + 1) * p.c]
            for t in range(p.tiles):
                out_ref[t, layer, o] = jnp.concatenate(
                    [
                        mine[f * rows : (f + 1) * rows, t * p.lanes : (t + 1) * p.lanes]
                        for f in range(p.fold)
                    ],
                    axis=1,
                )


def dual_body(plan, layer, parity_ref, got_ref, w_ref, out_ref):
    p = plan
    total = got_ref[0]
    for d in range(1, p.half):
        total = total + got_ref[d]
    down = total.T
    ks = [down[k * p.c : (k + 1) * p.c, :] for k in range(p.per_row)]
    modes = jnp.concatenate(ks * p.fold, axis=1)
    rows = p.c // p.fold
    sums = jnp.zeros((rows, LANES), F32)
    for o in range(p.c):
        sums = sums + w_ref[o // p.own, layer, o % p.own] * modes[o : o + 1, :]
    down = sums.T
    pieces = []
    for k in range(p.per_row):
        for f in range(p.fold):
            start = (f * p.per_row + k) * p.slot
            pieces.append(down[start : start + p.slot, :])
    dual = jnp.concatenate(pieces, axis=1)
    parity = parity_ref[0]
    for q in range(p.tiles // 2):
        even = modes[2 * q * p.own : (2 * q + 1) * p.own, :]
        odd = modes[(2 * q + 1) * p.own : (2 * q + 2) * p.own, :]
        mine = jnp.where(parity == 0, even, odd)
        other = jnp.where(parity == 0, odd, even)
        pieces = [mine, other]
        if 2 * p.own < SUB:
            pieces.append(jnp.zeros((SUB - 2 * p.own, LANES), F32))
        both = jnp.concatenate(pieces, axis=0)
        for g in range(p.groups):
            d = g * (p.tiles // 2) + q
            out_ref[d, : p.slot, :] = dual
            out_ref[d, p.slot :, :] = both


def grad_body(plan, place_ref, got_ref, more_ref, saved_ref, out_ref):
    p = plan
    base = place_ref[1] * (p.tiles // 2)
    parity = place_ref[0]
    lane = lax.broadcasted_iota(jnp.int32, (SUB, LANES), 1)
    source = lane % p.per_row * p.slot + lane % K // p.per_row * p.run + lane // K
    source = jnp.clip(source, 0, LANES - 1)
    pieces = []
    for q in range(p.tiles // 2):
        one = jnp.take_along_axis(got_ref[base + q, p.slot :, :], source, axis=1)[: p.own]
        two = jnp.take_along_axis(more_ref[base + q, p.slot :, :], source, axis=1)[p.own : 2 * p.own]
        for t, piece in (
            (2 * q, jnp.where(parity == 0, one, two)),
            (2 * q + 1, jnp.where(parity == 0, two, one)),
        ):
            if p.valid(t) > 0:
                pieces.append(piece[:, : p.valid(t) * K])
    spectrum = jnp.concatenate(pieces, axis=1)
    for o in range(p.own):
        out_ref[o] = saved_ref[...] * spectrum[o : o + 1, :]


def solution(mesh):
    def local(cotangent, deriv_two, deriv_one, point_two, point_one, modes_two, modes_one, saved_two, saved_one):
        shape = cotangent.shape
        channels = shape[1]
        plan = p = Plan(mesh, shape[2:], channels)
        xy = p.x * p.y
        g = lax.axis_index("grp")
        t = lax.axis_index("tile")

        full_x, full_y, full_z = basis(p.x * p.groups), basis(p.y * p.tiles), basis(p.z)
        rows_x, rows_y = [], []
        for parity in range(2):
            pair, used = [], []
            for h in (parity, 1 - parity):
                for d in range(p.half):
                    tile = d % (p.tiles // 2) * 2 + h
                    own = np.arange(p.run)
                    used.append(own < p.valid(tile))
                    start = d // (p.tiles // 2) * p.pairs + tile * p.run
                    pair.append(np.where(used[-1], start + own, 0))
            pair, used = np.concatenate(pair), np.concatenate(used)
            rows_x.append(full_x[pair // K] * used[:, None].astype(np.float32))
            rows_y.append(full_y[pair % K])
        rows_x = np.stack(rows_x).reshape(2, p.rows, p.groups, p.x).transpose(0, 2, 3, 1)
        rows_x = rows_x.reshape(2 * p.groups, p.x, p.rows)
        rows_y = np.stack(rows_y).reshape(2, p.rows, p.tiles // 2, 2, p.y)
        rows_y = np.stack([rows_y[h, :, :, h] for h in range(2)]).transpose(2, 0, 3, 1)
        rows_y = rows_y.reshape(p.tiles, p.y, p.rows)
        parity = t % 2
        rows_x, rows_y = jnp.asarray(rows_x), jnp.asarray(rows_y)
        ex = jnp.asarray(np.repeat(np.eye(p.x, dtype=np.float32), p.y, axis=1))
        ey = jnp.asarray(np.tile(np.eye(p.y, dtype=np.float32), (1, p.x)))
        tz = jnp.asarray(np.repeat(full_z.T, p.c, axis=1)).astype(BF16)
        mask = np.zeros((p.c, 1, K, p.c), np.float32)
        mask[np.arange(p.c), 0, :, np.arange(p.c)] = 1.0
        mask = jnp.asarray(mask.reshape(p.c, 1, p.width)).astype(BF16)
        spread = jnp.asarray(np.repeat(np.eye(p.c, dtype=np.float32), p.y, axis=0)).astype(BF16)

        order = np.zeros((p.pairs * K, p.tiles * p.lanes), np.float32)
        for tile in range(p.tiles):
            for r in range(p.valid(tile)):
                for k in range(K):
                    lane = k % p.per_row * p.slot + k // p.per_row * p.run + r
                    order[(tile * p.run + r) * K + k, tile * p.lanes + lane] = 1.0
        order = jnp.asarray(order).astype(BF16)

        field = (p.c, xy, p.z)
        slots = (p.half, p.slot, LANES)
        packed = (p.half, p.packed, LANES)
        acc = pltpu.VMEM((xy, p.width), F32)
        s_scr = pltpu.VMEM((p.rows, p.width), F32)
        modes_scr = pltpu.VMEM((xy, p.width), BF16)
        blocked = pl.BlockSpec((p.step, xy, p.z), lambda n: (n, 0, 0))
        steps = (p.c // p.step,)
        place = jnp.stack([parity, g, parity * p.groups + g, t]).astype(jnp.int32)
        partners = [(i, i ^ 1) for i in range(p.tiles)]
        same = [
            [e * p.tiles + 2 * q + h for e in range(p.groups) for q in range(p.tiles // 2)] for h in range(2)
        ]

        def in_hbm(array):
            return pltpu.with_memory_space_constraint(array, pltpu.HBM)

        weights = call(
            pack_body, p, [((p.tiles, 2, p.own, p.c // p.fold, LANES), F32)],
            [
                pltpu.VMEM((p.own, p.c, p.pairs * K), F32),
                pltpu.VMEM((p.own, p.c, p.pairs * K), F32),
                pltpu.VMEM(order.shape, BF16),
                pltpu.SemaphoreType.DMA((3,)),
            ],
            specs=[HBM] * 3,
        )(in_hbm(modes_two.transpose(1, 2, 0)), in_hbm(modes_one.transpose(1, 2, 0)), in_hbm(order))[0]
        weights = lax.all_to_all(weights, "tile", 0, 0, tiled=True)

        def exchange(parts):
            return lax.all_to_all(parts, BOTH, 0, 0, tiled=True, axis_index_groups=same)

        def partner(parts):
            return lax.ppermute(parts, "tile", partners)

        def dual(got, layer):
            body = functools.partial(dual_body, p, layer)
            return call(lambda _, *refs: body(*refs), p, [(packed, F32)], specs=[SMEM, VMEM, VMEM])(
                place, got, weights
            )[0]

        def pointwise(w, *factors):
            return call(
                pointwise_body, p, [(field, F32)], [pltpu.VMEM((p.c * p.y, p.c * p.y), BF16)],
                count=2 + len(factors),
            )(*factors, w, spread)[0]

        def grad(got, more, saved):
            out = call(
                grad_body, p, [((p.own, p.c, p.pairs * K), F32)], specs=[SMEM, VMEM, VMEM, VMEM]
            )(place, got, more, saved[0].T)[0]
            return out.transpose(2, 0, 1)

        keep, send, table = call(
            analyse_body, p, [(slots, F32), (slots, F32), ((p.rows, xy), F32)],
            [acc, s_scr, pltpu.VMEM(field, BF16), pltpu.SemaphoreType.DMA(steps)],
            specs=[SMEM, VMEM, HBM] + [VMEM] * 6, grid=steps,
        )(place, cotangent.reshape(field), in_hbm(deriv_two.reshape(field)), tz, mask, rows_x, rows_y, ex, ey)
        part_two = keep + partner(send)
        got_two = exchange(part_two)
        point_out = pointwise(point_two, cotangent.reshape(field), deriv_two.reshape(field))
        share_two = dual(got_two, 0)
        all_two = exchange(share_two)
        more_two = partner(all_two)
        gated_one, keep, send = call(
            synth_analyse_body, p, [(field, BF16), (slots, F32), (slots, F32)], [acc, s_scr, s_scr, modes_scr, pltpu.VMEM(field, BF16), pltpu.SemaphoreType.DMA(steps)],
            count=7, out_specs=[HBM, VMEM, VMEM], grid=steps,
        )(all_two, more_two, point_out, deriv_one.reshape(field), tz, mask, table)
        part_one = keep + partner(send)
        got_one = exchange(part_one)
        grad_two = grad(all_two, more_two, saved_two)
        point_out = pointwise(point_one, gated_one)
        share_one = dual(got_one, 1)
        all_one = exchange(share_one)
        more_one = partner(all_one)
        result, grad_one = call(
            synth_body, p, [(field, BF16), ((p.own, p.c, p.pairs * K), F32)], [s_scr, modes_scr],
            specs=[SMEM] + [VMEM] * 7,
            out_specs=[blocked, pl.BlockSpec((p.own, p.c, p.pairs * K), lambda n: (0, 0, 0))],
            grid=steps,
        )(place, all_one, more_one, point_out, tz, mask, table, saved_one[0].T)
        grad_one = grad_one.transpose(2, 0, 1)
        return (result.reshape(shape), grad_one, grad_two)

    return jax.shard_map(
        local,
        mesh=mesh,
        in_specs=(
            P(None, None, "grp", "tile", None),
            P(None, None, "grp", "tile", None),
            P(None, None, "grp", "tile", None),
            P(),
            P(),
            P("grp", "tile", None),
            P("grp", "tile", None),
            P(None, "grp", None),
            P(None, "grp", None),
        ),
        out_specs=(
            P(None, None, "grp", "tile", None),
            P("grp", "tile", None),
            P("grp", "tile", None),
        ),
        check_vma=False,
    )
```

profile of v0, /device:TPU:0, one launch (start us, length us, event | category | flops | bytes accessed | tf_op | source)
XLA Modules:
  0.0 91.0 jit_solution(10080021771195008560)
XLA Ops:
  0.6 0.1 pad_add_fusion.place_ref.refs_0_
  0.7 1.4 %copy-done = bf16[1,32,12,16,128]{4,3,2,1,0:T(8,128)(2,1)S(1)} copy-done((bf16[1,32,12,16,128]{4,3,2,1,0:T(8,128)(2,1)S(1)}, bf16[1,32,12,16,128]{4,3,2,1,0:T(8,128)(2,1)}, u32[]{:S(2)}) %copy-start) | copy-done | bytes 1572888
  2.1 0.9 copy-done.9
  3.0 0.9 copy-done.10
  3.9 0.9 copy-done.11
  4.8 0.8 copy-done.13
  5.6 0.7 copy-done.15
  6.4 0.7 copy-done.16
  7.1 3.8 %shard_map.184 = (f32[16,16,128]{2,1,0:T(8,128)S(1)}, f32[16,16,128]{2,1,0:T(8,128)S(1)}, f32[160,192]{1,0:T(8,128)S(1)}) custom-call(s32[4]{0:T(128)S(1)} %pad_add_fusion.place_ref.refs_0_, bf16[32,192,128]{2,1,0:T(8,128)(2,1)S(1)} %bitcast.18, bf16[32,192,128]{2,1,0:T(8,128)(2,1)} %bitcast.20, bf16[128,384]{1,0:T(8,128)(2,1)S(1)} %copy-done.11, ...), custom_call_target="tpu_custom_call" | custom-call | flops 2147483648 | bytes 2147483 | tf_op jit(solution)/shard_map/pallas_call | solution.py:419
  10.9 0.6 collective-permute-start
  11.5 1.0 %collective-permute-done = f32[16,16,128]{2,1,0:T(8,128)S(1)} collective-permute-done((f32[16,16,128]{2,1,0:T(8,128)S(1)}, f32[16,16,128]{2,1,0:T(8,128)S(1)}, u32[]{:S(2)}, u32[]{:S(2)}) %collective-permute-start) | collective-permute-done | bytes 131104 | tf_op jit(solution)/shard_map/ppermute | solution.py:399
  12.5 0.7 add.15
  13.1 8.2 %all-to-all-start = ((f32[16,16,128]{2,1,0:T(8,128)}), f32[16,16,128]{2,1,0:T(8,128)S(1)}, u32[]{:S(2)}, u32[]{:S(2)}) async-start(f32[16,16,128]{2,1,0:T(8,128)} %add.15), calls=%async_computation | async-start | bytes 262144 | tf_op jit(solution)/shard_map/all_to_all | solution.py:396
  21.3 2.1 %shard_map.185 = f32[8,2,4,16,128]{4,3,2,1,0:T(8,128)S(1)} custom-call(f32[4,32,432]{2,1,0:T(8,128)} %bitcast.25, f32[4,32,432]{2,1,0:T(8,128)} %bitcast.26, bf16[432,512]{1,0:T(8,128)(2,1)} %constant.51.order_hbm), custom_call_target="tpu_custom_call" | custom-call | flops 2147483648 | bytes 2147483 | tf_op jit(solution)/shard_map/pallas_call | solution.py:383
  23.4 5.7 %all-to-all-done.refs_1_ = f32[16,16,128]{2,1,0:T(8,128)S(1)} async-done(((f32[16,16,128]{2,1,0:T(8,128)}), f32[16,16,128]{2,1,0:T(8,128)S(1)}, u32[]{:S(2)}, u32[]{:S(2)}) %all-to-all-start) | async-done | bytes 131104 | tf_op jit(solution)/shard_map/all_to_all | solution.py:396
  29.1 12.1 %all_to_all.25.refs_2_ = f32[8,2,4,16,128]{4,3,2,1,0:T(8,128)S(1)} all-to-all(f32[8,2,4,16,128]{4,3,2,1,0:T(8,128)S(1)} %shard_map.185), channel_id=1, replica_groups=mesh['grp'=4,'tile'=8] {'tile'}, dimensions={0} | all-to-all | bytes 1048576 | tf_op jit(solution)/shard_map/all_to_all | solution.py:393
  41.3 0.9 %shard_map.186 = f32[16,24,128]{2,1,0:T(8,128)S(1)} custom-call(s32[4]{0:T(128)S(1)} %pad_add_fusion.place_ref.refs_0_, f32[16,16,128]{2,1,0:T(8,128)S(1)} %all-to-all-done.refs_1_, f32[8,2,4,16,128]{4,3,2,1,0:T(8,128)S(1)} %all_to_all.25.refs_2_), custom_call_target="tpu_custom_call" | custom-call | flops 2147483648 | bytes 2147483 | tf_op jit(solution)/shard_map/pallas_call | solution.py:403
  42.2 11.6 %all_to_all.26.got_ref = f32[16,24,128]{2,1,0:T(8,128)S(1)} all-to-all(f32[16,24,128]{2,1,0:T(8,128)S(1)} %shard_map.186), channel_id=1, replica_groups={{0,2,4,6,8,10,12,14,16,18,20,22,24,26,28,30},{1,3,5,7,9,11,13,15,17,19,..., dimensions={0} | all-to-all | bytes 393216 | tf_op jit(solution)/shard_map/all_to_all | solution.py:396
  53.8 0.0 collective-permute-start.1
  53.8 0.0 copy-done.1
  53.8 0.0 copy-done.2
  53.8 0.0 copy-done.6
  53.8 0.0 copy-done.8
  53.8 1.3 %shard_map.187.point_ref = f32[32,192,128]{2,1,0:T(8,128)S(1)} custom-call(bf16[32,192,128]{2,1,0:T(8,128)(2,1)S(1)} %bitcast.19, bf16[32,192,128]{2,1,0:T(8,128)(2,1)S(1)} %bitcast.21, bf16[32,32]{1,0:T(8,128)(2,1)S(1)} %copy-done.6, bf16[512,32]{1,0:T(8,128)(2,1)S(1)} %copy-done.8), custom_call_target="tpu_custom_call" | custom-call | flops 2147483648 | bytes 2147483 | tf_op jit(solution)/shard_map/pallas_call | solution.py:408
  55.1 0.1 collective-permute-done.1.more_ref
  55.2 0.0 copy-done.3
  55.2 0.0 copy-done.12
  55.2 0.0 copy-done.14
  55.2 4.0 %shard_map.188 = (bf16[32,192,128]{2,1,0:T(8,128)(2,1)}, f32[16,16,128]{2,1,0:T(8,128)S(1)}, f32[16,16,128]{2,1,0:T(8,128)S(1)}) custom-call(f32[16,24,128]{2,1,0:T(8,128)S(1)} %all_to_all.26.got_ref, f32[16,24,128]{2,1,0:T(8,128)S(1)} %collective-permute-done.1.more_ref, f32[32,192,128]{2,1,0:T(8,128)S(1)} %shard_map.187.point_ref, ...), custom_call_target="tpu_custom_call" | custom-call | flops 2147483648 | bytes 2147483 | tf_op jit(solution)/shard_map/pallas_call | solution.py:430
  59.2 0.4 collective-permute-start.2
  59.7 1.0 %collective-permute-done.2 = f32[16,16,128]{2,1,0:T(8,128)S(1)} collective-permute-done((f32[16,16,128]{2,1,0:T(8,128)S(1)}, f32[16,16,128]{2,1,0:T(8,128)S(1)}, u32[]{:S(2)}, u32[]{:S(2)}) %collective-permute-start.2) | collective-permute-done | bytes 131104 | tf_op jit(solution)/shard_map/ppermute | solution.py:399
  60.7 11.1 %all_to_all.27.refs_1_ = f32[16,16,128]{2,1,0:T(8,128)S(1)} all-to-all(f32[16,16,128]{2,1,0:T(8,128)S(1)} %add.16), channel_id=1, replica_groups={{0,2,4,6,8,10,12,14,16,18,20,22,24,26,28,30},{1,3,5,7,9,11,13,15,17,19,..., dimensions={0} | all-to-all | bytes 262144 | tf_op jit(solution)/shard_map/all_to_all | solution.py:396
  71.8 1.6 %shard_map.189 = f32[16,24,128]{2,1,0:T(8,128)} custom-call(s32[4]{0:T(128)S(1)} %pad_add_fusion.place_ref.refs_0_, f32[16,16,128]{2,1,0:T(8,128)S(1)} %all_to_all.27.refs_1_, f32[8,2,4,16,128]{4,3,2,1,0:T(8,128)S(1)} %all_to_all.25.refs_2_), custom_call_target="tpu_custom_call" | custom-call | flops 2147483648 | bytes 2147483 | tf_op jit(solution)/shard_map/pallas_call | solution.py:403
  73.4 3.5 %all-to-all-start.4 = ((f32[16,24,128]{2,1,0:T(8,128)}), f32[16,24,128]{2,1,0:T(8,128)S(1)}, u32[]{:S(2)}, u32[]{:S(2)}) async-start(f32[16,24,128]{2,1,0:T(8,128)} %shard_map.189), calls=%async_computation.4 | async-start | bytes 393216 | tf_op jit(solution)/shard_map/all_to_all | solution.py:396
  77.0 0.0 copy-done.7
  77.0 0.0 copy-done.19
  77.0 0.0 copy-start.4
  77.0 1.2 %shard_map.190.point_ref = f32[32,192,128]{2,1,0:T(8,128)S(1)} custom-call(bf16[32,192,128]{2,1,0:T(8,128)(2,1)S(1)} %copy-done.19, bf16[32,32]{1,0:T(8,128)(2,1)S(1)} %copy-done.7, bf16[512,32]{1,0:T(8,128)(2,1)S(1)} %copy-done.8), custom_call_target="tpu_custom_call" | custom-call | flops 2147483648 | bytes 2147483 | tf_op jit(solution)/shard_map/pallas_call | solution.py:408
  78.2 0.0 copy-start.17
  78.2 1.6 %copy-done.17 = f32[32,192,128]{2,1,0:T(8,128)} copy-done((f32[32,192,128]{2,1,0:T(8,128)}, f32[32,192,128]{2,1,0:T(8,128)S(1)}, u32[]{:S(2)}) %copy-start.17) | copy-done | bytes 3145752
  79.8 5.2 %all-to-all-done.4.got_ref = f32[16,24,128]{2,1,0:T(8,128)S(1)} async-done(((f32[16,24,128]{2,1,0:T(8,128)}), f32[16,24,128]{2,1,0:T(8,128)S(1)}, u32[]{:S(2)}, u32[]{:S(2)}) %all-to-all-start.4) | async-done | bytes 196640 | tf_op jit(solution)/shard_map/all_to_all | solution.py:396
  85.0 0.0 collective-permute-start.3
  85.0 0.0 copy-done.4
  85.0 0.0 copy-start.18
  85.0 1.4 %shard_map.192 = f32[4,32,432]{2,1,0:T(8,128)} custom-call(s32[4]{0:T(128)S(1)} %pad_add_fusion.place_ref.refs_0_, f32[16,24,128]{2,1,0:T(8,128)S(1)} %all_to_all.26.got_ref, f32[16,24,128]{2,1,0:T(8,128)S(1)} %collective-permute-done.1.more_ref, f32[32,432]{1,0:T(8,128)S(1)} %bitcast.23), custom_call_target="tpu_custom_call" | custom-call | flops 2147483648 | bytes 2147483 | tf_op jit(solution)/shard_map/pallas_call | solution.py:414
  86.5 0.0 collective-permute-done.3.more_ref
  86.5 0.6 copy-done.18
  87.0 4.0 %shard_map.191 = (bf16[32,192,128]{2,1,0:T(8,128)(2,1)}, f32[4,32,432]{2,1,0:T(8,128)}) custom-call(s32[4]{0:T(128)S(1)} %pad_add_fusion.place_ref.refs_0_, f32[16,24,128]{2,1,0:T(8,128)S(1)} %all-to-all-done.4.got_ref, f32[16,24,128]{2,1,0:T(8,128)S(1)} %collective-permute-done.3.more_ref, f32[32,192,128]{2,1,0:T(8,128)S(1)} %copy-done.18, ...), custom_call_target="tpu_custom_call" | custom-call | flops 2147483648 | bytes 2147483 | tf_op jit(solution)/shard_map/pallas_call | solution.py:441
  (19 shorter events, 0.0 us)
Async XLA Ops:
  0.7 1.4 %copy-start = (bf16[1,32,12,16,128]{4,3,2,1,0:T(8,128)(2,1)S(1)}, bf16[1,32,12,16,128]{4,3,2,1,0:T(8,128)(2,1)}, u32[]{:S(2)}) copy-start(bf16[1,32,12,16,128]{4,3,2,1,0:T(8,128)(2,1)} %param.17) | copy-start | bytes 4718596
  2.1 0.9 copy-start.9
  3.0 0.9 copy-start.10
  3.9 0.9 copy-start.11
  4.8 0.8 copy-start.13
  5.6 0.7 copy-start.15
  6.3 0.7 copy-start.16
  10.9 1.5 %collective-permute-start = (f32[16,16,128]{2,1,0:T(8,128)S(1)}, f32[16,16,128]{2,1,0:T(8,128)S(1)}, u32[]{:S(2)}, u32[]{:S(2)}) collective-permute-start(f32[16,16,128]{2,1,0:T(8,128)S(1)} %get-tuple-element.12), channel_id=1, source_target_pairs={{0,1},{1,0},{2,3},{3,2},{4,5},{5,4},{6,7},{7,6},{8,9},{9,8},{10,11... | collective-permute-start | bytes 393224 | tf_op jit(solution)/shard_map/ppermute | solution.py:399
  13.1 16.0 %all-to-all-start = ((f32[16,16,128]{2,1,0:T(8,128)}), f32[16,16,128]{2,1,0:T(8,128)S(1)}, u32[]{:S(2)}, u32[]{:S(2)}) async-start(f32[16,16,128]{2,1,0:T(8,128)} %add.15), calls=%async_computation | async-start | bytes 262144 | tf_op jit(solution)/shard_map/all_to_all | solution.py:396
  41.3 12.5 %copy-start.1 = (bf16[1,32,12,16,128]{4,3,2,1,0:T(8,128)(2,1)S(1)}, bf16[1,32,12,16,128]{4,3,2,1,0:T(8,128)(2,1)}, u32[]{:S(2)}) copy-start(bf16[1,32,12,16,128]{4,3,2,1,0:T(8,128)(2,1)} %param.17) | copy-start | bytes 4718596
  41.3 12.6 %copy-start.2 = (bf16[1,32,12,16,128]{4,3,2,1,0:T(8,128)(2,1)S(1)}, bf16[1,32,12,16,128]{4,3,2,1,0:T(8,128)(2,1)}, u32[]{:S(2)}) copy-start(bf16[1,32,12,16,128]{4,3,2,1,0:T(8,128)(2,1)} %param.18) | copy-start | bytes 4718596
  41.3 12.6 %copy-start.6 = (bf16[32,32]{1,0:T(8,128)(2,1)S(1)}, bf16[32,32]{1,0:T(8,128)(2,1)}, u32[]{:S(2)}) copy-start(bf16[32,32]{1,0:T(8,128)(2,1)} %refs_2_.1) | copy-start | bytes 6148
  41.3 12.6 %copy-start.8 = (bf16[512,32]{1,0:T(8,128)(2,1)S(1)}, bf16[512,32]{1,0:T(8,128)(2,1)}, u32[]{:S(2)}) copy-start(bf16[512,32]{1,0:T(8,128)(2,1)} %constant.52.refs_3_.refs_2_) | copy-start | bytes 98308
  53.8 1.5 %copy-start.3 = (bf16[1,32,12,16,128]{4,3,2,1,0:T(8,128)(2,1)S(1)}, bf16[1,32,12,16,128]{4,3,2,1,0:T(8,128)(2,1)}, u32[]{:S(2)}) copy-start(bf16[1,32,12,16,128]{4,3,2,1,0:T(8,128)(2,1)} %param.19) | copy-start | bytes 4718596
  53.8 1.5 %copy-start.12 = (bf16[128,384]{1,0:T(8,128)(2,1)S(1)}, bf16[128,384]{1,0:T(8,128)(2,1)}, u32[]{:S(2)}) copy-start(bf16[128,384]{1,0:T(8,128)(2,1)} %constant.49.tz_ref) | copy-start | bytes 294916
  53.8 1.5 %copy-start.14 = (bf16[32,1,384]{2,1,0:T(2,128)(2,1)S(1)}, bf16[32,1,384]{2,1,0:T(2,128)(2,1)}, u32[]{:S(2)}) copy-start(bf16[32,1,384]{2,1,0:T(2,128)(2,1)} %constant.50.mask_ref) | copy-start | bytes 73732
  53.8 1.4 %collective-permute-start.1 = (f32[16,24,128]{2,1,0:T(8,128)S(1)}, f32[16,24,128]{2,1,0:T(8,128)S(1)}, u32[]{:S(2)}, u32[]{:S(2)}) collective-permute-start(f32[16,24,128]{2,1,0:T(8,128)S(1)} %all_to_all.26.got_ref), channel_id=1, source_target_pairs={{0,1},{1,0},{2,3},{3,2},{4,5},{5,4},{6,7},{7,6},{8,9},{9,8},{10,11... | collective-permute-start | bytes 589832 | tf_op jit(solution)/shard_map/ppermute | solution.py:399
  59.2 1.4 %collective-permute-start.2 = (f32[16,16,128]{2,1,0:T(8,128)S(1)}, f32[16,16,128]{2,1,0:T(8,128)S(1)}, u32[]{:S(2)}, u32[]{:S(2)}) collective-permute-start(f32[16,16,128]{2,1,0:T(8,128)S(1)} %get-tuple-element.15), channel_id=1, source_target_pairs={{0,1},{1,0},{2,3},{3,2},{4,5},{5,4},{6,7},{7,6},{8,9},{9,8},{10,11... | collective-permute-start | bytes 393224 | tf_op jit(solution)/shard_map/ppermute | solution.py:399
  71.8 5.2 %copy-start.7 = (bf16[32,32]{1,0:T(8,128)(2,1)S(1)}, bf16[32,32]{1,0:T(8,128)(2,1)}, u32[]{:S(2)}) copy-start(bf16[32,32]{1,0:T(8,128)(2,1)} %refs_1_.1) | copy-start | bytes 6148
  71.8 5.2 %copy-start.19 = (bf16[32,192,128]{2,1,0:T(8,128)(2,1)S(1)}, bf16[32,192,128]{2,1,0:T(8,128)(2,1)}, u32[]{:S(2)}) copy-start(bf16[32,192,128]{2,1,0:T(8,128)(2,1)} %get-tuple-element.16.refs_0_) | copy-start | bytes 4718596
  73.4 11.6 %all-to-all-start.4 = ((f32[16,24,128]{2,1,0:T(8,128)}), f32[16,24,128]{2,1,0:T(8,128)S(1)}, u32[]{:S(2)}, u32[]{:S(2)}) async-start(f32[16,24,128]{2,1,0:T(8,128)} %shard_map.189), calls=%async_computation.4 | async-start | bytes 393216 | tf_op jit(solution)/shard_map/all_to_all | solution.py:396
  77.0 8.0 %copy-start.4 = (f32[1,432,32]{1,2,0:T(8,128)S(1)}, f32[1,432,32]{1,2,0:T(8,128)}, u32[]{:S(2)}) copy-start(f32[1,432,32]{1,2,0:T(8,128)} %param.24) | copy-start | bytes 165892
  78.2 1.6 %copy-start.17 = (f32[32,192,128]{2,1,0:T(8,128)}, f32[32,192,128]{2,1,0:T(8,128)S(1)}, u32[]{:S(2)}) copy-start(f32[32,192,128]{2,1,0:T(8,128)S(1)} %shard_map.190.point_ref) | copy-start | bytes 9437188
  85.0 1.5 %collective-permute-start.3 = (f32[16,24,128]{2,1,0:T(8,128)S(1)}, f32[16,24,128]{2,1,0:T(8,128)S(1)}, u32[]{:S(2)}, u32[]{:S(2)}) collective-permute-start(f32[16,24,128]{2,1,0:T(8,128)S(1)} %all-to-all-done.4.got_ref), channel_id=1, source_target_pairs={{0,1},{1,0},{2,3},{3,2},{4,5},{5,4},{6,7},{7,6},{8,9},{9,8},{10,11... | collective-permute-start | bytes 589832 | tf_op jit(solution)/shard_map/ppermute | solution.py:399
  85.0 1.5 %copy-start.5 = (f32[1,432,32]{1,2,0:T(8,128)S(1)}, f32[1,432,32]{1,2,0:T(8,128)}, u32[]{:S(2)}) copy-start(f32[1,432,32]{1,2,0:T(8,128)} %param.25) | copy-start | bytes 165892
  85.0 2.0 %copy-start.18 = (f32[32,192,128]{2,1,0:T(8,128)S(1)}, f32[32,192,128]{2,1,0:T(8,128)}, u32[]{:S(2)}) copy-start(f32[32,192,128]{2,1,0:T(8,128)} %copy-done.17) | copy-start | bytes 9437188
where the time goes:
time: 91.7 us; the launch traced here: 91 us
  blocking collectives  34.8 us (38%)
  Pallas kernels  20.3 us (22%)
  waiting for transfers between devices  13 us (14%)
  starting transfers between devices  12.7 us (14%)
  local copies, waits for them, and re-layouts  8.57 us (9%)
    all_to_all x2, blocking collectives, exchange(): return lax.all_to_all(parts, BOTH, 0, 0, tiled=True, axis_index_groups=same)  22.7 us
    all_to_all x1, blocking collectives, local(): weights = lax.all_to_all(weights, 'tile', 0, 0, tiled=True)  12.1 us
    all_to_all x2, starting transfers between devices, exchange(): return lax.all_to_all(parts, BOTH, 0, 0, tiled=True, axis_index_groups=same)  11.7 us
    all_to_all x2, waiting for transfers between devices, exchange(): return lax.all_to_all(parts, BOTH, 0, 0, tiled=True, axis_index_groups=same)  10.9 us
    unnamed x40, local copies, waits for them, and re-layouts  8.57 us
    pallas_call x1, Pallas kernels, local(): call(synth_body, p, [(field, BF16), ((p.own, p.c, p.pairs * K), F32)], [s...  4 us
    pallas_call x1, Pallas kernels, local(): call(synth_analyse_body, p, [(field, BF16), (slots, F32), (slots, F32)],...  3.96 us
    pallas_call x1, Pallas kernels, local(): call(analyse_body, p, [(slots, F32), (slots, F32), ((p.rows, xy), F32)],...  3.84 us
  transfers between devices with their start and end apart: 6, of which 5 were waited for; matrix products, arithmetic and copies ran while one was open for 0% of the time, Pallas kernels for 7%

commit v1 on v0

--- a/solution.py
+++ b/solution.py
@@ -49,6 +49,7 @@
         self.slot = -(-self.run * self.blocks // SUB) * SUB
         self.packed = self.slot + SUB
         self.half = self.devices // 2
+        self.chips = self.tiles // 2
         self.lanes = self.per_row * self.slot
         self.fold = LANES // self.lanes
         self.rows = self.devices * self.run
@@ -75,19 +76,15 @@
     )
 
 
-def forward_weights(plan, tz_ref, mask_ref, first):
-    table = tz_ref[...]
-    parts = []
-    for u in range(plan.step):
-        parts.append(table * mask_ref[first + u])
-    return jnp.concatenate(parts, axis=0)
-
-
-def emit_slots(plan, acc, table, keep_ref, send_ref, s_ref):
-    p = plan
-    s_ref[...] = jnp.dot(table, acc, precision=HIGH, preferred_element_type=F32)
+def emit_slots(plan, place_ref, g_ref, order_ref, table_ref, slots_ref, s_ref):
+    p = plan
+    lines = jnp.concatenate([g_ref[n] for n in range(p.c // p.step)], axis=1)
+    lines = lax.dot_general(lines, order_ref[...], (((1,), (1,)), ((), ())), preferred_element_type=F32).astype(BF16)
+    both = jnp.dot(table_ref[...], lines, preferred_element_type=F32)
+    s_ref[...] = both[: p.rows] + both[p.rows :]
     for d in range(p.devices):
-        slots_ref, n = (keep_ref, d) if d < p.half else (send_ref, d - p.half)
+        parity = place_ref[0] if d < p.half else 1 - place_ref[0]
+        n = (d % p.half // p.chips) * p.tiles + d % p.chips * 2 + parity
         for j in range(p.blocks):
             slots_ref[n, j * p.run : (j + 1) * p.run, :] = s_ref[
                 d * p.run : (d + 1) * p.run, j * LANES : (j + 1) * LANES
@@ -107,8 +104,8 @@
 
 
 def analyse_body(
-    plan, place_ref, up_ref, der_hbm, tz_ref, mask_ref, rx_ref, ry_ref, ex_ref, ey_ref,
-    keep_ref, send_ref, table_ref, acc_ref, s_ref, der_ref, sems,
+    plan, place_ref, up_ref, der_hbm, tz_ref, order_ref, rx_ref, ry_ref, ex_ref, ey_ref,
+    slots_ref, table_hbm, turned_hbm, g_ref, s_ref, der_ref, table_ref, turned_ref, sems,
 ):
     p = plan
     step = pl.program_id(0)
@@ -116,30 +113,40 @@
     def fetch(n):
         part = pl.ds(n * p.step, p.step)
         return pltpu.make_async_copy(der_hbm.at[part], der_ref.at[part], sems.at[n])
+
+    last = p.c // p.step
+    tables = (
+        pltpu.make_async_copy(table_ref, table_hbm, sems.at[last]),
+        pltpu.make_async_copy(turned_ref, turned_hbm, sems.at[last + 1]),
+    )
 
     @pl.when(step == 0)
     def _():
         for n in range(p.c // p.step):
             fetch(n).start()
-        table_ref[...] = spread_rows(rx_ref[place_ref[2]], ex_ref[...]) * spread_rows(
-            ry_ref[place_ref[3]], ey_ref[...]
-        )
-        acc_ref[...] = jnp.zeros_like(acc_ref)
+        table = spread_rows(rx_ref[place_ref[2]], ex_ref[...]) * spread_rows(ry_ref[place_ref[3]], ey_ref[...])
+        high = table.astype(BF16)
+        table_ref[: p.rows] = high
+        table_ref[p.rows :] = (table - high.astype(F32)).astype(BF16)
+        turned_ref[...] = table.T.astype(BF16)
+        for copy in tables:
+            copy.start()
 
     first = step * p.step
-    weights = forward_weights(p, tz_ref, mask_ref, first)
     fetch(step).wait()
-    parts = []
-    for u in range(p.step):
-        parts.append(product(up_ref[first + u], der_ref[first + u]))
-    acc_ref[...] += jnp.dot(jnp.concatenate(parts, axis=1), weights, preferred_element_type=F32)
+    parts = [product(up_ref[first + u], der_ref[first + u]) for u in range(p.step)]
+    g_ref[step] = lax.dot_general(
+        jnp.concatenate(parts, axis=1), tz_ref[...], (((1,), (1,)), ((), ())), preferred_element_type=F32
+    ).astype(BF16)
 
     @pl.when(step == pl.num_programs(0) - 1)
     def _():
-        emit_slots(p, acc_ref[...], table_ref[...], keep_ref, send_ref, s_ref)
-
-
-def gather_modes(plan, got_ref, more_ref, table_ref, d_ref):
+        emit_slots(p, place_ref, g_ref, order_ref, table_ref, slots_ref, s_ref)
+        for copy in tables:
+            copy.wait()
+
+
+def gather_modes(plan, got_ref, more_ref, order_ref, turned_ref, d_ref, modes_ref, ready=None):
     p = plan
     for d in range(p.devices):
         from_ref, n = (got_ref, d) if d < p.half else (more_ref, d - p.half)
@@ -147,17 +154,22 @@
             d_ref[d * p.run : (d + 1) * p.run, j * LANES : (j + 1) * LANES] = from_ref[
                 n, j * p.run : (j + 1) * p.run, :
             ]
-    return lax.dot_general(
-        table_ref[...], d_ref[...], (((0,), (0,)), ((), ())), precision=HIGH, preferred_element_type=F32
-    ).astype(BF16)
+    if ready is not None:
+        ready()
+    lines = jnp.dot(turned_ref[...], d_ref[...].astype(BF16), preferred_element_type=F32).astype(BF16)
+    lines = jnp.dot(lines, order_ref[...], preferred_element_type=F32).astype(BF16)
+    for n in range(p.c // p.step):
+        modes_ref[n] = lines[:, n * LANES : (n + 1) * LANES]
 
 
 def synth_analyse_body(
-    plan, got_ref, more_ref, point_ref, der_ref, tz_ref, mask_ref, table_ref, gated_ref, keep_ref, send_ref,
-    acc_ref, s_ref, d_ref, modes_ref, field_ref, sems,
+    plan, place_ref, got_ref, more_ref, point_ref, der_ref, order_ref, tz_hbm, turned_hbm, table_hbm,
+    gated_ref, slots_ref, g_ref, s_ref, d_ref, modes_ref, field_ref, tz_ref, turned_ref, table_ref, sems, table_sems,
 ):
     p = plan
     step = pl.program_id(0)
+    pairs = ((turned_hbm, turned_ref), (tz_hbm, tz_ref), (table_hbm, table_ref))
+    tables = [pltpu.make_async_copy(*pair, table_sems.at[n]) for n, pair in enumerate(pairs)]
 
     def store(n):
         part = pl.ds(n * p.step, p.step)
@@ -165,12 +177,14 @@
 
     @pl.when(step == 0)
     def _():
-        modes_ref[...] = gather_modes(p, got_ref, more_ref, table_ref, d_ref)
-        acc_ref[...] = jnp.zeros_like(acc_ref)
+        for copy in tables:
+            copy.start()
+        gather_modes(p, got_ref, more_ref, order_ref, turned_ref, d_ref, modes_ref, tables[0].wait)
+        for copy in tables[1:]:
+            copy.wait()
 
     first = step * p.step
-    weights = forward_weights(p, tz_ref, mask_ref, first)
-    synth = lax.dot_general(modes_ref[...], weights, (((1,), (1,)), ((), ())), preferred_element_type=F32)
+    synth = jnp.dot(modes_ref[step], tz_ref[...], preferred_element_type=F32)
     parts = []
     for u in range(p.step):
         middle = (point_ref[first + u] + synth[:, u * p.z : (u + 1) * p.z]).astype(BF16)
@@ -178,29 +192,31 @@
         field_ref[first + u] = gated
         parts.append(gated)
     store(step).start()
-    acc_ref[...] += jnp.dot(jnp.concatenate(parts, axis=1), weights, preferred_element_type=F32)
+    g_ref[step] = lax.dot_general(
+        jnp.concatenate(parts, axis=1), tz_ref[...], (((1,), (1,)), ((), ())), preferred_element_type=F32
+    ).astype(BF16)
 
     @pl.when(step == pl.num_programs(0) - 1)
     def _():
-        emit_slots(p, acc_ref[...], table_ref[...], keep_ref, send_ref, s_ref)
+        emit_slots(p, place_ref, g_ref, order_ref, table_ref, slots_ref, s_ref)
         for n in range(p.c // p.step):
             store(n).wait()
 
 
 def synth_body(
-    plan, place_ref, got_ref, more_ref, point_ref, tz_ref, mask_ref, table_ref, saved_ref, out_ref, grad_ref,
+    plan, place_ref, got_ref, more_ref, point_ref, tz_ref, order_ref, turned_ref, saved_ref, out_ref, grad_ref,
     d_ref, modes_ref,
 ):
     p = plan
-
-    @pl.when(pl.program_id(0) == 0)
+    step = pl.program_id(0)
+
+    @pl.when(step == 0)
     def _():
-        modes_ref[...] = gather_modes(p, got_ref, more_ref, table_ref, d_ref)
+        gather_modes(p, got_ref, more_ref, order_ref, turned_ref, d_ref, modes_ref)
         grad_body(p, place_ref, got_ref, more_ref, saved_ref, grad_ref)
 
-    first = pl.program_id(0) * p.step
-    weights = forward_weights(p, tz_ref, mask_ref, first)
-    synth = lax.dot_general(modes_ref[...], weights, (((1,), (1,)), ((), ())), preferred_element_type=F32)
+    first = step * p.step
+    synth = jnp.dot(modes_ref[step], tz_ref[...], preferred_element_type=F32)
     for u in range(p.step):
         out_ref[u] = (point_ref[first + u] + synth[:, u * p.z : (u + 1) * p.z]).astype(BF16)
 
@@ -228,50 +244,56 @@
             )
 
 
-def pack_body(plan, two_hbm, one_hbm, order_hbm, out_ref, two_ref, one_ref, order_ref, sems):
-    p = plan
+def pack_body(plan, place_ref, two_hbm, one_hbm, order_hbm, *refs):
+    p = plan
+    *out_refs, two_ref, one_ref, order_ref, sems = refs
     n = p.own * p.c
     rows = p.c // p.fold
     copies = [
-        pltpu.make_async_copy(source, target, sems.at[n])
-        for n, (source, target) in enumerate(((order_hbm, order_ref), (two_hbm, two_ref), (one_hbm, one_ref)))
+        pltpu.make_async_copy(two_hbm, two_ref, sems.at[0]),
+        pltpu.make_async_copy(order_hbm.at[place_ref[3] // 2], order_ref, sems.at[1]),
+        pltpu.make_async_copy(one_hbm, one_ref, sems.at[2]),
     ]
     for copy in copies:
         copy.start()
-    copies[0].wait()
     for layer, w_ref in enumerate((two_ref, one_ref)):
-        copies[1 + layer].wait()
+        copies[2 * layer].wait()
         rest = w_ref[...].reshape(n, p.pairs * K)
         parts = []
-        for _ in range(3):
+        for _ in range(2):
             parts.append(rest.astype(BF16))
             rest = rest - parts[-1].astype(F32)
+        if layer == 0:
+            copies[1].wait()
         moved = jnp.dot(jnp.concatenate(parts, axis=0), order_ref[...], preferred_element_type=F32)
-        moved = moved[:n] + moved[n : 2 * n] + moved[2 * n :]
+        moved = moved[:n] + moved[n:]
         for o in range(p.own):
             mine = moved[o * p.c : (o + 1) * p.c]
             for t in range(p.tiles):
-                out_ref[t, layer, o] = jnp.concatenate(
-                    [
-                        mine[f * rows : (f + 1) * rows, t * p.lanes : (t + 1) * p.lanes]
-                        for f in range(p.fold)
-                    ],
-                    axis=1,
+                core = jnp.bitwise_xor(place_ref[0], t % 2)
+                out_refs[t // 2][core, layer, o] = jnp.concatenate(
+                    [mine[f * rows : (f + 1) * rows, t * p.lanes : (t + 1) * p.lanes] for f in range(p.fold)], axis=1
                 )
 
 
-def dual_body(plan, layer, parity_ref, got_ref, w_ref, out_ref):
-    p = plan
+def dual_body(plan, layer, place_ref, got_ref, *refs):
+    p = plan
+    *w_refs, cross_ref, out_ref, modes_ref = refs
     total = got_ref[0]
-    for d in range(1, p.half):
+    for d in range(1, p.devices):
         total = total + got_ref[d]
     down = total.T
     ks = [down[k * p.c : (k + 1) * p.c, :] for k in range(p.per_row)]
     modes = jnp.concatenate(ks * p.fold, axis=1)
+    modes_ref[...] = modes
     rows = p.c // p.fold
     sums = jnp.zeros((rows, LANES), F32)
-    for o in range(p.c):
-        sums = sums + w_ref[o // p.own, layer, o % p.own] * modes[o : o + 1, :]
+    for chip in range(p.chips):
+        for core in range(2):
+            tile = jnp.bitwise_xor(place_ref[3] // 2, chip) * 2 + jnp.bitwise_xor(place_ref[0], core)
+            for o in range(p.own):
+                w = cross_ref[chip, layer, o] if core else w_refs[chip][0, layer, o]
+                sums = sums + w * modes_ref[pl.ds(tile * p.own + o, 1), :]
     down = sums.T
     pieces = []
     for k in range(p.per_row):
@@ -279,7 +301,7 @@
             start = (f * p.per_row + k) * p.slot
             pieces.append(down[start : start + p.slot, :])
     dual = jnp.concatenate(pieces, axis=1)
-    parity = parity_ref[0]
+    parity = place_ref[0]
     for q in range(p.tiles // 2):
         even = modes[2 * q * p.own : (2 * q + 1) * p.own, :]
         odd = modes[(2 * q + 1) * p.own : (2 * q + 2) * p.own, :]
@@ -349,26 +371,33 @@
         rows_x, rows_y = jnp.asarray(rows_x), jnp.asarray(rows_y)
         ex = jnp.asarray(np.repeat(np.eye(p.x, dtype=np.float32), p.y, axis=1))
         ey = jnp.asarray(np.tile(np.eye(p.y, dtype=np.float32), (1, p.x)))
-        tz = jnp.asarray(np.repeat(full_z.T, p.c, axis=1)).astype(BF16)
-        mask = np.zeros((p.c, 1, K, p.c), np.float32)
-        mask[np.arange(p.c), 0, :, np.arange(p.c)] = 1.0
-        mask = jnp.asarray(mask.reshape(p.c, 1, p.width)).astype(BF16)
+        groups = p.c // p.step
+        tz = np.zeros((LANES, p.step, p.z), np.float32)
+        lines = np.zeros((K, groups, p.step, groups, LANES), np.float32)
+        for u in range(p.step):
+            for k in range(K):
+                tz[k * p.step + u, u] = full_z[k]
+                lines[k, np.arange(groups), u, np.arange(groups), k * p.step + u] = 1.0
+        tz = jnp.asarray(tz.reshape(LANES, p.step * p.z)).astype(BF16)
+        lines = jnp.asarray(lines.reshape(p.width, groups * LANES)).astype(BF16)
         spread = jnp.asarray(np.repeat(np.eye(p.c, dtype=np.float32), p.y, axis=0)).astype(BF16)
 
-        order = np.zeros((p.pairs * K, p.tiles * p.lanes), np.float32)
-        for tile in range(p.tiles):
-            for r in range(p.valid(tile)):
-                for k in range(K):
-                    lane = k % p.per_row * p.slot + k // p.per_row * p.run + r
-                    order[(tile * p.run + r) * K + k, tile * p.lanes + lane] = 1.0
+        order = np.zeros((p.chips, p.pairs * K, p.tiles * p.lanes), np.float32)
+        for chip in range(p.chips):
+            for tile in range(p.tiles):
+                at = ((tile // 2 ^ chip) * 2 + tile % 2) * p.lanes
+                for r in range(p.valid(tile)):
+                    for k in range(K):
+                        lane = k % p.per_row * p.slot + k // p.per_row * p.run + r
+                        order[chip, (tile * p.run + r) * K + k, at + lane] = 1.0
         order = jnp.asarray(order).astype(BF16)
 
         field = (p.c, xy, p.z)
-        slots = (p.half, p.slot, LANES)
+        slots = (p.devices, p.slot, LANES)
         packed = (p.half, p.packed, LANES)
-        acc = pltpu.VMEM((xy, p.width), F32)
+        g_scr = pltpu.VMEM((groups, xy, LANES), BF16)
         s_scr = pltpu.VMEM((p.rows, p.width), F32)
-        modes_scr = pltpu.VMEM((xy, p.width), BF16)
+        modes_scr = g_scr
         blocked = pl.BlockSpec((p.step, xy, p.z), lambda n: (n, 0, 0))
         steps = (p.c // p.step,)
         place = jnp.stack([parity, g, parity * p.groups + g, t]).astype(jnp.int32)
@@ -380,17 +409,21 @@
         def in_hbm(array):
             return pltpu.with_memory_space_constraint(array, pltpu.HBM)
 
-        weights = call(
-            pack_body, p, [((p.tiles, 2, p.own, p.c // p.fold, LANES), F32)],
+        packs = call(
+            pack_body, p, [((2, 2, p.own, p.c // p.fold, LANES), F32)] * p.chips,
             [
                 pltpu.VMEM((p.own, p.c, p.pairs * K), F32),
                 pltpu.VMEM((p.own, p.c, p.pairs * K), F32),
-                pltpu.VMEM(order.shape, BF16),
+                pltpu.VMEM(order.shape[1:], BF16),
                 pltpu.SemaphoreType.DMA((3,)),
             ],
-            specs=[HBM] * 3,
-        )(in_hbm(modes_two.transpose(1, 2, 0)), in_hbm(modes_one.transpose(1, 2, 0)), in_hbm(order))[0]
-        weights = lax.all_to_all(weights, "tile", 0, 0, tiled=True)
+            specs=[SMEM] + [HBM] * 3,
+        )(place, in_hbm(modes_two.transpose(1, 2, 0)), in_hbm(modes_one.transpose(1, 2, 0)), in_hbm(order))
+        dealt = [packs[0]]
+        for chip in range(1, p.chips):
+            dealt.append(lax.ppermute(packs[chip], "tile", [(i, i ^ (2 * chip)) for i in range(p.tiles)]))
+        crossing = jnp.stack([part[1] for part in dealt])
+        crossed = lax.ppermute(crossing, "tile", partners)
 
         def exchange(parts):
             return lax.all_to_all(parts, BOTH, 0, 0, tiled=True, axis_index_groups=same)
@@ -400,9 +433,10 @@
 
         def dual(got, layer):
             body = functools.partial(dual_body, p, layer)
-            return call(lambda _, *refs: body(*refs), p, [(packed, F32)], specs=[SMEM, VMEM, VMEM])(
-                place, got, weights
-            )[0]
+            return call(
+                lambda _, *refs: body(*refs), p, [(packed, F32)], [pltpu.VMEM((p.c, LANES), F32)],
+                specs=[SMEM] + [VMEM] * (p.chips + 2),
+            )(place, got, *dealt, crossed)[0]
 
         def pointwise(w, *factors):
             return call(
@@ -416,23 +450,28 @@
             )(place, got, more, saved[0].T)[0]
             return out.transpose(2, 0, 1)
 
-        keep, send, table = call(
-            analyse_body, p, [(slots, F32), (slots, F32), ((p.rows, xy), F32)],
-            [acc, s_scr, pltpu.VMEM(field, BF16), pltpu.SemaphoreType.DMA(steps)],
-            specs=[SMEM, VMEM, HBM] + [VMEM] * 6, grid=steps,
-        )(place, cotangent.reshape(field), in_hbm(deriv_two.reshape(field)), tz, mask, rows_x, rows_y, ex, ey)
-        part_two = keep + partner(send)
-        got_two = exchange(part_two)
+        part_two, table, turned = call(
+            analyse_body, p, [(slots, F32), ((2 * p.rows, xy), BF16), ((xy, p.rows), BF16)],
+            [
+                g_scr, s_scr, pltpu.VMEM(field, BF16), pltpu.VMEM((2 * p.rows, xy), BF16),
+                pltpu.VMEM((xy, p.rows), BF16), pltpu.SemaphoreType.DMA((groups + 2,)),
+            ],
+            specs=[SMEM, VMEM, HBM] + [VMEM] * 6, out_specs=[VMEM, HBM, HBM], grid=steps,
+        )(place, cotangent.reshape(field), in_hbm(deriv_two.reshape(field)), tz, lines, rows_x, rows_y, ex, ey)
+        got_two = lax.all_to_all(part_two, BOTH, 0, 0, tiled=True)
         point_out = pointwise(point_two, cotangent.reshape(field), deriv_two.reshape(field))
         share_two = dual(got_two, 0)
         all_two = exchange(share_two)
         more_two = partner(all_two)
-        gated_one, keep, send = call(
-            synth_analyse_body, p, [(field, BF16), (slots, F32), (slots, F32)], [acc, s_scr, s_scr, modes_scr, pltpu.VMEM(field, BF16), pltpu.SemaphoreType.DMA(steps)],
-            count=7, out_specs=[HBM, VMEM, VMEM], grid=steps,
-        )(all_two, more_two, point_out, deriv_one.reshape(field), tz, mask, table)
-        part_one = keep + partner(send)
-        got_one = exchange(part_one)
+        gated_one, part_one = call(
+            synth_analyse_body, p, [(field, BF16), (slots, F32)], [
+                g_scr, s_scr, s_scr, modes_scr, pltpu.VMEM(field, BF16), pltpu.VMEM(tz.shape, BF16),
+                pltpu.VMEM(turned.shape, BF16), pltpu.VMEM(table.shape, BF16),
+                pltpu.SemaphoreType.DMA(steps), pltpu.SemaphoreType.DMA((3,)),
+            ],
+            specs=[SMEM] + [VMEM] * 5 + [HBM] * 3, out_specs=[HBM, VMEM], grid=steps,
+        )(place, all_two, more_two, point_out, deriv_one.reshape(field), lines, in_hbm(tz), in_hbm(turned), in_hbm(table))
+        got_one = lax.all_to_all(part_one, BOTH, 0, 0, tiled=True)
         grad_two = grad(all_two, more_two, saved_two)
         point_out = pointwise(point_one, gated_one)
         share_one = dual(got_one, 1)
@@ -443,7 +482,7 @@
             specs=[SMEM] + [VMEM] * 7,
             out_specs=[blocked, pl.BlockSpec((p.own, p.c, p.pairs * K), lambda n: (0, 0, 0))],
             grid=steps,
-        )(place, all_one, more_one, point_out, tz, mask, table, saved_one[0].T)
+        )(place, all_one, more_one, point_out, tz, lines, turned, saved_one[0].T)
         grad_one = grad_one.transpose(2, 0, 1)
         return (result.reshape(shape), grad_one, grad_two)
 

time: 91.7 us -> 80.1 us (0.87)
  blocking collectives: 34.8 us -> 24.5 us
  local copies, waits for them, and re-layouts: 8.57 us -> 3.77 us
  starting transfers between devices: 12.7 us -> 14.7 us
  waiting for transfers between devices: 13 us -> 14.7 us
    all_to_all x2 -> x1, blocking collectives: 22.7 us -> 11.8 us  [exchange(): return lax.all_to_all(parts, BOTH, 0, 0, tiled=True, axis_index_groups=same)]
    all_to_all x0 -> x1, waiting for transfers between devices: none -> 8.83 us  [local(): got_two = lax.all_to_all(part_two, BOTH, 0, 0, tiled=True)]
    all_to_all x2 -> x1, starting transfers between devices: 11.7 us -> 3.52 us  [exchange(): return lax.all_to_all(parts, BOTH, 0, 0, tiled=True, axis_index_groups=same)]
    all_to_all x2 -> x1, waiting for transfers between devices: 10.9 us -> 4.41 us  [exchange(): return lax.all_to_all(parts, BOTH, 0, 0, tiled=True, axis_index_groups=same)]
    all_to_all x0 -> x1, starting transfers between devices: none -> 6.32 us  [local(): got_two = lax.all_to_all(part_two, BOTH, 0, 0, tiled=True)]
    ppermute x0 -> x4, starting transfers between devices: none -> 4.88 us  [the longest x3 4.57 us: local(): lax.ppermute(packs[chip], 'tile', [(i, i ^ 2 * chip) for i in range(p.til...]
    unnamed x40 -> x38, local copies, waits for them, and re-layouts: 8.57 us -> 3.74 us
    ppermute x4 -> x2, waiting for transfers between devices: 2.1 us -> 0.16 us  [partner(): return lax.ppermute(parts, 'tile', partners)]
  transfers between devices with their start and end apart: 6 -> 8, of which waited for: 5 -> 4; matrix products, arithmetic and copies ran while one was open for 0% -> 0% of each run, Pallas kernels for 7% -> 10%
where the time goes in v1:
time: 80.1 us; the launch traced here: 79.7 us
  blocking collectives  24.5 us (31%)
  Pallas kernels  20.9 us (26%)
  starting transfers between devices  14.7 us (18%)
  waiting for transfers between devices  14.7 us (18%)
  local copies, waits for them, and re-layouts  3.77 us (5%)
  between operations  0.92 us (1%)
    all_to_all x1, blocking collectives, local(): got_one = lax.all_to_all(part_one, BOTH, 0, 0, tiled=True)  12.7 us
    all_to_all x1, blocking collectives, exchange(): return lax.all_to_all(parts, BOTH, 0, 0, tiled=True, axis_index_groups=same)  11.8 us
    all_to_all x1, waiting for transfers between devices, local(): got_two = lax.all_to_all(part_two, BOTH, 0, 0, tiled=True)  8.83 us
    all_to_all x1, starting transfers between devices, local(): got_two = lax.all_to_all(part_two, BOTH, 0, 0, tiled=True)  6.32 us
    ppermute x3, starting transfers between devices, local(): lax.ppermute(packs[chip], 'tile', [(i, i ^ 2 * chip) for i in range(p.til...  4.57 us
    pallas_call x1, Pallas kernels, local(): call(synth_analyse_body, p, [(field, BF16), (slots, F32)], [g_scr, s_scr,...  4.42 us
    all_to_all x1, waiting for transfers between devices, exchange(): return lax.all_to_all(parts, BOTH, 0, 0, tiled=True, axis_index_groups=same)  4.41 us
    pallas_call x1, Pallas kernels, local(): call(analyse_body, p, [(slots, F32), ((2 * p.rows, xy), BF16), ((xy, p.ro...  4.08 us
  transfers between devices with their start and end apart: 8, of which 4 were waited for; matrix products, arithmetic and copies ran while one was open for 0% of the time, Pallas kernels for 10%

profile of v1, /device:TPU:0, one launch (start us, length us, event | category | flops | bytes accessed | tf_op | source)
XLA Modules:
  0.0 79.7 jit_solution(1908268233757149684)
XLA Ops:
  0.6 0.1 pad_add_fusion.place_ref.refs_0_
  0.7 0.0 copy-start.12
  0.7 0.0 copy-start.13
  0.8 0.0 copy-start.14
  0.8 2.7 %shard_map.185 = (f32[2,2,4,16,128]{4,3,2,1,0:T(8,128)S(1)}, f32[2,2,4,16,128]{4,3,2,1,0:T(8,128)S(1)}, f32[2,2,4,16,128]{4,3,2,1,0:T(8,128)S(1)}, f32[2,2,4,16,128]{4,3,2,1,0:T(8,128)S(1)}) custom-call(s32[4]{0:T(128)S(1)} %pad_add_fusion.place_ref.refs_0_, f32[4,32,432]{2,1,0:T(8,128)} %bitcast.25, f32[4,32,432]{2,1,0:T(8,128)} %bitcast.26, ...), custom_call_target="tpu_custom_call" | custom-call | flops 2147483648 | bytes 2147483 | tf_op jit(solution)/shard_map/pallas_call | solution.py:412
  3.4 3.0 %collective-permute-start = (f32[2,2,4,16,128]{4,3,2,1,0:T(8,128)S(1)}, f32[2,2,4,16,128]{4,3,2,1,0:T(8,128)S(1)}, u32[]{:S(2)}, u32[]{:S(2)}) collective-permute-start(f32[2,2,4,16,128]{4,3,2,1,0:T(8,128)S(1)} %get-tuple-element.16), channel_id=1, source_target_pairs={{0,2},{1,3},{2,0},{3,1},{4,6},{5,7},{6,4},{7,5},{8,10},{9,11},{10,... | collective-permute-start | bytes 393224 | tf_op jit(solution)/shard_map/ppermute | solution.py:424
  6.5 1.5 %collective-permute-start.1 = (f32[2,2,4,16,128]{4,3,2,1,0:T(8,128)S(1)}, f32[2,2,4,16,128]{4,3,2,1,0:T(8,128)S(1)}, u32[]{:S(2)}, u32[]{:S(2)}) collective-permute-start(f32[2,2,4,16,128]{4,3,2,1,0:T(8,128)S(1)} %get-tuple-element.17), channel_id=1, source_target_pairs={{0,4},{1,5},{2,6},{3,7},{4,0},{5,1},{6,2},{7,3},{8,12},{9,13},{10,... | collective-permute-start | bytes 393224 | tf_op jit(solution)/shard_map/ppermute | solution.py:424
  8.0 0.0 collective-permute-start.2
  8.0 0.0 copy-done
  8.0 0.0 copy-done.7
  8.0 0.0 copy-done.8
  8.0 0.0 copy-done.11
  8.0 0.0 copy-done.12
  8.0 4.1 %shard_map.184 = (f32[32,16,128]{2,1,0:T(8,128)}, bf16[320,192]{1,0:T(8,128)(2,1)}, bf16[192,160]{1,0:T(8,128)(2,1)}) custom-call(s32[4]{0:T(128)S(1)} %pad_add_fusion.place_ref.refs_0_, bf16[32,192,128]{2,1,0:T(8,128)(2,1)S(1)} %bitcast.18, bf16[32,192,128]{2,1,0:T(8,128)(2,1)} %bitcast.20, bf16[128,1024]{1,0:T(8,128)(2,1)S(1)} %copy-done.8, ...), custom_call_target="tpu_custom_call" | custom-call | flops 2147483648 | bytes 2147483 | tf_op jit(solution)/shard_map/pallas_call | solution.py:453
  12.1 6.3 %all-to-all-start = ((f32[32,16,128]{2,1,0:T(8,128)}), f32[32,16,128]{2,1,0:T(8,128)S(1)}, u32[]{:S(2)}, u32[]{:S(2)}) async-start(f32[32,16,128]{2,1,0:T(8,128)} %get-tuple-element.14), calls=%async_computation | async-start | bytes 524288 | tf_op jit(solution)/shard_map/all_to_all | solution.py:461
  18.5 0.0 collective-permute-done.refs_3_
  18.5 0.0 collective-permute-done.1.refs_4_
  18.5 0.0 collective-permute-done.2.refs_5_
  18.6 0.0 copy-start.5
  18.6 0.0 copy-start.10
  18.6 0.3 collective-permute-start.3
  18.9 1.3 %collective-permute-done.3.refs_6_ = f32[4,2,4,16,128]{4,3,2,1,0:T(8,128)S(1)} collective-permute-done((f32[4,2,4,16,128]{4,3,2,1,0:T(8,128)S(1)}, f32[4,2,4,16,128]{4,3,2,1,0:T(8,128)S(1)}, u32[]{:S(2)}, u32[]{:S(2)}) %collective-permute-start.3) | collective-permute-done | bytes 262176 | tf_op jit(solution)/shard_map/ppermute | solution.py:426
  20.2 8.8 %all-to-all-done.refs_1_ = f32[32,16,128]{2,1,0:T(8,128)S(1)} async-done(((f32[32,16,128]{2,1,0:T(8,128)}), f32[32,16,128]{2,1,0:T(8,128)S(1)}, u32[]{:S(2)}, u32[]{:S(2)}) %all-to-all-start) | async-done | bytes 262176 | tf_op jit(solution)/shard_map/all_to_all | solution.py:461
  29.0 1.0 %shard_map.186 = f32[16,24,128]{2,1,0:T(8,128)S(1)} custom-call(s32[4]{0:T(128)S(1)} %pad_add_fusion.place_ref.refs_0_, f32[32,16,128]{2,1,0:T(8,128)S(1)} %all-to-all-done.refs_1_, f32[2,2,4,16,128]{4,3,2,1,0:T(8,128)S(1)} %get-tuple-element.15.refs_2_, f32[2,2,4,16,128]{4,3,2,1,0:T(8,128)S(1)} %collective-permute-done.refs_3_, ...), custom_call_target="tpu_custom_call" | custom-call | flops 2147483648 | bytes 2147483 | tf_op jit(solution)/shard_map/pallas_call | solution.py:436
  30.0 11.8 %all_to_all.20.got_ref = f32[16,24,128]{2,1,0:T(8,128)S(1)} all-to-all(f32[16,24,128]{2,1,0:T(8,128)S(1)} %shard_map.186), channel_id=1, replica_groups={{0,2,4,6,8,10,12,14,16,18,20,22,24,26,28,30},{1,3,5,7,9,11,13,15,17,19,..., dimensions={0} | all-to-all | bytes 393216 | tf_op jit(solution)/shard_map/all_to_all | solution.py:429
  41.9 0.0 collective-permute-start.4
  41.9 1.3 %shard_map.187.point_ref = f32[32,192,128]{2,1,0:T(8,128)S(1)} custom-call(bf16[32,192,128]{2,1,0:T(8,128)(2,1)S(1)} %bitcast.19, bf16[32,192,128]{2,1,0:T(8,128)(2,1)S(1)} %bitcast.21, bf16[32,32]{1,0:T(8,128)(2,1)S(1)} %copy-done.5, bf16[512,32]{1,0:T(8,128)(2,1)S(1)} %copy-done.10), custom_call_target="tpu_custom_call" | custom-call | flops 2147483648 | bytes 2147483 | tf_op jit(solution)/shard_map/pallas_call | solution.py:442
  43.1 0.2 collective-permute-done.4.more_ref
  43.3 0.0 copy-done.2
  43.3 4.4 %shard_map.188 = (bf16[32,192,128]{2,1,0:T(8,128)(2,1)}, f32[32,16,128]{2,1,0:T(8,128)S(1)}) custom-call(s32[4]{0:T(128)S(1)} %pad_add_fusion.place_ref.refs_0_, f32[16,24,128]{2,1,0:T(8,128)S(1)} %all_to_all.20.got_ref, f32[16,24,128]{2,1,0:T(8,128)S(1)} %collective-permute-done.4.more_ref, f32[32,192,128]{2,1,0:T(8,128)S(1)} %shard_map.187.point_ref, ...), custom_call_target="tpu_custom_call" | custom-call | flops 2147483648 | bytes 2147483 | tf_op jit(solution)/shard_map/pallas_call | solution.py:466
  47.7 12.7 %all_to_all.21.refs_1_ = f32[32,16,128]{2,1,0:T(8,128)S(1)} all-to-all(f32[32,16,128]{2,1,0:T(8,128)S(1)} %get-tuple-element.21), channel_id=1, replica_groups=mesh['grp'=4,'tile'=8] {'grp','tile'}, dimensions={0} | all-to-all | bytes 524288 | tf_op jit(solution)/shard_map/all_to_all | solution.py:474
  60.4 1.7 %shard_map.189 = f32[16,24,128]{2,1,0:T(8,128)} custom-call(s32[4]{0:T(128)S(1)} %pad_add_fusion.place_ref.refs_0_, f32[32,16,128]{2,1,0:T(8,128)S(1)} %all_to_all.21.refs_1_, f32[2,2,4,16,128]{4,3,2,1,0:T(8,128)S(1)} %get-tuple-element.15.refs_2_, f32[2,2,4,16,128]{4,3,2,1,0:T(8,128)S(1)} %collective-permute-done.refs_3_, ...), custom_call_target="tpu_custom_call" | custom-call | flops 2147483648 | bytes 2147483 | tf_op jit(solution)/shard_map/pallas_call | solution.py:436
  62.1 3.5 %all-to-all-start.3 = ((f32[16,24,128]{2,1,0:T(8,128)}), f32[16,24,128]{2,1,0:T(8,128)S(1)}, u32[]{:S(2)}, u32[]{:S(2)}) async-start(f32[16,24,128]{2,1,0:T(8,128)} %shard_map.189), calls=%async_computation.3 | async-start | bytes 393216 | tf_op jit(solution)/shard_map/all_to_all | solution.py:429
  65.6 0.0 copy-start.15
  65.6 1.4 %copy-done.15 = bf16[32,192,128]{2,1,0:T(8,128)(2,1)S(1)} copy-done((bf16[32,192,128]{2,1,0:T(8,128)(2,1)S(1)}, bf16[32,192,128]{2,1,0:T(8,128)(2,1)}, u32[]{:S(2)}) %copy-start.15) | copy-done | bytes 1572888
  67.0 1.2 %shard_map.190.point_ref = f32[32,192,128]{2,1,0:T(8,128)S(1)} custom-call(bf16[32,192,128]{2,1,0:T(8,128)(2,1)S(1)} %copy-done.15, bf16[32,32]{1,0:T(8,128)(2,1)S(1)} %copy-done.6, bf16[512,32]{1,0:T(8,128)(2,1)S(1)} %copy-done.10), custom_call_target="tpu_custom_call" | custom-call | flops 2147483648 | bytes 2147483 | tf_op jit(solution)/shard_map/pallas_call | solution.py:442
  68.3 1.6 %copy-done.16 = f32[32,192,128]{2,1,0:T(8,128)} copy-done((f32[32,192,128]{2,1,0:T(8,128)}, f32[32,192,128]{2,1,0:T(8,128)S(1)}, u32[]{:S(2)}) %copy-start.16) | copy-done | bytes 3145752
  69.9 4.4 %all-to-all-done.3.got_ref = f32[16,24,128]{2,1,0:T(8,128)S(1)} async-done(((f32[16,24,128]{2,1,0:T(8,128)}), f32[16,24,128]{2,1,0:T(8,128)S(1)}, u32[]{:S(2)}, u32[]{:S(2)}) %all-to-all-start.3) | async-done | bytes 196640 | tf_op jit(solution)/shard_map/all_to_all | solution.py:429
  74.3 0.0 collective-permute-start.5
  74.3 0.0 copy-done.3
  74.3 0.0 copy-start.9
  74.3 0.0 copy-start.17
  74.3 0.0 copy-start.18
  74.3 1.4 %shard_map.192 = f32[4,32,432]{2,1,0:T(8,128)} custom-call(s32[4]{0:T(128)S(1)} %pad_add_fusion.place_ref.refs_0_, f32[16,24,128]{2,1,0:T(8,128)S(1)} %all_to_all.20.got_ref, f32[16,24,128]{2,1,0:T(8,128)S(1)} %collective-permute-done.4.more_ref, f32[32,432]{1,0:T(8,128)S(1)} %bitcast.23), custom_call_target="tpu_custom_call" | custom-call | flops 2147483648 | bytes 2147483 | tf_op jit(solution)/shard_map/pallas_call | solution.py:448
  75.8 0.0 collective-permute-done.5.more_ref
  75.8 0.0 copy-done.9
  75.8 0.6 copy-done.17
  76.4 3.2 %shard_map.191 = (bf16[32,192,128]{2,1,0:T(8,128)(2,1)}, f32[4,32,432]{2,1,0:T(8,128)}) custom-call(s32[4]{0:T(128)S(1)} %pad_add_fusion.place_ref.refs_0_, f32[16,24,128]{2,1,0:T(8,128)S(1)} %all-to-all-done.3.got_ref, f32[16,24,128]{2,1,0:T(8,128)S(1)} %collective-permute-done.5.more_ref, f32[32,192,128]{2,1,0:T(8,128)S(1)} %copy-done.17, ...), custom_call_target="tpu_custom_call" | custom-call | flops 2147483648 | bytes 2147483 | tf_op jit(solution)/shard_map/pallas_call | solution.py:480
  (23 shorter events, 0.1 us)
Async XLA Ops:
  0.7 7.3 %copy-start = (bf16[1,32,12,16,128]{4,3,2,1,0:T(8,128)(2,1)S(1)}, bf16[1,32,12,16,128]{4,3,2,1,0:T(8,128)(2,1)}, u32[]{:S(2)}) copy-start(bf16[1,32,12,16,128]{4,3,2,1,0:T(8,128)(2,1)} %param.17) | copy-start | bytes 4718596
  0.7 7.3 %copy-start.7 = (bf16[384,512]{1,0:T(8,128)(2,1)S(1)}, bf16[384,512]{1,0:T(8,128)(2,1)}, u32[]{:S(2)}) copy-start(bf16[384,512]{1,0:T(8,128)(2,1)} %constant.50.order_ref) | copy-start | bytes 1179652
  0.7 7.3 %copy-start.8 = (bf16[128,1024]{1,0:T(8,128)(2,1)S(1)}, bf16[128,1024]{1,0:T(8,128)(2,1)}, u32[]{:S(2)}) copy-start(bf16[128,1024]{1,0:T(8,128)(2,1)} %constant.49.tz_ref.tz_hbm) | copy-start | bytes 786436
  0.7 7.3 %copy-start.11 = (f32[8,12,160]{2,1,0:T(8,128)S(1)}, f32[8,12,160]{2,1,0:T(8,128)}, u32[]{:S(2)}) copy-start(f32[8,12,160]{2,1,0:T(8,128)} %constant.39.clone.rx_ref) | copy-start | bytes 184324
  0.7 7.3 %copy-start.12 = (f32[8,16,160]{2,1,0:T(8,128)S(1)}, f32[8,16,160]{2,1,0:T(8,128)}, u32[]{:S(2)}) copy-start(f32[8,16,160]{2,1,0:T(8,128)} %constant.40.clone.ry_ref) | copy-start | bytes 245764
  0.7 7.3 %copy-start.13 = (f32[12,192]{1,0:T(8,128)S(1)}, f32[12,192]{1,0:T(8,128)}, u32[]{:S(2)}) copy-start(f32[12,192]{1,0:T(8,128)} %constant.41.clone.ex_ref) | copy-start | bytes 27652
  0.8 7.3 %copy-start.14 = (f32[16,192]{1,0:T(8,128)S(1)}, f32[16,192]{1,0:T(8,128)}, u32[]{:S(2)}) copy-start(f32[16,192]{1,0:T(8,128)} %constant.42.clone.ey_ref) | copy-start | bytes 36868
  3.4 15.0 %collective-permute-start = (f32[2,2,4,16,128]{4,3,2,1,0:T(8,128)S(1)}, f32[2,2,4,16,128]{4,3,2,1,0:T(8,128)S(1)}, u32[]{:S(2)}, u32[]{:S(2)}) collective-permute-start(f32[2,2,4,16,128]{4,3,2,1,0:T(8,128)S(1)} %get-tuple-element.16), channel_id=1, source_target_pairs={{0,2},{1,3},{2,0},{3,1},{4,6},{5,7},{6,4},{7,5},{8,10},{9,11},{10,... | collective-permute-start | bytes 393224 | tf_op jit(solution)/shard_map/ppermute | solution.py:424
  6.5 12.0 %collective-permute-start.1 = (f32[2,2,4,16,128]{4,3,2,1,0:T(8,128)S(1)}, f32[2,2,4,16,128]{4,3,2,1,0:T(8,128)S(1)}, u32[]{:S(2)}, u32[]{:S(2)}) collective-permute-start(f32[2,2,4,16,128]{4,3,2,1,0:T(8,128)S(1)} %get-tuple-element.17), channel_id=1, source_target_pairs={{0,4},{1,5},{2,6},{3,7},{4,0},{5,1},{6,2},{7,3},{8,12},{9,13},{10,... | collective-permute-start | bytes 393224 | tf_op jit(solution)/shard_map/ppermute | solution.py:424
  8.0 10.5 %collective-permute-start.2 = (f32[2,2,4,16,128]{4,3,2,1,0:T(8,128)S(1)}, f32[2,2,4,16,128]{4,3,2,1,0:T(8,128)S(1)}, u32[]{:S(2)}, u32[]{:S(2)}) collective-permute-start(f32[2,2,4,16,128]{4,3,2,1,0:T(8,128)S(1)} %get-tuple-element.18), channel_id=1, source_target_pairs={{0,6},{1,7},{2,4},{3,5},{4,2},{5,3},{6,0},{7,1},{8,14},{9,15},{10,... | collective-permute-start | bytes 393224 | tf_op jit(solution)/shard_map/ppermute | solution.py:424
  12.1 16.9 %all-to-all-start = ((f32[32,16,128]{2,1,0:T(8,128)}), f32[32,16,128]{2,1,0:T(8,128)S(1)}, u32[]{:S(2)}, u32[]{:S(2)}) async-start(f32[32,16,128]{2,1,0:T(8,128)} %get-tuple-element.14), calls=%async_computation | async-start | bytes 524288 | tf_op jit(solution)/shard_map/all_to_all | solution.py:461
  18.6 23.3 %copy-start.5 = (bf16[32,32]{1,0:T(8,128)(2,1)S(1)}, bf16[32,32]{1,0:T(8,128)(2,1)}, u32[]{:S(2)}) copy-start(bf16[32,32]{1,0:T(8,128)(2,1)} %refs_2_.1) | copy-start | bytes 6148
  18.6 23.3 %copy-start.10 = (bf16[512,32]{1,0:T(8,128)(2,1)S(1)}, bf16[512,32]{1,0:T(8,128)(2,1)}, u32[]{:S(2)}) copy-start(bf16[512,32]{1,0:T(8,128)(2,1)} %constant.52.refs_3_.refs_2_) | copy-start | bytes 98308
  18.6 1.6 %collective-permute-start.3 = (f32[4,2,4,16,128]{4,3,2,1,0:T(8,128)S(1)}, f32[4,2,4,16,128]{4,3,2,1,0:T(8,128)S(1)}, u32[]{:S(2)}, u32[]{:S(2)}) collective-permute-start(f32[4,2,4,16,128]{4,3,2,1,0:T(8,128)S(1)} %pad_maximum_fusion), channel_id=1, source_target_pairs={{0,1},{1,0},{2,3},{3,2},{4,5},{5,4},{6,7},{7,6},{8,9},{9,8},{10,11... | collective-permute-start | bytes 786440 | tf_op jit(solution)/shard_map/ppermute | solution.py:426
  29.0 12.8 %copy-start.1 = (bf16[1,32,12,16,128]{4,3,2,1,0:T(8,128)(2,1)S(1)}, bf16[1,32,12,16,128]{4,3,2,1,0:T(8,128)(2,1)}, u32[]{:S(2)}) copy-start(bf16[1,32,12,16,128]{4,3,2,1,0:T(8,128)(2,1)} %param.18) | copy-start | bytes 4718596
  41.9 1.4 %copy-start.2 = (bf16[1,32,12,16,128]{4,3,2,1,0:T(8,128)(2,1)S(1)}, bf16[1,32,12,16,128]{4,3,2,1,0:T(8,128)(2,1)}, u32[]{:S(2)}) copy-start(bf16[1,32,12,16,128]{4,3,2,1,0:T(8,128)(2,1)} %param.19) | copy-start | bytes 4718596
  41.9 1.4 %collective-permute-start.4 = (f32[16,24,128]{2,1,0:T(8,128)S(1)}, f32[16,24,128]{2,1,0:T(8,128)S(1)}, u32[]{:S(2)}, u32[]{:S(2)}) collective-permute-start(f32[16,24,128]{2,1,0:T(8,128)S(1)} %all_to_all.20.got_ref), channel_id=1, source_target_pairs={{0,1},{1,0},{2,3},{3,2},{4,5},{5,4},{6,7},{7,6},{8,9},{9,8},{10,11... | collective-permute-start | bytes 589832 | tf_op jit(solution)/shard_map/ppermute | solution.py:432
  60.4 5.2 %copy-start.6 = (bf16[32,32]{1,0:T(8,128)(2,1)S(1)}, bf16[32,32]{1,0:T(8,128)(2,1)}, u32[]{:S(2)}) copy-start(bf16[32,32]{1,0:T(8,128)(2,1)} %refs_1_.1) | copy-start | bytes 6148
  62.1 12.2 %all-to-all-start.3 = ((f32[16,24,128]{2,1,0:T(8,128)}), f32[16,24,128]{2,1,0:T(8,128)S(1)}, u32[]{:S(2)}, u32[]{:S(2)}) async-start(f32[16,24,128]{2,1,0:T(8,128)} %shard_map.189), calls=%async_computation.3 | async-start | bytes 393216 | tf_op jit(solution)/shard_map/all_to_all | solution.py:429
  65.6 1.4 %copy-start.15 = (bf16[32,192,128]{2,1,0:T(8,128)(2,1)S(1)}, bf16[32,192,128]{2,1,0:T(8,128)(2,1)}, u32[]{:S(2)}) copy-start(bf16[32,192,128]{2,1,0:T(8,128)(2,1)} %get-tuple-element.22.refs_0_) | copy-start | bytes 4718596
  67.0 7.3 %copy-start.3 = (f32[1,432,32]{1,2,0:T(8,128)S(1)}, f32[1,432,32]{1,2,0:T(8,128)}, u32[]{:S(2)}) copy-start(f32[1,432,32]{1,2,0:T(8,128)} %param.24) | copy-start | bytes 165892
  68.3 1.6 %copy-start.16 = (f32[32,192,128]{2,1,0:T(8,128)}, f32[32,192,128]{2,1,0:T(8,128)S(1)}, u32[]{:S(2)}) copy-start(f32[32,192,128]{2,1,0:T(8,128)S(1)} %shard_map.190.point_ref) | copy-start | bytes 9437188
  74.3 1.5 %collective-permute-start.5 = (f32[16,24,128]{2,1,0:T(8,128)S(1)}, f32[16,24,128]{2,1,0:T(8,128)S(1)}, u32[]{:S(2)}, u32[]{:S(2)}) collective-permute-start(f32[16,24,128]{2,1,0:T(8,128)S(1)} %all-to-all-done.3.got_ref), channel_id=1, source_target_pairs={{0,1},{1,0},{2,3},{3,2},{4,5},{5,4},{6,7},{7,6},{8,9},{9,8},{10,11... | collective-permute-start | bytes 589832 | tf_op jit(solution)/shard_map/ppermute | solution.py:432
  74.3 1.5 %copy-start.4 = (f32[1,432,32]{1,2,0:T(8,128)S(1)}, f32[1,432,32]{1,2,0:T(8,128)}, u32[]{:S(2)}) copy-start(f32[1,432,32]{1,2,0:T(8,128)} %param.25) | copy-start | bytes 165892
  74.3 1.5 %copy-start.9 = (bf16[128,1024]{1,0:T(8,128)(2,1)S(1)}, bf16[128,1024]{1,0:T(8,128)(2,1)}, u32[]{:S(2)}) copy-start(bf16[128,1024]{1,0:T(8,128)(2,1)} %constant.49.tz_ref.tz_hbm) | copy-start | bytes 786436
  74.3 2.1 %copy-start.17 = (f32[32,192,128]{2,1,0:T(8,128)S(1)}, f32[32,192,128]{2,1,0:T(8,128)}, u32[]{:S(2)}) copy-start(f32[32,192,128]{2,1,0:T(8,128)} %copy-done.16) | copy-start | bytes 9437188
  74.3 2.1 %copy-start.18 = (bf16[192,160]{1,0:T(8,128)(2,1)S(1)}, bf16[192,160]{1,0:T(8,128)(2,1)}, u32[]{:S(2)}) copy-start(bf16[192,160]{1,0:T(8,128)(2,1)} %get-tuple-element.19.turned_hbm.turned_ref) | copy-start | bytes 184324

commit v2 on v1

--- a/solution.py
+++ b/solution.py
@@ -14,11 +14,9 @@
 LANES = 128
 SUB = 8
 COST = 1 << 31
-HIGH = lax.Precision.HIGHEST
 BOTH = ("grp", "tile")
 VMEM = pl.BlockSpec(memory_space=pltpu.VMEM)
 HBM = pl.BlockSpec(memory_space=pltpu.HBM)
-SMEM = pl.BlockSpec(memory_space=pltpu.SMEM)
 F32 = jnp.float32
 BF16 = jnp.bfloat16
 
@@ -33,6 +31,17 @@
     values = np.where(orders[:, None] % 2 == 1, factor * np.cos(angle), factor * np.sin(angle))
     values[0] = 1.0 / math.sqrt(length)
     return values.astype(np.float32)
+
+
+def place_of(plan):
+    group, tile = lax.axis_index("grp"), lax.axis_index("tile")
+    parity = jnp.bitwise_and(tile, 1)
+    return parity, group, parity * plan.groups + group, tile
+
+
+def two_parts(table):
+    high = table.astype(jnp.bfloat16)
+    return jnp.asarray(np.concatenate([high, (table - high.astype(np.float32)).astype(jnp.bfloat16)], axis=1))
 
 
 class Plan:
@@ -76,8 +85,9 @@
     )
 
 
-def emit_slots(plan, place_ref, g_ref, order_ref, table_ref, slots_ref, s_ref):
-    p = plan
+def emit_slots(plan, g_ref, order_ref, table_ref, slots_ref, s_ref):
+    p = plan
+    place_ref = place_of(p)
     lines = jnp.concatenate([g_ref[n] for n in range(p.c // p.step)], axis=1)
     lines = lax.dot_general(lines, order_ref[...], (((1,), (1,)), ((), ())), preferred_element_type=F32).astype(BF16)
     both = jnp.dot(table_ref[...], lines, preferred_element_type=F32)
@@ -98,16 +108,15 @@
 
 
 def spread_rows(rows, cells):
-    return lax.dot_general(
-        rows, cells, (((0,), (0,)), ((), ())), precision=HIGH, preferred_element_type=F32
-    )
+    return lax.dot_general(rows, cells, (((0,), (0,)), ((), ())), preferred_element_type=F32)
 
 
 def analyse_body(
-    plan, place_ref, up_ref, der_hbm, tz_ref, order_ref, rx_ref, ry_ref, ex_ref, ey_ref,
+    plan, up_ref, der_hbm, tz_ref, order_ref, rx_ref, ry_ref, ex_ref, ey_ref,
     slots_ref, table_hbm, turned_hbm, g_ref, s_ref, der_ref, table_ref, turned_ref, sems,
 ):
     p = plan
+    place_ref = place_of(p)
     step = pl.program_id(0)
 
     def fetch(n):
@@ -141,7 +150,7 @@
 
     @pl.when(step == pl.num_programs(0) - 1)
     def _():
-        emit_slots(p, place_ref, g_ref, order_ref, table_ref, slots_ref, s_ref)
+        emit_slots(p, g_ref, order_ref, table_ref, slots_ref, s_ref)
         for copy in tables:
             copy.wait()
 
@@ -163,7 +172,7 @@
 
 
 def synth_analyse_body(
-    plan, place_ref, got_ref, more_ref, point_ref, der_ref, order_ref, tz_hbm, turned_hbm, table_hbm,
+    plan, got_ref, more_ref, point_ref, der_ref, order_ref, tz_hbm, turned_hbm, table_hbm,
     gated_ref, slots_ref, g_ref, s_ref, d_ref, modes_ref, field_ref, tz_ref, turned_ref, table_ref, sems, table_sems,
 ):
     p = plan
@@ -198,13 +207,13 @@
 
     @pl.when(step == pl.num_programs(0) - 1)
     def _():
-        emit_slots(p, place_ref, g_ref, order_ref, table_ref, slots_ref, s_ref)
+        emit_slots(p, g_ref, order_ref, table_ref, slots_ref, s_ref)
         for n in range(p.c // p.step):
             store(n).wait()
 
 
 def synth_body(
-    plan, place_ref, got_ref, more_ref, point_ref, tz_ref, order_ref, turned_ref, saved_ref, out_ref, grad_ref,
+    plan, got_ref, more_ref, point_ref, tz_ref, order_ref, turned_ref, saved_ref, out_ref, grad_ref,
     d_ref, modes_ref,
 ):
     p = plan
@@ -213,7 +222,7 @@
     @pl.when(step == 0)
     def _():
         gather_modes(p, got_ref, more_ref, order_ref, turned_ref, d_ref, modes_ref)
-        grad_body(p, place_ref, got_ref, more_ref, saved_ref, grad_ref)
+        grad_body(p, got_ref, more_ref, saved_ref, grad_ref)
 
     first = step * p.step
     synth = jnp.dot(modes_ref[step], tz_ref[...], preferred_element_type=F32)
@@ -244,41 +253,49 @@
             )
 
 
-def pack_body(plan, place_ref, two_hbm, one_hbm, order_hbm, *refs):
-    p = plan
-    *out_refs, two_ref, one_ref, order_ref, sems = refs
+def pack_body(plan, two_hbm, one_hbm, target_hbm, odd_ref, *refs):
+    p = plan
+    place_ref = place_of(p)
+    *even_refs, two_ref, one_ref, target_ref, order_ref, sems = refs
     n = p.own * p.c
     rows = p.c // p.fold
     copies = [
         pltpu.make_async_copy(two_hbm, two_ref, sems.at[0]),
-        pltpu.make_async_copy(order_hbm.at[place_ref[3] // 2], order_ref, sems.at[1]),
-        pltpu.make_async_copy(one_hbm, one_ref, sems.at[2]),
+        pltpu.make_async_copy(one_hbm, one_ref, sems.at[1]),
+        pltpu.make_async_copy(target_hbm, target_ref, sems.at[2]),
     ]
-    for copy in copies:
+    for copy in (copies[2], *copies[:2]):
         copy.start()
+    copies[2].wait()
+    mode = lax.broadcasted_iota(jnp.int32, order_ref.shape, 0)
+    order_ref[...] = jnp.where(mode == target_ref[lax.div(place_ref[3], 2)], 1.0, 0.0).astype(BF16)
     for layer, w_ref in enumerate((two_ref, one_ref)):
-        copies[2 * layer].wait()
+        copies[layer].wait()
         rest = w_ref[...].reshape(n, p.pairs * K)
         parts = []
         for _ in range(2):
             parts.append(rest.astype(BF16))
             rest = rest - parts[-1].astype(F32)
-        if layer == 0:
-            copies[1].wait()
         moved = jnp.dot(jnp.concatenate(parts, axis=0), order_ref[...], preferred_element_type=F32)
         moved = moved[:n] + moved[n:]
         for o in range(p.own):
             mine = moved[o * p.c : (o + 1) * p.c]
             for t in range(p.tiles):
                 core = jnp.bitwise_xor(place_ref[0], t % 2)
-                out_refs[t // 2][core, layer, o] = jnp.concatenate(
+                chip = t // 2
+                block = jnp.concatenate(
                     [mine[f * rows : (f + 1) * rows, t * p.lanes : (t + 1) * p.lanes] for f in range(p.fold)], axis=1
                 )
-
-
-def dual_body(plan, layer, place_ref, got_ref, *refs):
-    p = plan
-    *w_refs, cross_ref, out_ref, modes_ref = refs
+                if chip % 2:
+                    odd_ref[chip // 2, core, layer, o] = block
+                else:
+                    even_refs[chip // 2][core, layer, o] = block
+
+
+def dual_body(plan, got_ref, *refs):
+    p = plan
+    place_ref = place_of(p)
+    w_refs, cross_ref, out_ref, modes_ref = refs[: p.chips], *refs[p.chips :]
     total = got_ref[0]
     for d in range(1, p.devices):
         total = total + got_ref[d]
@@ -290,9 +307,9 @@
     sums = jnp.zeros((rows, LANES), F32)
     for chip in range(p.chips):
         for core in range(2):
-            tile = jnp.bitwise_xor(place_ref[3] // 2, chip) * 2 + jnp.bitwise_xor(place_ref[0], core)
+            tile = jnp.bitwise_xor(lax.div(place_ref[3], 2), chip) * 2 + jnp.bitwise_xor(place_ref[0], core)
             for o in range(p.own):
-                w = cross_ref[chip, layer, o] if core else w_refs[chip][0, layer, o]
+                w = cross_ref[chip, o] if core else w_refs[chip][0, o]
                 sums = sums + w * modes_ref[pl.ds(tile * p.own + o, 1), :]
     down = sums.T
     pieces = []
@@ -317,8 +334,9 @@
             out_ref[d, p.slot :, :] = both
 
 
-def grad_body(plan, place_ref, got_ref, more_ref, saved_ref, out_ref):
-    p = plan
+def grad_body(plan, got_ref, more_ref, saved_ref, out_ref):
+    p = plan
+    place_ref = place_of(p)
     base = place_ref[1] * (p.tiles // 2)
     parity = place_ref[0]
     lane = lax.broadcasted_iota(jnp.int32, (SUB, LANES), 1)
@@ -345,8 +363,6 @@
         channels = shape[1]
         plan = p = Plan(mesh, shape[2:], channels)
         xy = p.x * p.y
-        g = lax.axis_index("grp")
-        t = lax.axis_index("tile")
 
         full_x, full_y, full_z = basis(p.x * p.groups), basis(p.y * p.tiles), basis(p.z)
         rows_x, rows_y = [], []
@@ -367,10 +383,9 @@
         rows_y = np.stack(rows_y).reshape(2, p.rows, p.tiles // 2, 2, p.y)
         rows_y = np.stack([rows_y[h, :, :, h] for h in range(2)]).transpose(2, 0, 3, 1)
         rows_y = rows_y.reshape(p.tiles, p.y, p.rows)
-        parity = t % 2
-        rows_x, rows_y = jnp.asarray(rows_x), jnp.asarray(rows_y)
-        ex = jnp.asarray(np.repeat(np.eye(p.x, dtype=np.float32), p.y, axis=1))
-        ey = jnp.asarray(np.tile(np.eye(p.y, dtype=np.float32), (1, p.x)))
+        rows_x, rows_y = two_parts(rows_x), two_parts(rows_y)
+        ex = jnp.asarray(np.tile(np.repeat(np.eye(p.x, dtype=np.float32), p.y, axis=1), (2, 1))).astype(BF16)
+        ey = jnp.asarray(np.tile(np.eye(p.y, dtype=np.float32), (2, p.x))).astype(BF16)
         groups = p.c // p.step
         tz = np.zeros((LANES, p.step, p.z), np.float32)
         lines = np.zeros((K, groups, p.step, groups, LANES), np.float32)
@@ -382,15 +397,15 @@
         lines = jnp.asarray(lines.reshape(p.width, groups * LANES)).astype(BF16)
         spread = jnp.asarray(np.repeat(np.eye(p.c, dtype=np.float32), p.y, axis=0)).astype(BF16)
 
-        order = np.zeros((p.chips, p.pairs * K, p.tiles * p.lanes), np.float32)
+        target = np.full((p.chips, 1, p.tiles * p.lanes), -1, np.int32)
         for chip in range(p.chips):
             for tile in range(p.tiles):
                 at = ((tile // 2 ^ chip) * 2 + tile % 2) * p.lanes
                 for r in range(p.valid(tile)):
                     for k in range(K):
                         lane = k % p.per_row * p.slot + k // p.per_row * p.run + r
-                        order[chip, (tile * p.run + r) * K + k, at + lane] = 1.0
-        order = jnp.asarray(order).astype(BF16)
+                        target[chip, 0, at + lane] = (tile * p.run + r) * K + k
+        target = jnp.asarray(target)
 
         field = (p.c, xy, p.z)
         slots = (p.devices, p.slot, LANES)
@@ -400,7 +415,6 @@
         modes_scr = g_scr
         blocked = pl.BlockSpec((p.step, xy, p.z), lambda n: (n, 0, 0))
         steps = (p.c // p.step,)
-        place = jnp.stack([parity, g, parity * p.groups + g, t]).astype(jnp.int32)
         partners = [(i, i ^ 1) for i in range(p.tiles)]
         same = [
             [e * p.tiles + 2 * q + h for e in range(p.groups) for q in range(p.tiles // 2)] for h in range(2)
@@ -409,21 +423,41 @@
         def in_hbm(array):
             return pltpu.with_memory_space_constraint(array, pltpu.HBM)
 
-        packs = call(
-            pack_body, p, [((2, 2, p.own, p.c // p.fold, LANES), F32)] * p.chips,
+        block = (2, 2, p.own, p.c // p.fold, LANES)
+        odd, *even = call(
+            pack_body, p, [((p.chips // 2, *block), F32)] + [(block, F32)] * (p.chips // 2),
             [
                 pltpu.VMEM((p.own, p.c, p.pairs * K), F32),
                 pltpu.VMEM((p.own, p.c, p.pairs * K), F32),
-                pltpu.VMEM(order.shape[1:], BF16),
+                pltpu.VMEM(target.shape, jnp.int32),
+                pltpu.VMEM((p.pairs * K, p.tiles * p.lanes), BF16),
                 pltpu.SemaphoreType.DMA((3,)),
             ],
-            specs=[SMEM] + [HBM] * 3,
-        )(place, in_hbm(modes_two.transpose(1, 2, 0)), in_hbm(modes_one.transpose(1, 2, 0)), in_hbm(order))
-        dealt = [packs[0]]
-        for chip in range(1, p.chips):
-            dealt.append(lax.ppermute(packs[chip], "tile", [(i, i ^ (2 * chip)) for i in range(p.tiles)]))
-        crossing = jnp.stack([part[1] for part in dealt])
-        crossed = lax.ppermute(crossing, "tile", partners)
+            specs=[HBM, HBM, HBM],
+        )(in_hbm(modes_two.transpose(1, 2, 0)), in_hbm(modes_one.transpose(1, 2, 0)), in_hbm(target))
+
+        def swap(blocks, bit):
+            return lax.ppermute(blocks, "tile", [(i, i ^ (2 * bit)) for i in range(p.tiles)])
+
+        got = swap(odd, 1)
+        first = {(0, 2 * n): part for n, part in enumerate(even)}
+        first |= {(1, 2 * n): got[n] for n in range(p.chips // 2)}
+
+        def deal(layer):
+            held = {key: part[:, layer] for key, part in first.items()}
+            bit = 2
+            while bit < p.chips:
+                leaving = sorted(key for key in held if key[1] & bit)
+                parts = jnp.stack([held.pop(key) for key in leaving])
+                got = swap(parts, bit)
+                held |= {(key[0] ^ bit, key[1] ^ bit): got[n] for n, key in enumerate(leaving)}
+                bit *= 2
+            dealt = [held[chip, 0] for chip in range(p.chips)]
+            crossing = jnp.stack([part[1] for part in dealt])
+            return (*dealt, lax.ppermute(crossing, "tile", partners))
+
+        weights_two = deal(0)
+        weights_one = deal(1)
 
         def exchange(parts):
             return lax.all_to_all(parts, BOTH, 0, 0, tiled=True, axis_index_groups=same)
@@ -431,12 +465,11 @@
         def partner(parts):
             return lax.ppermute(parts, "tile", partners)
 
-        def dual(got, layer):
-            body = functools.partial(dual_body, p, layer)
+        def dual(got, weights):
             return call(
-                lambda _, *refs: body(*refs), p, [(packed, F32)], [pltpu.VMEM((p.c, LANES), F32)],
-                specs=[SMEM] + [VMEM] * (p.chips + 2),
-            )(place, got, *dealt, crossed)[0]
+                dual_body, p, [(packed, F32)], [pltpu.VMEM((p.c, LANES), F32)],
+                count=p.chips + 2,
+            )(got, *weights)[0]
 
         def pointwise(w, *factors):
             return call(
@@ -445,9 +478,7 @@
             )(*factors, w, spread)[0]
 
         def grad(got, more, saved):
-            out = call(
-                grad_body, p, [((p.own, p.c, p.pairs * K), F32)], specs=[SMEM, VMEM, VMEM, VMEM]
-            )(place, got, more, saved[0].T)[0]
+            out = call(grad_body, p, [((p.own, p.c, p.pairs * K), F32)], count=3)(got, more, saved[0].T)[0]
             return out.transpose(2, 0, 1)
 
         part_two, table, turned = call(
@@ -456,11 +487,11 @@
                 g_scr, s_scr, pltpu.VMEM(field, BF16), pltpu.VMEM((2 * p.rows, xy), BF16),
                 pltpu.VMEM((xy, p.rows), BF16), pltpu.SemaphoreType.DMA((groups + 2,)),
             ],
-            specs=[SMEM, VMEM, HBM] + [VMEM] * 6, out_specs=[VMEM, HBM, HBM], grid=steps,
-        )(place, cotangent.reshape(field), in_hbm(deriv_two.reshape(field)), tz, lines, rows_x, rows_y, ex, ey)
+            specs=[VMEM, HBM] + [VMEM] * 6, out_specs=[VMEM, HBM, HBM], grid=steps,
+        )(cotangent.reshape(field), in_hbm(deriv_two.reshape(field)), tz, lines, rows_x, rows_y, ex, ey)
         got_two = lax.all_to_all(part_two, BOTH, 0, 0, tiled=True)
         point_out = pointwise(point_two, cotangent.reshape(field), deriv_two.reshape(field))
-        share_two = dual(got_two, 0)
+        share_two = dual(got_two, weights_two)
         all_two = exchange(share_two)
         more_two = partner(all_two)
         gated_one, part_one = call(
@@ -469,20 +500,20 @@
                 pltpu.VMEM(turned.shape, BF16), pltpu.VMEM(table.shape, BF16),
                 pltpu.SemaphoreType.DMA(steps), pltpu.SemaphoreType.DMA((3,)),
             ],
-            specs=[SMEM] + [VMEM] * 5 + [HBM] * 3, out_specs=[HBM, VMEM], grid=steps,
-        )(place, all_two, more_two, point_out, deriv_one.reshape(field), lines, in_hbm(tz), in_hbm(turned), in_hbm(table))
+            specs=[VMEM] * 5 + [HBM] * 3, out_specs=[HBM, VMEM], grid=steps,
+        )(all_two, more_two, point_out, deriv_one.reshape(field), lines, in_hbm(tz), in_hbm(turned), in_hbm(table))
         got_one = lax.all_to_all(part_one, BOTH, 0, 0, tiled=True)
         grad_two = grad(all_two, more_two, saved_two)
         point_out = pointwise(point_one, gated_one)
-        share_one = dual(got_one, 1)
+        share_one = dual(got_one, weights_one)
         all_one = exchange(share_one)
         more_one = partner(all_one)
         result, grad_one = call(
             synth_body, p, [(field, BF16), ((p.own, p.c, p.pairs * K), F32)], [s_scr, modes_scr],
-            specs=[SMEM] + [VMEM] * 7,
+            specs=[VMEM] * 7,
             out_specs=[blocked, pl.BlockSpec((p.own, p.c, p.pairs * K), lambda n: (0, 0, 0))],
             grid=steps,
-        )(place, all_one, more_one, point_out, tz, lines, turned, saved_one[0].T)
+        )(all_one, more_one, point_out, tz, lines, turned, saved_one[0].T)
         grad_one = grad_one.transpose(2, 0, 1)
         return (result.reshape(shape), grad_one, grad_two)
 

time: 80.1 us -> 77.7 us (0.970)
  blocking collectives: 24.5 us -> 13.7 us
  waiting for transfers between devices: 14.7 us -> 23.5 us
  Pallas kernels: 20.9 us -> 17.6 us
  starting transfers between devices: 14.7 us -> 17.3 us
    all_to_all x1 -> x0, blocking collectives: 12.7 us -> none  [local(): got_one = lax.all_to_all(part_one, BOTH, 0, 0, tiled=True)]
    all_to_all x0 -> x1, waiting for transfers between devices: none -> 9.11 us  [local(): got_one = lax.all_to_all(part_one, BOTH, 0, 0, tiled=True)]
    all_to_all x1, waiting for transfers between devices: 8.83 us -> 2.6 us  [local(): got_two = lax.all_to_all(part_two, BOTH, 0, 0, tiled=True)]
    ppermute x4 -> x5, waiting for transfers between devices: 1.29 us -> 6.95 us  [the longest x3 5.86 us: swap(): lax.ppermute(blocks, 'tile', [(i, i ^ 2 * bit) for i in range(p.tiles)])]
    all_to_all x0 -> x1, starting transfers between devices: none -> 2.73 us  [local(): got_one = lax.all_to_all(part_one, BOTH, 0, 0, tiled=True)]
    pallas_call x4, Pallas kernels: 6.74 us -> 4.4 us  [the longest x1 1.94 us: local(): call(pack_body, p, [((p.chips // 2, *block), F32)] + [(block, F32)] * (p....]
    all_to_all x1, blocking collectives: 11.8 us -> 13.7 us  [exchange(): return lax.all_to_all(parts, BOTH, 0, 0, tiled=True, axis_index_groups=same)]
    all_to_all x1, starting transfers between devices: 6.32 us -> 4.93 us  [local(): got_two = lax.all_to_all(part_two, BOTH, 0, 0, tiled=True)]
  transfers between devices with their start and end apart: 8 -> 10, of which waited for: 4 -> 6; matrix products, arithmetic and copies ran while one was open for 0% -> 0% of each run, Pallas kernels for 10% -> 15%
where the time goes in v2:
time: 77.7 us; the launch traced here: 77.2 us
  waiting for transfers between devices  23.5 us (30%)
  Pallas kernels  17.6 us (23%)
  starting transfers between devices  17.3 us (22%)
  blocking collectives  13.7 us (18%)
  local copies, waits for them, and re-layouts  3.92 us (5%)
  between operations  0.99 us (1%)
    all_to_all x1, blocking collectives, exchange(): return lax.all_to_all(parts, BOTH, 0, 0, tiled=True, axis_index_groups=same)  13.7 us
    all_to_all x1, waiting for transfers between devices, local(): got_one = lax.all_to_all(part_one, BOTH, 0, 0, tiled=True)  9.11 us
    ppermute x3, waiting for transfers between devices, swap(): lax.ppermute(blocks, 'tile', [(i, i ^ 2 * bit) for i in range(p.tiles)])  5.86 us
    ppermute x3, starting transfers between devices, swap(): lax.ppermute(blocks, 'tile', [(i, i ^ 2 * bit) for i in range(p.tiles)])  5.76 us
    all_to_all x1, starting transfers between devices, local(): got_two = lax.all_to_all(part_two, BOTH, 0, 0, tiled=True)  4.93 us
    pallas_call x1, Pallas kernels, local(): call(synth_analyse_body, p, [(field, BF16), (slots, F32)], [g_scr, s_scr,...  4.55 us
    all_to_all x1, waiting for transfers between devices, exchange(): return lax.all_to_all(parts, BOTH, 0, 0, tiled=True, axis_index_groups=same)  4.38 us
    unnamed x38, local copies, waits for them, and re-layouts  3.81 us
  transfers between devices with their start and end apart: 10, of which 6 were waited for; matrix products, arithmetic and copies ran while one was open for 0% of the time, Pallas kernels for 15%

profile of v2, /device:TPU:0, one launch (start us, length us, event | category | flops | bytes accessed | tf_op | source)
XLA Modules:
  0.0 77.2 jit_solution(5754060756942879279)
XLA Ops:
  0.6 0.0 copy-start.7
  0.7 0.0 copy-start.8
  0.7 0.0 copy-start.11
  0.7 0.0 copy-start.12
  0.7 0.0 copy-start.13
  0.7 0.0 copy-start.14
  0.7 1.9 %shard_map.185 = (f32[2,2,2,4,16,128]{5,4,3,2,1,0:T(8,128)S(1)}, f32[2,2,4,16,128]{4,3,2,1,0:T(8,128)S(1)}, f32[2,2,4,16,128]{4,3,2,1,0:T(8,128)S(1)}) custom-call(f32[4,32,432]{2,1,0:T(8,128)} %bitcast.67, f32[4,32,432]{2,1,0:T(8,128)} %bitcast.68, s32[4,1,512]{2,1,0:T(1,128)} %constant.23.clone.target_hbm), custom_call_target="tpu_custom_call" | custom-call | flops 2147483648 | bytes 2147483 | tf_op jit(solution)/shard_map/pallas_call | solution.py:427
  2.7 3.0 %collective-permute-start = (f32[2,2,2,4,16,128]{5,4,3,2,1,0:T(8,128)S(1)}, f32[2,2,2,4,16,128]{5,4,3,2,1,0:T(8,128)S(1)}, u32[]{:S(2)}, u32[]{:S(2)}) collective-permute-start(f32[2,2,2,4,16,128]{5,4,3,2,1,0:T(8,128)S(1)} %get-tuple-element.15), channel_id=1, source_target_pairs={{0,2},{1,3},{2,0},{3,1},{4,6},{5,7},{6,4},{7,5},{8,10},{9,11},{10,... | collective-permute-start | bytes 786440 | tf_op jit(solution)/shard_map/ppermute | solution.py:440
  5.7 0.0 copy-done
  5.7 0.0 copy-done.12
  5.7 0.0 copy-done.13
  5.7 0.0 copy-done.14
  5.7 3.5 %shard_map.184 = (f32[32,16,128]{2,1,0:T(8,128)}, bf16[320,192]{1,0:T(8,128)(2,1)}, bf16[192,160]{1,0:T(8,128)(2,1)}) custom-call(bf16[32,192,128]{2,1,0:T(8,128)(2,1)S(1)} %bitcast.59, bf16[32,192,128]{2,1,0:T(8,128)(2,1)} %bitcast.61, bf16[128,1024]{1,0:T(8,128)(2,1)S(1)} %copy-done.8, bf16[384,512]{1,0:T(8,128)(2,1)S(1)} %copy-done.7, ...), custom_call_target="tpu_custom_call" | custom-call | flops 2147483648 | bytes 2147483 | tf_op jit(solution)/shard_map/pallas_call | solution.py:484
  9.3 4.9 %all-to-all-start = ((f32[32,16,128]{2,1,0:T(8,128)}), f32[32,16,128]{2,1,0:T(8,128)S(1)}, u32[]{:S(2)}, u32[]{:S(2)}) async-start(f32[32,16,128]{2,1,0:T(8,128)} %get-tuple-element.13), calls=%async_computation | async-start | bytes 524288 | tf_op jit(solution)/shard_map/all_to_all | solution.py:492
  14.2 0.0 collective-permute-done
  14.3 1.8 %collective-permute-start.1 = (f32[2,2,4,16,128]{4,3,2,1,0:T(8,128)S(1)}, f32[2,2,4,16,128]{4,3,2,1,0:T(8,128)S(1)}, u32[]{:S(2)}, u32[]{:S(2)}) collective-permute-start(f32[2,2,4,16,128]{4,3,2,1,0:T(8,128)S(1)} %pad_maximum_fusion), channel_id=1, source_target_pairs={{0,4},{1,5},{2,6},{3,7},{4,0},{5,1},{6,2},{7,3},{8,12},{9,13},{10,... | collective-permute-start | bytes 393224 | tf_op jit(solution)/shard_map/ppermute | solution.py:440
  16.2 5.9 %collective-permute-done.1 = f32[2,2,4,16,128]{4,3,2,1,0:T(8,128)S(1)} collective-permute-done((f32[2,2,4,16,128]{4,3,2,1,0:T(8,128)S(1)}, f32[2,2,4,16,128]{4,3,2,1,0:T(8,128)S(1)}, u32[]{:S(2)}, u32[]{:S(2)}) %collective-permute-start.1) | collective-permute-done | bytes 131104 | tf_op jit(solution)/shard_map/ppermute | solution.py:440
  22.1 0.1 collective-permute-start.2
  22.2 2.6 %all-to-all-done.got_ref = f32[32,16,128]{2,1,0:T(8,128)S(1)} async-done(((f32[32,16,128]{2,1,0:T(8,128)}), f32[32,16,128]{2,1,0:T(8,128)S(1)}, u32[]{:S(2)}, u32[]{:S(2)}) %all-to-all-start) | async-done | bytes 262176 | tf_op jit(solution)/shard_map/all_to_all | solution.py:492
  24.8 0.0 collective-permute-done.2.refs_4_
  24.8 0.4 shard_map.186
  25.2 13.7 %all_to_all.20.got_ref = f32[16,24,128]{2,1,0:T(8,128)S(1)} all-to-all(f32[16,24,128]{2,1,0:T(8,128)S(1)} %shard_map.186), channel_id=1, replica_groups={{0,2,4,6,8,10,12,14,16,18,20,22,24,26,28,30},{1,3,5,7,9,11,13,15,17,19,..., dimensions={0} | all-to-all | bytes 393216 | tf_op jit(solution)/shard_map/all_to_all | solution.py:463
  39.0 0.0 collective-permute-start.3
  39.0 0.0 copy-done.1
  39.0 0.0 copy-done.5
  39.0 0.0 copy-done.10
  39.0 1.2 %shard_map.187.point_ref = f32[32,192,128]{2,1,0:T(8,128)S(1)} custom-call(bf16[32,192,128]{2,1,0:T(8,128)(2,1)S(1)} %bitcast.60, bf16[32,192,128]{2,1,0:T(8,128)(2,1)S(1)} %bitcast.62, bf16[32,32]{1,0:T(8,128)(2,1)S(1)} %copy-done.5, bf16[512,32]{1,0:T(8,128)(2,1)S(1)} %copy-done.10), custom_call_target="tpu_custom_call" | custom-call | flops 2147483648 | bytes 2147483 | tf_op jit(solution)/shard_map/pallas_call | solution.py:475
  40.3 0.9 %collective-permute-start.4 = (f32[2,2,4,16,128]{4,3,2,1,0:T(8,128)S(1)}, f32[2,2,4,16,128]{4,3,2,1,0:T(8,128)S(1)}, u32[]{:S(2)}, u32[]{:S(2)}) collective-permute-start(f32[2,2,4,16,128]{4,3,2,1,0:T(8,128)S(1)} %pad_maximum_fusion.2), channel_id=1, source_target_pairs={{0,4},{1,5},{2,6},{3,7},{4,0},{5,1},{6,2},{7,3},{8,12},{9,13},{10,... | collective-permute-start | bytes 393224 | tf_op jit(solution)/shard_map/ppermute | solution.py:440
  41.2 0.0 collective-permute-done.3.more_ref
  41.2 4.6 %shard_map.188 = (bf16[32,192,128]{2,1,0:T(8,128)(2,1)}, f32[32,16,128]{2,1,0:T(8,128)}) custom-call(f32[16,24,128]{2,1,0:T(8,128)S(1)} %all_to_all.20.got_ref, f32[16,24,128]{2,1,0:T(8,128)S(1)} %collective-permute-done.3.more_ref, f32[32,192,128]{2,1,0:T(8,128)S(1)} %shard_map.187.point_ref, bf16[32,192,128]{2,1,0:T(8,128)(2,1)S(1)} %bitcast.63, ...), custom_call_target="tpu_custom_call" | custom-call | flops 2147483648 | bytes 2147483 | tf_op jit(solution)/shard_map/pallas_call | solution.py:497
  45.7 2.7 %all-to-all-start.2 = ((f32[32,16,128]{2,1,0:T(8,128)}), f32[32,16,128]{2,1,0:T(8,128)S(1)}, u32[]{:S(2)}, u32[]{:S(2)}) async-start(f32[32,16,128]{2,1,0:T(8,128)} %get-tuple-element.19), calls=%async_computation.2 | async-start | bytes 524288 | tf_op jit(solution)/shard_map/all_to_all | solution.py:505
  48.5 0.0 collective-permute-done.4
  48.5 0.3 collective-permute-start.5
  48.8 1.1 %collective-permute-done.5.refs_4_ = f32[4,4,16,128]{3,2,1,0:T(8,128)S(1)} collective-permute-done((f32[4,4,16,128]{3,2,1,0:T(8,128)S(1)}, f32[4,4,16,128]{3,2,1,0:T(8,128)S(1)}, u32[]{:S(2)}, u32[]{:S(2)}) %collective-permute-start.5) | collective-permute-done | bytes 131104 | tf_op jit(solution)/shard_map/ppermute | solution.py:457
  49.9 9.1 %all-to-all-done.2.got_ref = f32[32,16,128]{2,1,0:T(8,128)S(1)} async-done(((f32[32,16,128]{2,1,0:T(8,128)}), f32[32,16,128]{2,1,0:T(8,128)S(1)}, u32[]{:S(2)}, u32[]{:S(2)}) %all-to-all-start.2) | async-done | bytes 262176 | tf_op jit(solution)/shard_map/all_to_all | solution.py:505
  59.0 1.1 %shard_map.189 = f32[16,24,128]{2,1,0:T(8,128)} custom-call(f32[32,16,128]{2,1,0:T(8,128)S(1)} %all-to-all-done.2.got_ref, f32[2,4,16,128]{3,2,1,0:T(8,128)S(1)} %get-tuple-element.39.refs_0_, f32[2,4,16,128]{3,2,1,0:T(8,128)S(1)} %get-tuple-element.37.refs_1_, f32[2,4,16,128]{3,2,1,0:T(8,128)S(1)} %get-tuple-element.32.refs_2_, ...), custom_call_target="tpu_custom_call" | custom-call | flops 2147483648 | bytes 2147483 | tf_op jit(solution)/shard_map/pallas_call | solution.py:469
  60.2 3.5 %all-to-all-start.3 = ((f32[16,24,128]{2,1,0:T(8,128)}), f32[16,24,128]{2,1,0:T(8,128)S(1)}, u32[]{:S(2)}, u32[]{:S(2)}) async-start(f32[16,24,128]{2,1,0:T(8,128)} %shard_map.189), calls=%async_computation.3 | async-start | bytes 393216 | tf_op jit(solution)/shard_map/all_to_all | solution.py:463
  63.7 0.0 copy-start.15
  63.7 1.4 %copy-done.15 = bf16[32,192,128]{2,1,0:T(8,128)(2,1)S(1)} copy-done((bf16[32,192,128]{2,1,0:T(8,128)(2,1)S(1)}, bf16[32,192,128]{2,1,0:T(8,128)(2,1)}, u32[]{:S(2)}) %copy-start.15) | copy-done | bytes 1572888
  65.1 1.2 %shard_map.190.point_ref = f32[32,192,128]{2,1,0:T(8,128)S(1)} custom-call(bf16[32,192,128]{2,1,0:T(8,128)(2,1)S(1)} %copy-done.15, bf16[32,32]{1,0:T(8,128)(2,1)S(1)} %copy-done.6, bf16[512,32]{1,0:T(8,128)(2,1)S(1)} %copy-done.10), custom_call_target="tpu_custom_call" | custom-call | flops 2147483648 | bytes 2147483 | tf_op jit(solution)/shard_map/pallas_call | solution.py:475
  66.4 1.6 %copy-done.16 = f32[32,192,128]{2,1,0:T(8,128)} copy-done((f32[32,192,128]{2,1,0:T(8,128)}, f32[32,192,128]{2,1,0:T(8,128)S(1)}, u32[]{:S(2)}) %copy-start.16) | copy-done | bytes 3145752
  68.0 4.4 %all-to-all-done.3.got_ref = f32[16,24,128]{2,1,0:T(8,128)S(1)} async-done(((f32[16,24,128]{2,1,0:T(8,128)}), f32[16,24,128]{2,1,0:T(8,128)S(1)}, u32[]{:S(2)}, u32[]{:S(2)}) %all-to-all-start.3) | async-done | bytes 196640 | tf_op jit(solution)/shard_map/all_to_all | solution.py:463
  72.4 0.0 collective-permute-start.6
  72.4 0.0 copy-start.9
  72.4 0.9 %shard_map.192 = f32[4,32,432]{2,1,0:T(8,128)} custom-call(f32[16,24,128]{2,1,0:T(8,128)S(1)} %all_to_all.20.got_ref, f32[16,24,128]{2,1,0:T(8,128)S(1)} %collective-permute-done.3.more_ref, f32[32,432]{1,0:T(8,128)S(1)} %bitcast.64), custom_call_target="tpu_custom_call" | custom-call | flops 2147483648 | bytes 2147483 | tf_op jit(solution)/shard_map/pallas_call | solution.py:481
  73.3 0.5 collective-permute-done.6.more_ref
  73.8 0.7 copy-done.17
  74.5 2.7 %shard_map.191 = (bf16[32,192,128]{2,1,0:T(8,128)(2,1)}, f32[4,32,432]{2,1,0:T(8,128)}) custom-call(f32[16,24,128]{2,1,0:T(8,128)S(1)} %all-to-all-done.3.got_ref, f32[16,24,128]{2,1,0:T(8,128)S(1)} %collective-permute-done.6.more_ref, f32[32,192,128]{2,1,0:T(8,128)S(1)} %copy-done.17, bf16[128,1024]{1,0:T(8,128)(2,1)S(1)} %copy-done.9, ...), custom_call_target="tpu_custom_call" | custom-call | flops 2147483648 | bytes 2147483 | tf_op jit(solution)/shard_map/pallas_call | solution.py:511
  (35 shorter events, 0.2 us)
Async XLA Ops:
  0.6 5.1 %copy-start = (bf16[1,32,12,16,128]{4,3,2,1,0:T(8,128)(2,1)S(1)}, bf16[1,32,12,16,128]{4,3,2,1,0:T(8,128)(2,1)}, u32[]{:S(2)}) copy-start(bf16[1,32,12,16,128]{4,3,2,1,0:T(8,128)(2,1)} %param.17) | copy-start | bytes 4718596
  0.6 5.1 %copy-start.7 = (bf16[384,512]{1,0:T(8,128)(2,1)S(1)}, bf16[384,512]{1,0:T(8,128)(2,1)}, u32[]{:S(2)}) copy-start(bf16[384,512]{1,0:T(8,128)(2,1)} %constant.27.order_ref) | copy-start | bytes 1179652
  0.7 5.0 %copy-start.8 = (bf16[128,1024]{1,0:T(8,128)(2,1)S(1)}, bf16[128,1024]{1,0:T(8,128)(2,1)}, u32[]{:S(2)}) copy-start(bf16[128,1024]{1,0:T(8,128)(2,1)} %constant.26.tz_ref.tz_hbm) | copy-start | bytes 786436
  0.7 5.0 %copy-start.11 = (bf16[8,32,160]{2,1,0:T(8,128)(2,1)S(1)}, bf16[8,32,160]{2,1,0:T(8,128)(2,1)}, u32[]{:S(2)}) copy-start(bf16[8,32,160]{2,1,0:T(8,128)(2,1)} %constant.17.clone.ry_ref) | copy-start | bytes 245764
  0.7 5.0 %copy-start.12 = (bf16[8,24,160]{2,1,0:T(8,128)(2,1)S(1)}, bf16[8,24,160]{2,1,0:T(8,128)(2,1)}, u32[]{:S(2)}) copy-start(bf16[8,24,160]{2,1,0:T(8,128)(2,1)} %constant.16.clone.rx_ref) | copy-start | bytes 184324
  0.7 5.0 %copy-start.13 = (bf16[32,192]{1,0:T(8,128)(2,1)S(1)}, bf16[32,192]{1,0:T(8,128)(2,1)}, u32[]{:S(2)}) copy-start(bf16[32,192]{1,0:T(8,128)(2,1)} %constant.29.ey_ref) | copy-start | bytes 36868
  0.7 5.0 %copy-start.14 = (bf16[24,192]{1,0:T(8,128)(2,1)S(1)}, bf16[24,192]{1,0:T(8,128)(2,1)}, u32[]{:S(2)}) copy-start(bf16[24,192]{1,0:T(8,128)(2,1)} %constant.28.ex_ref) | copy-start | bytes 27652
  2.7 11.6 %collective-permute-start = (f32[2,2,2,4,16,128]{5,4,3,2,1,0:T(8,128)S(1)}, f32[2,2,2,4,16,128]{5,4,3,2,1,0:T(8,128)S(1)}, u32[]{:S(2)}, u32[]{:S(2)}) collective-permute-start(f32[2,2,2,4,16,128]{5,4,3,2,1,0:T(8,128)S(1)} %get-tuple-element.15), channel_id=1, source_target_pairs={{0,2},{1,3},{2,0},{3,1},{4,6},{5,7},{6,4},{7,5},{8,10},{9,11},{10,... | collective-permute-start | bytes 786440 | tf_op jit(solution)/shard_map/ppermute | solution.py:440
  9.3 15.5 %all-to-all-start = ((f32[32,16,128]{2,1,0:T(8,128)}), f32[32,16,128]{2,1,0:T(8,128)S(1)}, u32[]{:S(2)}, u32[]{:S(2)}) async-start(f32[32,16,128]{2,1,0:T(8,128)} %get-tuple-element.13), calls=%async_computation | async-start | bytes 524288 | tf_op jit(solution)/shard_map/all_to_all | solution.py:492
  14.3 7.7 %collective-permute-start.1 = (f32[2,2,4,16,128]{4,3,2,1,0:T(8,128)S(1)}, f32[2,2,4,16,128]{4,3,2,1,0:T(8,128)S(1)}, u32[]{:S(2)}, u32[]{:S(2)}) collective-permute-start(f32[2,2,4,16,128]{4,3,2,1,0:T(8,128)S(1)} %pad_maximum_fusion), channel_id=1, source_target_pairs={{0,4},{1,5},{2,6},{3,7},{4,0},{5,1},{6,2},{7,3},{8,12},{9,13},{10,... | collective-permute-start | bytes 393224 | tf_op jit(solution)/shard_map/ppermute | solution.py:440
  22.1 2.7 %collective-permute-start.2 = (f32[4,4,16,128]{3,2,1,0:T(8,128)S(1)}, f32[4,4,16,128]{3,2,1,0:T(8,128)S(1)}, u32[]{:S(2)}, u32[]{:S(2)}) collective-permute-start(f32[4,4,16,128]{3,2,1,0:T(8,128)S(1)} %pad_maximum_fusion.1), channel_id=1, source_target_pairs={{0,1},{1,0},{2,3},{3,2},{4,5},{5,4},{6,7},{7,6},{8,9},{9,8},{10,11... | collective-permute-start | bytes 393224 | tf_op jit(solution)/shard_map/ppermute | solution.py:457
  24.8 14.2 %copy-start.1 = (bf16[1,32,12,16,128]{4,3,2,1,0:T(8,128)(2,1)S(1)}, bf16[1,32,12,16,128]{4,3,2,1,0:T(8,128)(2,1)}, u32[]{:S(2)}) copy-start(bf16[1,32,12,16,128]{4,3,2,1,0:T(8,128)(2,1)} %param.18) | copy-start | bytes 4718596
  24.8 14.2 %copy-start.5 = (bf16[32,32]{1,0:T(8,128)(2,1)S(1)}, bf16[32,32]{1,0:T(8,128)(2,1)}, u32[]{:S(2)}) copy-start(bf16[32,32]{1,0:T(8,128)(2,1)} %refs_2_.1) | copy-start | bytes 6148
  24.8 14.2 %copy-start.10 = (bf16[512,32]{1,0:T(8,128)(2,1)S(1)}, bf16[512,32]{1,0:T(8,128)(2,1)}, u32[]{:S(2)}) copy-start(bf16[512,32]{1,0:T(8,128)(2,1)} %constant.30.refs_3_.refs_2_) | copy-start | bytes 98308
  39.0 2.2 %copy-start.2 = (bf16[1,32,12,16,128]{4,3,2,1,0:T(8,128)(2,1)S(1)}, bf16[1,32,12,16,128]{4,3,2,1,0:T(8,128)(2,1)}, u32[]{:S(2)}) copy-start(bf16[1,32,12,16,128]{4,3,2,1,0:T(8,128)(2,1)} %param.19) | copy-start | bytes 4718596
  39.0 2.2 %collective-permute-start.3 = (f32[16,24,128]{2,1,0:T(8,128)S(1)}, f32[16,24,128]{2,1,0:T(8,128)S(1)}, u32[]{:S(2)}, u32[]{:S(2)}) collective-permute-start(f32[16,24,128]{2,1,0:T(8,128)S(1)} %all_to_all.20.got_ref), channel_id=1, source_target_pairs={{0,1},{1,0},{2,3},{3,2},{4,5},{5,4},{6,7},{7,6},{8,9},{9,8},{10,11... | collective-permute-start | bytes 589832 | tf_op jit(solution)/shard_map/ppermute | solution.py:466
  40.3 8.2 %collective-permute-start.4 = (f32[2,2,4,16,128]{4,3,2,1,0:T(8,128)S(1)}, f32[2,2,4,16,128]{4,3,2,1,0:T(8,128)S(1)}, u32[]{:S(2)}, u32[]{:S(2)}) collective-permute-start(f32[2,2,4,16,128]{4,3,2,1,0:T(8,128)S(1)} %pad_maximum_fusion.2), channel_id=1, source_target_pairs={{0,4},{1,5},{2,6},{3,7},{4,0},{5,1},{6,2},{7,3},{8,12},{9,13},{10,... | collective-permute-start | bytes 393224 | tf_op jit(solution)/shard_map/ppermute | solution.py:440
  45.7 13.3 %all-to-all-start.2 = ((f32[32,16,128]{2,1,0:T(8,128)}), f32[32,16,128]{2,1,0:T(8,128)S(1)}, u32[]{:S(2)}, u32[]{:S(2)}) async-start(f32[32,16,128]{2,1,0:T(8,128)} %get-tuple-element.19), calls=%async_computation.2 | async-start | bytes 524288 | tf_op jit(solution)/shard_map/all_to_all | solution.py:505
  48.5 1.4 %collective-permute-start.5 = (f32[4,4,16,128]{3,2,1,0:T(8,128)S(1)}, f32[4,4,16,128]{3,2,1,0:T(8,128)S(1)}, u32[]{:S(2)}, u32[]{:S(2)}) collective-permute-start(f32[4,4,16,128]{3,2,1,0:T(8,128)S(1)} %pad_maximum_fusion.3), channel_id=1, source_target_pairs={{0,1},{1,0},{2,3},{3,2},{4,5},{5,4},{6,7},{7,6},{8,9},{9,8},{10,11... | collective-permute-start | bytes 393224 | tf_op jit(solution)/shard_map/ppermute | solution.py:457
  59.0 4.7 %copy-start.6 = (bf16[32,32]{1,0:T(8,128)(2,1)S(1)}, bf16[32,32]{1,0:T(8,128)(2,1)}, u32[]{:S(2)}) copy-start(bf16[32,32]{1,0:T(8,128)(2,1)} %refs_1_.1) | copy-start | bytes 6148
  60.2 12.2 %all-to-all-start.3 = ((f32[16,24,128]{2,1,0:T(8,128)}), f32[16,24,128]{2,1,0:T(8,128)S(1)}, u32[]{:S(2)}, u32[]{:S(2)}) async-start(f32[16,24,128]{2,1,0:T(8,128)} %shard_map.189), calls=%async_computation.3 | async-start | bytes 393216 | tf_op jit(solution)/shard_map/all_to_all | solution.py:463
  63.7 1.4 %copy-start.15 = (bf16[32,192,128]{2,1,0:T(8,128)(2,1)S(1)}, bf16[32,192,128]{2,1,0:T(8,128)(2,1)}, u32[]{:S(2)}) copy-start(bf16[32,192,128]{2,1,0:T(8,128)(2,1)} %get-tuple-element.20.refs_0_) | copy-start | bytes 4718596
  65.1 7.3 %copy-start.3 = (f32[1,432,32]{1,2,0:T(8,128)S(1)}, f32[1,432,32]{1,2,0:T(8,128)}, u32[]{:S(2)}) copy-start(f32[1,432,32]{1,2,0:T(8,128)} %param.24) | copy-start | bytes 165892
  66.3 1.7 %copy-start.16 = (f32[32,192,128]{2,1,0:T(8,128)}, f32[32,192,128]{2,1,0:T(8,128)S(1)}, u32[]{:S(2)}) copy-start(f32[32,192,128]{2,1,0:T(8,128)S(1)} %shard_map.190.point_ref) | copy-start | bytes 9437188
  72.4 1.4 %collective-permute-start.6 = (f32[16,24,128]{2,1,0:T(8,128)S(1)}, f32[16,24,128]{2,1,0:T(8,128)S(1)}, u32[]{:S(2)}, u32[]{:S(2)}) collective-permute-start(f32[16,24,128]{2,1,0:T(8,128)S(1)} %all-to-all-done.3.got_ref), channel_id=1, source_target_pairs={{0,1},{1,0},{2,3},{3,2},{4,5},{5,4},{6,7},{7,6},{8,9},{9,8},{10,11... | collective-permute-start | bytes 589832 | tf_op jit(solution)/shard_map/ppermute | solution.py:466
  72.4 1.4 %copy-start.4 = (f32[1,432,32]{1,2,0:T(8,128)S(1)}, f32[1,432,32]{1,2,0:T(8,128)}, u32[]{:S(2)}) copy-start(f32[1,432,32]{1,2,0:T(8,128)} %param.25) | copy-start | bytes 165892
  72.4 1.4 %copy-start.9 = (bf16[128,1024]{1,0:T(8,128)(2,1)S(1)}, bf16[128,1024]{1,0:T(8,128)(2,1)}, u32[]{:S(2)}) copy-start(bf16[128,1024]{1,0:T(8,128)(2,1)} %constant.26.tz_ref.tz_hbm) | copy-start | bytes 786436
  72.4 2.1 %copy-start.17 = (f32[32,192,128]{2,1,0:T(8,128)S(1)}, f32[32,192,128]{2,1,0:T(8,128)}, u32[]{:S(2)}) copy-start(f32[32,192,128]{2,1,0:T(8,128)} %copy-done.16) | copy-start | bytes 9437188
  72.4 2.1 %copy-start.18 = (bf16[192,160]{1,0:T(8,128)(2,1)S(1)}, bf16[192,160]{1,0:T(8,128)(2,1)}, u32[]{:S(2)}) copy-start(bf16[192,160]{1,0:T(8,128)(2,1)} %get-tuple-element.17.turned_hbm.turned_ref) | copy-start | bytes 184324

commit v3 on v2

--- a/solution.py
+++ b/solution.py
@@ -155,7 +155,7 @@
             copy.wait()
 
 
-def gather_modes(plan, got_ref, more_ref, order_ref, turned_ref, d_ref, modes_ref, ready=None):
+def gather_modes(plan, got_ref, more_ref, order_ref, turned_ref, d_ref, modes_ref):
     p = plan
     for d in range(p.devices):
         from_ref, n = (got_ref, d) if d < p.half else (more_ref, d - p.half)
@@ -163,8 +163,6 @@
             d_ref[d * p.run : (d + 1) * p.run, j * LANES : (j + 1) * LANES] = from_ref[
                 n, j * p.run : (j + 1) * p.run, :
             ]
-    if ready is not None:
-        ready()
     lines = jnp.dot(turned_ref[...], d_ref[...].astype(BF16), preferred_element_type=F32).astype(BF16)
     lines = jnp.dot(lines, order_ref[...], preferred_element_type=F32).astype(BF16)
     for n in range(p.c // p.step):
@@ -172,13 +170,11 @@
 
 
 def synth_analyse_body(
-    plan, got_ref, more_ref, point_ref, der_ref, order_ref, tz_hbm, turned_hbm, table_hbm,
-    gated_ref, slots_ref, g_ref, s_ref, d_ref, modes_ref, field_ref, tz_ref, turned_ref, table_ref, sems, table_sems,
+    plan, got_ref, more_ref, point_ref, der_ref, order_ref, tz_ref, turned_ref, table_ref,
+    gated_ref, slots_ref, g_ref, s_ref, d_ref, modes_ref, field_ref, sems,
 ):
     p = plan
     step = pl.program_id(0)
-    pairs = ((turned_hbm, turned_ref), (tz_hbm, tz_ref), (table_hbm, table_ref))
-    tables = [pltpu.make_async_copy(*pair, table_sems.at[n]) for n, pair in enumerate(pairs)]
 
     def store(n):
         part = pl.ds(n * p.step, p.step)
@@ -186,17 +182,13 @@
 
     @pl.when(step == 0)
     def _():
-        for copy in tables:
-            copy.start()
-        gather_modes(p, got_ref, more_ref, order_ref, turned_ref, d_ref, modes_ref, tables[0].wait)
-        for copy in tables[1:]:
-            copy.wait()
+        gather_modes(p, got_ref, more_ref, order_ref, turned_ref, d_ref, modes_ref)
 
     first = step * p.step
     synth = jnp.dot(modes_ref[step], tz_ref[...], preferred_element_type=F32)
     parts = []
     for u in range(p.step):
-        middle = (point_ref[first + u] + synth[:, u * p.z : (u + 1) * p.z]).astype(BF16)
+        middle = (point_ref[first + u].astype(F32) + synth[:, u * p.z : (u + 1) * p.z]).astype(BF16)
         gated = product(middle, der_ref[first + u])
         field_ref[first + u] = gated
         parts.append(gated)
@@ -227,7 +219,7 @@
     first = step * p.step
     synth = jnp.dot(modes_ref[step], tz_ref[...], preferred_element_type=F32)
     for u in range(p.step):
-        out_ref[u] = (point_ref[first + u] + synth[:, u * p.z : (u + 1) * p.z]).astype(BF16)
+        out_ref[u] = (point_ref[first + u].astype(F32) + synth[:, u * p.z : (u + 1) * p.z]).astype(BF16)
 
 
 def pointwise_body(plan, *refs):
@@ -248,8 +240,8 @@
             pair.append((product(*cells) if len(cells) == 2 else cells[0]).reshape(n, p.z))
         out = jnp.dot(big_ref[...], jnp.concatenate(pair, axis=1), preferred_element_type=F32)
         for h in range(2):
-            out_ref[:, (x + h) * p.y : (x + h + 1) * p.y, :] = out[:, h * p.z : (h + 1) * p.z].reshape(
-                p.c, p.y, p.z
+            out_ref[:, (x + h) * p.y : (x + h + 1) * p.y, :] = (
+                out[:, h * p.z : (h + 1) * p.z].astype(BF16).reshape(p.c, p.y, p.z)
             )
 
 
@@ -473,7 +465,7 @@
 
         def pointwise(w, *factors):
             return call(
-                pointwise_body, p, [(field, F32)], [pltpu.VMEM((p.c * p.y, p.c * p.y), BF16)],
+                pointwise_body, p, [(field, BF16)], [pltpu.VMEM((p.c * p.y, p.c * p.y), BF16)],
                 count=2 + len(factors),
             )(*factors, w, spread)[0]
 
@@ -496,12 +488,10 @@
         more_two = partner(all_two)
         gated_one, part_one = call(
             synth_analyse_body, p, [(field, BF16), (slots, F32)], [
-                g_scr, s_scr, s_scr, modes_scr, pltpu.VMEM(field, BF16), pltpu.VMEM(tz.shape, BF16),
-                pltpu.VMEM(turned.shape, BF16), pltpu.VMEM(table.shape, BF16),
-                pltpu.SemaphoreType.DMA(steps), pltpu.SemaphoreType.DMA((3,)),
+                g_scr, s_scr, s_scr, modes_scr, pltpu.VMEM(field, BF16), pltpu.SemaphoreType.DMA(steps),
             ],
-            specs=[VMEM] * 5 + [HBM] * 3, out_specs=[HBM, VMEM], grid=steps,
-        )(all_two, more_two, point_out, deriv_one.reshape(field), lines, in_hbm(tz), in_hbm(turned), in_hbm(table))
+            count=8, out_specs=[HBM, VMEM], grid=steps,
+        )(all_two, more_two, point_out, deriv_one.reshape(field), lines, tz, turned, table)
         got_one = lax.all_to_all(part_one, BOTH, 0, 0, tiled=True)
         grad_two = grad(all_two, more_two, saved_two)
         point_out = pointwise(point_one, gated_one)

time: 77.7 us -> 76.3 us (0.982)
  Pallas kernels: 17.6 us -> 16.8 us
    unnamed x38 -> x40, local copies, waits for them, and re-layouts: 3.81 us -> 2.73 us
    pallas_call x1, Pallas kernels: 4.55 us -> 3.74 us  [local(): call(synth_analyse_body, p, [(field, BF16), (slots, F32)], [g_scr, s_scr,...]
  transfers between devices with their start and end apart: 10 -> 10, of which waited for: 6 -> 6; matrix products, arithmetic and copies ran while one was open for 0% -> 1% of each run, Pallas kernels for 15% -> 14%
where the time goes in v3:
time: 76.3 us; the launch traced here: 75.8 us
  waiting for transfers between devices  23.5 us (31%)
  starting transfers between devices  17.3 us (23%)
  Pallas kernels  16.8 us (22%)
  blocking collectives  13.7 us (18%)
  local copies, waits for them, and re-layouts  3.45 us (5%)
  between operations  1.01 us (1%)
    all_to_all x1, blocking collectives, exchange(): return lax.all_to_all(parts, BOTH, 0, 0, tiled=True, axis_index_groups=same)  13.7 us
    all_to_all x1, waiting for transfers between devices, local(): got_one = lax.all_to_all(part_one, BOTH, 0, 0, tiled=True)  9.1 us
    ppermute x3, starting transfers between devices, swap(): lax.ppermute(blocks, 'tile', [(i, i ^ 2 * bit) for i in range(p.tiles)])  5.76 us
    ppermute x3, waiting for transfers between devices, swap(): lax.ppermute(blocks, 'tile', [(i, i ^ 2 * bit) for i in range(p.tiles)])  5.26 us
    all_to_all x1, starting transfers between devices, local(): got_two = lax.all_to_all(part_two, BOTH, 0, 0, tiled=True)  4.93 us
    all_to_all x1, waiting for transfers between devices, exchange(): return lax.all_to_all(parts, BOTH, 0, 0, tiled=True, axis_index_groups=same)  4.89 us
    pallas_call x1, Pallas kernels, local(): call(synth_analyse_body, p, [(field, BF16), (slots, F32)], [g_scr, s_scr,...  3.74 us
    all_to_all x1, starting transfers between devices, exchange(): return lax.all_to_all(parts, BOTH, 0, 0, tiled=True, axis_index_groups=same)  3.52 us
  transfers between devices with their start and end apart: 10, of which 6 were waited for; matrix products, arithmetic and copies ran while one was open for 1% of the time, Pallas kernels for 14%

profile of v3, /device:TPU:0, one launch (start us, length us, event | category | flops | bytes accessed | tf_op | source)
XLA Modules:
  0.0 75.8 jit_solution(6097688336083776408)
XLA Ops:
  0.6 0.0 copy-start.7
  0.7 0.0 copy-start.8
  0.7 0.0 copy-start.10
  0.7 0.0 copy-start.11
  0.7 0.0 copy-start.12
  0.7 0.0 copy-start.13
  0.7 1.9 %shard_map.185 = (f32[2,2,2,4,16,128]{5,4,3,2,1,0:T(8,128)S(1)}, f32[2,2,4,16,128]{4,3,2,1,0:T(8,128)S(1)}, f32[2,2,4,16,128]{4,3,2,1,0:T(8,128)S(1)}) custom-call(f32[4,32,432]{2,1,0:T(8,128)} %bitcast.67, f32[4,32,432]{2,1,0:T(8,128)} %bitcast.68, s32[4,1,512]{2,1,0:T(1,128)} %constant.23.clone.target_hbm), custom_call_target="tpu_custom_call" | custom-call | flops 2147483648 | bytes 2147483 | tf_op jit(solution)/shard_map/pallas_call | solution.py:419
  2.7 3.0 %collective-permute-start = (f32[2,2,2,4,16,128]{5,4,3,2,1,0:T(8,128)S(1)}, f32[2,2,2,4,16,128]{5,4,3,2,1,0:T(8,128)S(1)}, u32[]{:S(2)}, u32[]{:S(2)}) collective-permute-start(f32[2,2,2,4,16,128]{5,4,3,2,1,0:T(8,128)S(1)} %get-tuple-element.15), channel_id=1, source_target_pairs={{0,2},{1,3},{2,0},{3,1},{4,6},{5,7},{6,4},{7,5},{8,10},{9,11},{10,... | collective-permute-start | bytes 786440 | tf_op jit(solution)/shard_map/ppermute | solution.py:432
  5.7 0.0 copy-done
  5.7 0.0 copy-done.11
  5.7 0.0 copy-done.12
  5.7 0.0 copy-done.13
  5.7 3.5 %shard_map.184 = (f32[32,16,128]{2,1,0:T(8,128)}, bf16[320,192]{1,0:T(8,128)(2,1)}, bf16[192,160]{1,0:T(8,128)(2,1)}) custom-call(bf16[32,192,128]{2,1,0:T(8,128)(2,1)S(1)} %bitcast.59, bf16[32,192,128]{2,1,0:T(8,128)(2,1)} %bitcast.61, bf16[128,1024]{1,0:T(8,128)(2,1)S(1)} %copy-done.8, bf16[384,512]{1,0:T(8,128)(2,1)S(1)} %copy-done.7, ...), custom_call_target="tpu_custom_call" | custom-call | flops 2147483648 | bytes 2147483 | tf_op jit(solution)/shard_map/pallas_call | solution.py:476
  9.3 4.9 %all-to-all-start = ((f32[32,16,128]{2,1,0:T(8,128)}), f32[32,16,128]{2,1,0:T(8,128)S(1)}, u32[]{:S(2)}, u32[]{:S(2)}) async-start(f32[32,16,128]{2,1,0:T(8,128)} %get-tuple-element.13), calls=%async_computation | async-start | bytes 524288 | tf_op jit(solution)/shard_map/all_to_all | solution.py:484
  14.2 0.0 collective-permute-done
  14.3 1.8 %collective-permute-start.1 = (f32[2,2,4,16,128]{4,3,2,1,0:T(8,128)S(1)}, f32[2,2,4,16,128]{4,3,2,1,0:T(8,128)S(1)}, u32[]{:S(2)}, u32[]{:S(2)}) collective-permute-start(f32[2,2,4,16,128]{4,3,2,1,0:T(8,128)S(1)} %pad_maximum_fusion), channel_id=1, source_target_pairs={{0,4},{1,5},{2,6},{3,7},{4,0},{5,1},{6,2},{7,3},{8,12},{9,13},{10,... | collective-permute-start | bytes 393224 | tf_op jit(solution)/shard_map/ppermute | solution.py:432
  16.2 0.6 slice_bitcast_fusion.15
  16.8 5.3 %collective-permute-done.1 = f32[2,2,4,16,128]{4,3,2,1,0:T(8,128)S(1)} collective-permute-done((f32[2,2,4,16,128]{4,3,2,1,0:T(8,128)S(1)}, f32[2,2,4,16,128]{4,3,2,1,0:T(8,128)S(1)}, u32[]{:S(2)}, u32[]{:S(2)}) %collective-permute-start.1) | collective-permute-done | bytes 131104 | tf_op jit(solution)/shard_map/ppermute | solution.py:432
  22.1 0.1 collective-permute-start.2
  22.2 2.6 %all-to-all-done.got_ref = f32[32,16,128]{2,1,0:T(8,128)S(1)} async-done(((f32[32,16,128]{2,1,0:T(8,128)}), f32[32,16,128]{2,1,0:T(8,128)S(1)}, u32[]{:S(2)}, u32[]{:S(2)}) %all-to-all-start) | async-done | bytes 262176 | tf_op jit(solution)/shard_map/all_to_all | solution.py:484
  24.8 0.0 collective-permute-done.2.refs_4_
  24.8 0.4 shard_map.186
  25.2 13.7 %all_to_all.20.got_ref = f32[16,24,128]{2,1,0:T(8,128)S(1)} all-to-all(f32[16,24,128]{2,1,0:T(8,128)S(1)} %shard_map.186), channel_id=1, replica_groups={{0,2,4,6,8,10,12,14,16,18,20,22,24,26,28,30},{1,3,5,7,9,11,13,15,17,19,..., dimensions={0} | all-to-all | bytes 393216 | tf_op jit(solution)/shard_map/all_to_all | solution.py:455
  39.0 0.0 collective-permute-start.3
  39.0 1.2 %shard_map.187.point_ref = bf16[32,192,128]{2,1,0:T(8,128)(2,1)S(1)} custom-call(bf16[32,192,128]{2,1,0:T(8,128)(2,1)S(1)} %bitcast.60, bf16[32,192,128]{2,1,0:T(8,128)(2,1)S(1)} %bitcast.62, bf16[32,32]{1,0:T(8,128)(2,1)S(1)} %copy-done.5, bf16[512,32]{1,0:T(8,128)(2,1)S(1)} %copy-done.9), custom_call_target="tpu_custom_call" | custom-call | flops 2147483648 | bytes 2147483 | tf_op jit(solution)/shard_map/pallas_call | solution.py:467
  40.3 0.9 %collective-permute-start.4 = (f32[2,2,4,16,128]{4,3,2,1,0:T(8,128)S(1)}, f32[2,2,4,16,128]{4,3,2,1,0:T(8,128)S(1)}, u32[]{:S(2)}, u32[]{:S(2)}) collective-permute-start(f32[2,2,4,16,128]{4,3,2,1,0:T(8,128)S(1)} %pad_maximum_fusion.2), channel_id=1, source_target_pairs={{0,4},{1,5},{2,6},{3,7},{4,0},{5,1},{6,2},{7,3},{8,12},{9,13},{10,... | collective-permute-start | bytes 393224 | tf_op jit(solution)/shard_map/ppermute | solution.py:432
  41.2 0.0 collective-permute-done.3.more_ref
  41.2 0.0 copy-done.2
  41.2 3.7 %shard_map.188 = (bf16[32,192,128]{2,1,0:T(8,128)(2,1)}, f32[32,16,128]{2,1,0:T(8,128)}) custom-call(f32[16,24,128]{2,1,0:T(8,128)S(1)} %all_to_all.20.got_ref, f32[16,24,128]{2,1,0:T(8,128)S(1)} %collective-permute-done.3.more_ref, bf16[32,192,128]{2,1,0:T(8,128)(2,1)S(1)} %shard_map.187.point_ref, bf16[32,192,128]{2,1,0:T(8,128)(2,1)S(1)} %bitcast.63, ...), custom_call_target="tpu_custom_call" | custom-call | flops 2147483648 | bytes 2147483 | tf_op jit(solution)/shard_map/pallas_call | solution.py:489
  45.0 2.7 %all-to-all-start.2 = ((f32[32,16,128]{2,1,0:T(8,128)}), f32[32,16,128]{2,1,0:T(8,128)S(1)}, u32[]{:S(2)}, u32[]{:S(2)}) async-start(f32[32,16,128]{2,1,0:T(8,128)} %get-tuple-element.19), calls=%async_computation.2 | async-start | bytes 524288 | tf_op jit(solution)/shard_map/all_to_all | solution.py:495
  47.7 0.0 collective-permute-done.4
  47.8 0.3 collective-permute-start.5
  48.1 1.1 %collective-permute-done.5.refs_4_ = f32[4,4,16,128]{3,2,1,0:T(8,128)S(1)} collective-permute-done((f32[4,4,16,128]{3,2,1,0:T(8,128)S(1)}, f32[4,4,16,128]{3,2,1,0:T(8,128)S(1)}, u32[]{:S(2)}, u32[]{:S(2)}) %collective-permute-start.5) | collective-permute-done | bytes 131104 | tf_op jit(solution)/shard_map/ppermute | solution.py:449
  49.2 9.1 %all-to-all-done.2.got_ref = f32[32,16,128]{2,1,0:T(8,128)S(1)} async-done(((f32[32,16,128]{2,1,0:T(8,128)}), f32[32,16,128]{2,1,0:T(8,128)S(1)}, u32[]{:S(2)}, u32[]{:S(2)}) %all-to-all-start.2) | async-done | bytes 262176 | tf_op jit(solution)/shard_map/all_to_all | solution.py:495
  58.3 1.1 %shard_map.189 = f32[16,24,128]{2,1,0:T(8,128)} custom-call(f32[32,16,128]{2,1,0:T(8,128)S(1)} %all-to-all-done.2.got_ref, f32[2,4,16,128]{3,2,1,0:T(8,128)S(1)} %get-tuple-element.39.refs_0_, f32[2,4,16,128]{3,2,1,0:T(8,128)S(1)} %get-tuple-element.37.refs_1_, f32[2,4,16,128]{3,2,1,0:T(8,128)S(1)} %get-tuple-element.32.refs_2_, ...), custom_call_target="tpu_custom_call" | custom-call | flops 2147483648 | bytes 2147483 | tf_op jit(solution)/shard_map/pallas_call | solution.py:461
  59.4 3.5 %all-to-all-start.3 = ((f32[16,24,128]{2,1,0:T(8,128)}), f32[16,24,128]{2,1,0:T(8,128)S(1)}, u32[]{:S(2)}, u32[]{:S(2)}) async-start(f32[16,24,128]{2,1,0:T(8,128)} %shard_map.189), calls=%async_computation.3 | async-start | bytes 393216 | tf_op jit(solution)/shard_map/all_to_all | solution.py:455
  62.9 0.0 copy-start.14
  63.0 1.4 %copy-done.14 = bf16[32,192,128]{2,1,0:T(8,128)(2,1)S(1)} copy-done((bf16[32,192,128]{2,1,0:T(8,128)(2,1)S(1)}, bf16[32,192,128]{2,1,0:T(8,128)(2,1)}, u32[]{:S(2)}) %copy-start.14) | copy-done | bytes 1572888
  64.4 1.2 %shard_map.190.point_ref = bf16[32,192,128]{2,1,0:T(8,128)(2,1)S(1)} custom-call(bf16[32,192,128]{2,1,0:T(8,128)(2,1)S(1)} %copy-done.14, bf16[32,32]{1,0:T(8,128)(2,1)S(1)} %copy-done.6, bf16[512,32]{1,0:T(8,128)(2,1)S(1)} %copy-done.9), custom_call_target="tpu_custom_call" | custom-call | flops 2147483648 | bytes 2147483 | tf_op jit(solution)/shard_map/pallas_call | solution.py:467
  65.6 0.0 copy-start.15
  65.6 1.1 %copy-done.15 = bf16[32,192,128]{2,1,0:T(8,128)(2,1)} copy-done((bf16[32,192,128]{2,1,0:T(8,128)(2,1)}, bf16[32,192,128]{2,1,0:T(8,128)(2,1)S(1)}, u32[]{:S(2)}) %copy-start.15) | copy-done | bytes 1572888
  66.7 4.9 %all-to-all-done.3.got_ref = f32[16,24,128]{2,1,0:T(8,128)S(1)} async-done(((f32[16,24,128]{2,1,0:T(8,128)}), f32[16,24,128]{2,1,0:T(8,128)S(1)}, u32[]{:S(2)}, u32[]{:S(2)}) %all-to-all-start.3) | async-done | bytes 196640 | tf_op jit(solution)/shard_map/all_to_all | solution.py:455
  71.6 0.0 collective-permute-start.6
  71.6 0.0 copy-start.16
  71.6 0.9 %shard_map.192 = f32[4,32,432]{2,1,0:T(8,128)} custom-call(f32[16,24,128]{2,1,0:T(8,128)S(1)} %all_to_all.20.got_ref, f32[16,24,128]{2,1,0:T(8,128)S(1)} %collective-permute-done.3.more_ref, f32[32,432]{1,0:T(8,128)S(1)} %bitcast.64), custom_call_target="tpu_custom_call" | custom-call | flops 2147483648 | bytes 2147483 | tf_op jit(solution)/shard_map/pallas_call | solution.py:473
  72.5 0.5 collective-permute-done.6.more_ref
  73.1 0.1 copy-done.16
  73.2 2.7 %shard_map.191 = (bf16[32,192,128]{2,1,0:T(8,128)(2,1)}, f32[4,32,432]{2,1,0:T(8,128)}) custom-call(f32[16,24,128]{2,1,0:T(8,128)S(1)} %all-to-all-done.3.got_ref, f32[16,24,128]{2,1,0:T(8,128)S(1)} %collective-permute-done.6.more_ref, bf16[32,192,128]{2,1,0:T(8,128)(2,1)S(1)} %copy-done.16, bf16[128,1024]{1,0:T(8,128)(2,1)S(1)} %copy-done.8, ...), custom_call_target="tpu_custom_call" | custom-call | flops 2147483648 | bytes 2147483 | tf_op jit(solution)/shard_map/pallas_call | solution.py:501
  (37 shorter events, 0.2 us)
Async XLA Ops:
  0.6 5.1 %copy-start = (bf16[1,32,12,16,128]{4,3,2,1,0:T(8,128)(2,1)S(1)}, bf16[1,32,12,16,128]{4,3,2,1,0:T(8,128)(2,1)}, u32[]{:S(2)}) copy-start(bf16[1,32,12,16,128]{4,3,2,1,0:T(8,128)(2,1)} %param.17) | copy-start | bytes 4718596
  0.6 5.1 %copy-start.7 = (bf16[384,512]{1,0:T(8,128)(2,1)S(1)}, bf16[384,512]{1,0:T(8,128)(2,1)}, u32[]{:S(2)}) copy-start(bf16[384,512]{1,0:T(8,128)(2,1)} %constant.27.order_ref) | copy-start | bytes 1179652
  0.7 5.0 %copy-start.8 = (bf16[128,1024]{1,0:T(8,128)(2,1)S(1)}, bf16[128,1024]{1,0:T(8,128)(2,1)}, u32[]{:S(2)}) copy-start(bf16[128,1024]{1,0:T(8,128)(2,1)} %constant.26.tz_ref) | copy-start | bytes 786436
  0.7 5.0 %copy-start.10 = (bf16[8,32,160]{2,1,0:T(8,128)(2,1)S(1)}, bf16[8,32,160]{2,1,0:T(8,128)(2,1)}, u32[]{:S(2)}) copy-start(bf16[8,32,160]{2,1,0:T(8,128)(2,1)} %constant.17.clone.ry_ref) | copy-start | bytes 245764
  0.7 5.0 %copy-start.11 = (bf16[8,24,160]{2,1,0:T(8,128)(2,1)S(1)}, bf16[8,24,160]{2,1,0:T(8,128)(2,1)}, u32[]{:S(2)}) copy-start(bf16[8,24,160]{2,1,0:T(8,128)(2,1)} %constant.16.clone.rx_ref) | copy-start | bytes 184324
  0.7 5.0 %copy-start.12 = (bf16[32,192]{1,0:T(8,128)(2,1)S(1)}, bf16[32,192]{1,0:T(8,128)(2,1)}, u32[]{:S(2)}) copy-start(bf16[32,192]{1,0:T(8,128)(2,1)} %constant.29.ey_ref) | copy-start | bytes 36868
  0.7 5.0 %copy-start.13 = (bf16[24,192]{1,0:T(8,128)(2,1)S(1)}, bf16[24,192]{1,0:T(8,128)(2,1)}, u32[]{:S(2)}) copy-start(bf16[24,192]{1,0:T(8,128)(2,1)} %constant.28.ex_ref) | copy-start | bytes 27652
  2.7 11.6 %collective-permute-start = (f32[2,2,2,4,16,128]{5,4,3,2,1,0:T(8,128)S(1)}, f32[2,2,2,4,16,128]{5,4,3,2,1,0:T(8,128)S(1)}, u32[]{:S(2)}, u32[]{:S(2)}) collective-permute-start(f32[2,2,2,4,16,128]{5,4,3,2,1,0:T(8,128)S(1)} %get-tuple-element.15), channel_id=1, source_target_pairs={{0,2},{1,3},{2,0},{3,1},{4,6},{5,7},{6,4},{7,5},{8,10},{9,11},{10,... | collective-permute-start | bytes 786440 | tf_op jit(solution)/shard_map/ppermute | solution.py:432
  9.3 15.5 %all-to-all-start = ((f32[32,16,128]{2,1,0:T(8,128)}), f32[32,16,128]{2,1,0:T(8,128)S(1)}, u32[]{:S(2)}, u32[]{:S(2)}) async-start(f32[32,16,128]{2,1,0:T(8,128)} %get-tuple-element.13), calls=%async_computation | async-start | bytes 524288 | tf_op jit(solution)/shard_map/all_to_all | solution.py:484
  14.3 7.7 %collective-permute-start.1 = (f32[2,2,4,16,128]{4,3,2,1,0:T(8,128)S(1)}, f32[2,2,4,16,128]{4,3,2,1,0:T(8,128)S(1)}, u32[]{:S(2)}, u32[]{:S(2)}) collective-permute-start(f32[2,2,4,16,128]{4,3,2,1,0:T(8,128)S(1)} %pad_maximum_fusion), channel_id=1, source_target_pairs={{0,4},{1,5},{2,6},{3,7},{4,0},{5,1},{6,2},{7,3},{8,12},{9,13},{10,... | collective-permute-start | bytes 393224 | tf_op jit(solution)/shard_map/ppermute | solution.py:432
  22.1 2.7 %collective-permute-start.2 = (f32[4,4,16,128]{3,2,1,0:T(8,128)S(1)}, f32[4,4,16,128]{3,2,1,0:T(8,128)S(1)}, u32[]{:S(2)}, u32[]{:S(2)}) collective-permute-start(f32[4,4,16,128]{3,2,1,0:T(8,128)S(1)} %pad_maximum_fusion.1), channel_id=1, source_target_pairs={{0,1},{1,0},{2,3},{3,2},{4,5},{5,4},{6,7},{7,6},{8,9},{9,8},{10,11... | collective-permute-start | bytes 393224 | tf_op jit(solution)/shard_map/ppermute | solution.py:449
  24.8 14.2 %copy-start.1 = (bf16[1,32,12,16,128]{4,3,2,1,0:T(8,128)(2,1)S(1)}, bf16[1,32,12,16,128]{4,3,2,1,0:T(8,128)(2,1)}, u32[]{:S(2)}) copy-start(bf16[1,32,12,16,128]{4,3,2,1,0:T(8,128)(2,1)} %param.18) | copy-start | bytes 4718596
  24.8 14.2 %copy-start.5 = (bf16[32,32]{1,0:T(8,128)(2,1)S(1)}, bf16[32,32]{1,0:T(8,128)(2,1)}, u32[]{:S(2)}) copy-start(bf16[32,32]{1,0:T(8,128)(2,1)} %refs_2_.1) | copy-start | bytes 6148
  24.8 14.2 %copy-start.9 = (bf16[512,32]{1,0:T(8,128)(2,1)S(1)}, bf16[512,32]{1,0:T(8,128)(2,1)}, u32[]{:S(2)}) copy-start(bf16[512,32]{1,0:T(8,128)(2,1)} %constant.30.refs_3_.refs_2_) | copy-start | bytes 98308
  39.0 2.2 %copy-start.2 = (bf16[1,32,12,16,128]{4,3,2,1,0:T(8,128)(2,1)S(1)}, bf16[1,32,12,16,128]{4,3,2,1,0:T(8,128)(2,1)}, u32[]{:S(2)}) copy-start(bf16[1,32,12,16,128]{4,3,2,1,0:T(8,128)(2,1)} %param.19) | copy-start | bytes 4718596
  39.0 2.2 %copy-start.17 = (bf16[320,192]{1,0:T(8,128)(2,1)S(1)}, bf16[320,192]{1,0:T(8,128)(2,1)}, u32[]{:S(2)}) copy-start(bf16[320,192]{1,0:T(8,128)(2,1)} %get-tuple-element.18.table_ref) | copy-start | bytes 368644
  39.0 2.2 %copy-start.18 = (bf16[192,160]{1,0:T(8,128)(2,1)S(1)}, bf16[192,160]{1,0:T(8,128)(2,1)}, u32[]{:S(2)}) copy-start(bf16[192,160]{1,0:T(8,128)(2,1)} %get-tuple-element.17.turned_ref) | copy-start | bytes 184324
  39.0 2.2 %collective-permute-start.3 = (f32[16,24,128]{2,1,0:T(8,128)S(1)}, f32[16,24,128]{2,1,0:T(8,128)S(1)}, u32[]{:S(2)}, u32[]{:S(2)}) collective-permute-start(f32[16,24,128]{2,1,0:T(8,128)S(1)} %all_to_all.20.got_ref), channel_id=1, source_target_pairs={{0,1},{1,0},{2,3},{3,2},{4,5},{5,4},{6,7},{7,6},{8,9},{9,8},{10,11... | collective-permute-start | bytes 589832 | tf_op jit(solution)/shard_map/ppermute | solution.py:458
  40.3 7.4 %collective-permute-start.4 = (f32[2,2,4,16,128]{4,3,2,1,0:T(8,128)S(1)}, f32[2,2,4,16,128]{4,3,2,1,0:T(8,128)S(1)}, u32[]{:S(2)}, u32[]{:S(2)}) collective-permute-start(f32[2,2,4,16,128]{4,3,2,1,0:T(8,128)S(1)} %pad_maximum_fusion.2), channel_id=1, source_target_pairs={{0,4},{1,5},{2,6},{3,7},{4,0},{5,1},{6,2},{7,3},{8,12},{9,13},{10,... | collective-permute-start | bytes 393224 | tf_op jit(solution)/shard_map/ppermute | solution.py:432
  41.2 6.5 %copy-start.19 = (f32[1,4,16,128]{3,2,1,0:T(8,128)S(1)}, f32[1,4,16,128]{3,2,1,0:T(8,128)}, u32[]{:S(2)}) copy-start(f32[1,4,16,128]{3,2,1,0:T(8,128)} %get-tuple-element.27) | copy-start | bytes 98308
  45.0 13.3 %all-to-all-start.2 = ((f32[32,16,128]{2,1,0:T(8,128)}), f32[32,16,128]{2,1,0:T(8,128)S(1)}, u32[]{:S(2)}, u32[]{:S(2)}) async-start(f32[32,16,128]{2,1,0:T(8,128)} %get-tuple-element.19), calls=%async_computation.2 | async-start | bytes 524288 | tf_op jit(solution)/shard_map/all_to_all | solution.py:495
  47.8 1.4 %collective-permute-start.5 = (f32[4,4,16,128]{3,2,1,0:T(8,128)S(1)}, f32[4,4,16,128]{3,2,1,0:T(8,128)S(1)}, u32[]{:S(2)}, u32[]{:S(2)}) collective-permute-start(f32[4,4,16,128]{3,2,1,0:T(8,128)S(1)} %pad_maximum_fusion.3), channel_id=1, source_target_pairs={{0,1},{1,0},{2,3},{3,2},{4,5},{5,4},{6,7},{7,6},{8,9},{9,8},{10,11... | collective-permute-start | bytes 393224 | tf_op jit(solution)/shard_map/ppermute | solution.py:449
  58.3 4.7 %copy-start.6 = (bf16[32,32]{1,0:T(8,128)(2,1)S(1)}, bf16[32,32]{1,0:T(8,128)(2,1)}, u32[]{:S(2)}) copy-start(bf16[32,32]{1,0:T(8,128)(2,1)} %refs_1_.1) | copy-start | bytes 6148
  59.4 12.2 %all-to-all-start.3 = ((f32[16,24,128]{2,1,0:T(8,128)}), f32[16,24,128]{2,1,0:T(8,128)S(1)}, u32[]{:S(2)}, u32[]{:S(2)}) async-start(f32[16,24,128]{2,1,0:T(8,128)} %shard_map.189), calls=%async_computation.3 | async-start | bytes 393216 | tf_op jit(solution)/shard_map/all_to_all | solution.py:455
  62.9 1.4 %copy-start.14 = (bf16[32,192,128]{2,1,0:T(8,128)(2,1)S(1)}, bf16[32,192,128]{2,1,0:T(8,128)(2,1)}, u32[]{:S(2)}) copy-start(bf16[32,192,128]{2,1,0:T(8,128)(2,1)} %get-tuple-element.20.refs_0_) | copy-start | bytes 4718596
  64.4 7.3 %copy-start.3 = (f32[1,432,32]{1,2,0:T(8,128)S(1)}, f32[1,432,32]{1,2,0:T(8,128)}, u32[]{:S(2)}) copy-start(f32[1,432,32]{1,2,0:T(8,128)} %param.24) | copy-start | bytes 165892
  65.6 1.1 %copy-start.15 = (bf16[32,192,128]{2,1,0:T(8,128)(2,1)}, bf16[32,192,128]{2,1,0:T(8,128)(2,1)S(1)}, u32[]{:S(2)}) copy-start(bf16[32,192,128]{2,1,0:T(8,128)(2,1)S(1)} %shard_map.190.point_ref) | copy-start | bytes 4718596
  71.6 1.4 %collective-permute-start.6 = (f32[16,24,128]{2,1,0:T(8,128)S(1)}, f32[16,24,128]{2,1,0:T(8,128)S(1)}, u32[]{:S(2)}, u32[]{:S(2)}) collective-permute-start(f32[16,24,128]{2,1,0:T(8,128)S(1)} %all-to-all-done.3.got_ref), channel_id=1, source_target_pairs={{0,1},{1,0},{2,3},{3,2},{4,5},{5,4},{6,7},{7,6},{8,9},{9,8},{10,11... | collective-permute-start | bytes 589832 | tf_op jit(solution)/shard_map/ppermute | solution.py:458
  71.6 1.4 %copy-start.4 = (f32[1,432,32]{1,2,0:T(8,128)S(1)}, f32[1,432,32]{1,2,0:T(8,128)}, u32[]{:S(2)}) copy-start(f32[1,432,32]{1,2,0:T(8,128)} %param.25) | copy-start | bytes 165892
  71.6 1.5 %copy-start.16 = (bf16[32,192,128]{2,1,0:T(8,128)(2,1)S(1)}, bf16[32,192,128]{2,1,0:T(8,128)(2,1)}, u32[]{:S(2)}) copy-start(bf16[32,192,128]{2,1,0:T(8,128)(2,1)} %copy-done.15) | copy-start | bytes 4718596

commit v4 on v3

--- a/solution.py
+++ b/solution.py
@@ -205,21 +205,27 @@
 
 
 def synth_body(
-    plan, got_ref, more_ref, point_ref, tz_ref, order_ref, turned_ref, saved_ref, out_ref, grad_ref,
-    d_ref, modes_ref,
+    plan, got_ref, more_ref, point_ref, tz_ref, order_ref, turned_ref, saved_ref, out_ref, grad_hbm,
+    d_ref, modes_ref, grad_ref, sem,
 ):
     p = plan
     step = pl.program_id(0)
+    leaving = pltpu.make_async_copy(grad_ref, grad_hbm, sem.at[0])
 
     @pl.when(step == 0)
     def _():
+        grad_body(p, got_ref, more_ref, saved_ref, grad_ref)
+        leaving.start()
         gather_modes(p, got_ref, more_ref, order_ref, turned_ref, d_ref, modes_ref)
-        grad_body(p, got_ref, more_ref, saved_ref, grad_ref)
 
     first = step * p.step
     synth = jnp.dot(modes_ref[step], tz_ref[...], preferred_element_type=F32)
     for u in range(p.step):
         out_ref[u] = (point_ref[first + u].astype(F32) + synth[:, u * p.z : (u + 1) * p.z]).astype(BF16)
+
+    @pl.when(step == pl.num_programs(0) - 1)
+    def _():
+        leaving.wait()
 
 
 def pointwise_body(plan, *refs):
@@ -499,9 +505,10 @@
         all_one = exchange(share_one)
         more_one = partner(all_one)
         result, grad_one = call(
-            synth_body, p, [(field, BF16), ((p.own, p.c, p.pairs * K), F32)], [s_scr, modes_scr],
+            synth_body, p, [(field, BF16), ((p.own, p.c, p.pairs * K), F32)],
+            [s_scr, modes_scr, pltpu.VMEM((p.own, p.c, p.pairs * K), F32), pltpu.SemaphoreType.DMA((1,))],
             specs=[VMEM] * 7,
-            out_specs=[blocked, pl.BlockSpec((p.own, p.c, p.pairs * K), lambda n: (0, 0, 0))],
+            out_specs=[blocked, HBM],
             grid=steps,
         )(all_one, more_one, point_out, tz, lines, turned, saved_one[0].T)
         grad_one = grad_one.transpose(2, 0, 1)

time: 76.3 us -> 76.3 us (level)
  no operation moved by 1% of the time
where the time goes in v4:
time: 76.3 us; the launch traced here: 75.8 us
  waiting for transfers between devices  23.5 us (31%)
  starting transfers between devices  17.3 us (23%)
  Pallas kernels  16.8 us (22%)
  blocking collectives  13.7 us (18%)
  local copies, waits for them, and re-layouts  3.45 us (5%)
  between operations  1.01 us (1%)
    all_to_all x1, blocking collectives, exchange(): return lax.all_to_all(parts, BOTH, 0, 0, tiled=True, axis_index_groups=same)  13.7 us
    all_to_all x1, waiting for transfers between devices, local(): got_one = lax.all_to_all(part_one, BOTH, 0, 0, tiled=True)  9.1 us
    ppermute x3, starting transfers between devices, swap(): lax.ppermute(blocks, 'tile', [(i, i ^ 2 * bit) for i in range(p.tiles)])  5.76 us
    ppermute x3, waiting for transfers between devices, swap(): lax.ppermute(blocks, 'tile', [(i, i ^ 2 * bit) for i in range(p.tiles)])  5.26 us
    all_to_all x1, starting transfers between devices, local(): got_two = lax.all_to_all(part_two, BOTH, 0, 0, tiled=True)  4.93 us
    all_to_all x1, waiting for transfers between devices, exchange(): return lax.all_to_all(parts, BOTH, 0, 0, tiled=True, axis_index_groups=same)  4.89 us
    pallas_call x1, Pallas kernels, local(): call(synth_analyse_body, p, [(field, BF16), (slots, F32)], [g_scr, s_scr,...  3.74 us
    all_to_all x1, starting transfers between devices, exchange(): return lax.all_to_all(parts, BOTH, 0, 0, tiled=True, axis_index_groups=same)  3.52 us
  transfers between devices with their start and end apart: 10, of which 6 were waited for; matrix products, arithmetic and copies ran while one was open for 1% of the time, Pallas kernels for 14%

profile of v4, /device:TPU:0, one launch (start us, length us, event | category | flops | bytes accessed | tf_op | source)
XLA Modules:
  0.0 75.8 jit_solution(6351368191320997180)
XLA Ops:
  0.6 0.0 copy-start.7
  0.7 0.0 copy-start.8
  0.7 0.0 copy-start.10
  0.7 0.0 copy-start.11
  0.7 0.0 copy-start.12
  0.7 0.0 copy-start.13
  0.7 1.9 %shard_map.185 = (f32[2,2,2,4,16,128]{5,4,3,2,1,0:T(8,128)S(1)}, f32[2,2,4,16,128]{4,3,2,1,0:T(8,128)S(1)}, f32[2,2,4,16,128]{4,3,2,1,0:T(8,128)S(1)}) custom-call(f32[4,32,432]{2,1,0:T(8,128)} %bitcast.67, f32[4,32,432]{2,1,0:T(8,128)} %bitcast.68, s32[4,1,512]{2,1,0:T(1,128)} %constant.23.clone.target_hbm), custom_call_target="tpu_custom_call" | custom-call | flops 2147483648 | bytes 2147483 | tf_op jit(solution)/shard_map/pallas_call | solution.py:425
  2.7 3.0 %collective-permute-start = (f32[2,2,2,4,16,128]{5,4,3,2,1,0:T(8,128)S(1)}, f32[2,2,2,4,16,128]{5,4,3,2,1,0:T(8,128)S(1)}, u32[]{:S(2)}, u32[]{:S(2)}) collective-permute-start(f32[2,2,2,4,16,128]{5,4,3,2,1,0:T(8,128)S(1)} %get-tuple-element.15), channel_id=1, source_target_pairs={{0,2},{1,3},{2,0},{3,1},{4,6},{5,7},{6,4},{7,5},{8,10},{9,11},{10,... | collective-permute-start | bytes 786440 | tf_op jit(solution)/shard_map/ppermute | solution.py:438
  5.7 0.0 copy-done
  5.7 0.0 copy-done.11
  5.7 0.0 copy-done.12
  5.7 0.0 copy-done.13
  5.7 3.5 %shard_map.184 = (f32[32,16,128]{2,1,0:T(8,128)}, bf16[320,192]{1,0:T(8,128)(2,1)}, bf16[192,160]{1,0:T(8,128)(2,1)}) custom-call(bf16[32,192,128]{2,1,0:T(8,128)(2,1)S(1)} %bitcast.59, bf16[32,192,128]{2,1,0:T(8,128)(2,1)} %bitcast.61, bf16[128,1024]{1,0:T(8,128)(2,1)S(1)} %copy-done.8, bf16[384,512]{1,0:T(8,128)(2,1)S(1)} %copy-done.7, ...), custom_call_target="tpu_custom_call" | custom-call | flops 2147483648 | bytes 2147483 | tf_op jit(solution)/shard_map/pallas_call | solution.py:482
  9.3 4.9 %all-to-all-start = ((f32[32,16,128]{2,1,0:T(8,128)}), f32[32,16,128]{2,1,0:T(8,128)S(1)}, u32[]{:S(2)}, u32[]{:S(2)}) async-start(f32[32,16,128]{2,1,0:T(8,128)} %get-tuple-element.13), calls=%async_computation | async-start | bytes 524288 | tf_op jit(solution)/shard_map/all_to_all | solution.py:490
  14.2 0.0 collective-permute-done
  14.3 1.8 %collective-permute-start.1 = (f32[2,2,4,16,128]{4,3,2,1,0:T(8,128)S(1)}, f32[2,2,4,16,128]{4,3,2,1,0:T(8,128)S(1)}, u32[]{:S(2)}, u32[]{:S(2)}) collective-permute-start(f32[2,2,4,16,128]{4,3,2,1,0:T(8,128)S(1)} %pad_maximum_fusion), channel_id=1, source_target_pairs={{0,4},{1,5},{2,6},{3,7},{4,0},{5,1},{6,2},{7,3},{8,12},{9,13},{10,... | collective-permute-start | bytes 393224 | tf_op jit(solution)/shard_map/ppermute | solution.py:438
  16.2 0.6 slice_bitcast_fusion.15
  16.8 5.3 %collective-permute-done.1 = f32[2,2,4,16,128]{4,3,2,1,0:T(8,128)S(1)} collective-permute-done((f32[2,2,4,16,128]{4,3,2,1,0:T(8,128)S(1)}, f32[2,2,4,16,128]{4,3,2,1,0:T(8,128)S(1)}, u32[]{:S(2)}, u32[]{:S(2)}) %collective-permute-start.1) | collective-permute-done | bytes 131104 | tf_op jit(solution)/shard_map/ppermute | solution.py:438
  22.1 0.1 collective-permute-start.2
  22.2 2.6 %all-to-all-done.got_ref = f32[32,16,128]{2,1,0:T(8,128)S(1)} async-done(((f32[32,16,128]{2,1,0:T(8,128)}), f32[32,16,128]{2,1,0:T(8,128)S(1)}, u32[]{:S(2)}, u32[]{:S(2)}) %all-to-all-start) | async-done | bytes 262176 | tf_op jit(solution)/shard_map/all_to_all | solution.py:490
  24.8 0.0 collective-permute-done.2.refs_4_
  24.8 0.4 shard_map.186
  25.2 13.7 %all_to_all.20.got_ref = f32[16,24,128]{2,1,0:T(8,128)S(1)} all-to-all(f32[16,24,128]{2,1,0:T(8,128)S(1)} %shard_map.186), channel_id=1, replica_groups={{0,2,4,6,8,10,12,14,16,18,20,22,24,26,28,30},{1,3,5,7,9,11,13,15,17,19,..., dimensions={0} | all-to-all | bytes 393216 | tf_op jit(solution)/shard_map/all_to_all | solution.py:461
  39.0 0.0 collective-permute-start.3
  39.0 1.2 %shard_map.187.point_ref = bf16[32,192,128]{2,1,0:T(8,128)(2,1)S(1)} custom-call(bf16[32,192,128]{2,1,0:T(8,128)(2,1)S(1)} %bitcast.60, bf16[32,192,128]{2,1,0:T(8,128)(2,1)S(1)} %bitcast.62, bf16[32,32]{1,0:T(8,128)(2,1)S(1)} %copy-done.5, bf16[512,32]{1,0:T(8,128)(2,1)S(1)} %copy-done.9), custom_call_target="tpu_custom_call" | custom-call | flops 2147483648 | bytes 2147483 | tf_op jit(solution)/shard_map/pallas_call | solution.py:473
  40.3 0.9 %collective-permute-start.4 = (f32[2,2,4,16,128]{4,3,2,1,0:T(8,128)S(1)}, f32[2,2,4,16,128]{4,3,2,1,0:T(8,128)S(1)}, u32[]{:S(2)}, u32[]{:S(2)}) collective-permute-start(f32[2,2,4,16,128]{4,3,2,1,0:T(8,128)S(1)} %pad_maximum_fusion.2), channel_id=1, source_target_pairs={{0,4},{1,5},{2,6},{3,7},{4,0},{5,1},{6,2},{7,3},{8,12},{9,13},{10,... | collective-permute-start | bytes 393224 | tf_op jit(solution)/shard_map/ppermute | solution.py:438
  41.2 0.0 collective-permute-done.3.more_ref
  41.2 0.0 copy-done.2
  41.2 3.7 %shard_map.188 = (bf16[32,192,128]{2,1,0:T(8,128)(2,1)}, f32[32,16,128]{2,1,0:T(8,128)}) custom-call(f32[16,24,128]{2,1,0:T(8,128)S(1)} %all_to_all.20.got_ref, f32[16,24,128]{2,1,0:T(8,128)S(1)} %collective-permute-done.3.more_ref, bf16[32,192,128]{2,1,0:T(8,128)(2,1)S(1)} %shard_map.187.point_ref, bf16[32,192,128]{2,1,0:T(8,128)(2,1)S(1)} %bitcast.63, ...), custom_call_target="tpu_custom_call" | custom-call | flops 2147483648 | bytes 2147483 | tf_op jit(solution)/shard_map/pallas_call | solution.py:495
  45.0 2.7 %all-to-all-start.2 = ((f32[32,16,128]{2,1,0:T(8,128)}), f32[32,16,128]{2,1,0:T(8,128)S(1)}, u32[]{:S(2)}, u32[]{:S(2)}) async-start(f32[32,16,128]{2,1,0:T(8,128)} %get-tuple-element.19), calls=%async_computation.2 | async-start | bytes 524288 | tf_op jit(solution)/shard_map/all_to_all | solution.py:501
  47.7 0.0 collective-permute-done.4
  47.8 0.3 collective-permute-start.5
  48.1 1.1 %collective-permute-done.5.refs_4_ = f32[4,4,16,128]{3,2,1,0:T(8,128)S(1)} collective-permute-done((f32[4,4,16,128]{3,2,1,0:T(8,128)S(1)}, f32[4,4,16,128]{3,2,1,0:T(8,128)S(1)}, u32[]{:S(2)}, u32[]{:S(2)}) %collective-permute-start.5) | collective-permute-done | bytes 131104 | tf_op jit(solution)/shard_map/ppermute | solution.py:455
  49.2 9.1 %all-to-all-done.2.got_ref = f32[32,16,128]{2,1,0:T(8,128)S(1)} async-done(((f32[32,16,128]{2,1,0:T(8,128)}), f32[32,16,128]{2,1,0:T(8,128)S(1)}, u32[]{:S(2)}, u32[]{:S(2)}) %all-to-all-start.2) | async-done | bytes 262176 | tf_op jit(solution)/shard_map/all_to_all | solution.py:501
  58.3 1.1 %shard_map.189 = f32[16,24,128]{2,1,0:T(8,128)} custom-call(f32[32,16,128]{2,1,0:T(8,128)S(1)} %all-to-all-done.2.got_ref, f32[2,4,16,128]{3,2,1,0:T(8,128)S(1)} %get-tuple-element.39.refs_0_, f32[2,4,16,128]{3,2,1,0:T(8,128)S(1)} %get-tuple-element.37.refs_1_, f32[2,4,16,128]{3,2,1,0:T(8,128)S(1)} %get-tuple-element.32.refs_2_, ...), custom_call_target="tpu_custom_call" | custom-call | flops 2147483648 | bytes 2147483 | tf_op jit(solution)/shard_map/pallas_call | solution.py:467
  59.4 3.5 %all-to-all-start.3 = ((f32[16,24,128]{2,1,0:T(8,128)}), f32[16,24,128]{2,1,0:T(8,128)S(1)}, u32[]{:S(2)}, u32[]{:S(2)}) async-start(f32[16,24,128]{2,1,0:T(8,128)} %shard_map.189), calls=%async_computation.3 | async-start | bytes 393216 | tf_op jit(solution)/shard_map/all_to_all | solution.py:461
  62.9 0.0 copy-start.14
  63.0 1.4 %copy-done.14 = bf16[32,192,128]{2,1,0:T(8,128)(2,1)S(1)} copy-done((bf16[32,192,128]{2,1,0:T(8,128)(2,1)S(1)}, bf16[32,192,128]{2,1,0:T(8,128)(2,1)}, u32[]{:S(2)}) %copy-start.14) | copy-done | bytes 1572888
  64.4 1.2 %shard_map.190.point_ref = bf16[32,192,128]{2,1,0:T(8,128)(2,1)S(1)} custom-call(bf16[32,192,128]{2,1,0:T(8,128)(2,1)S(1)} %copy-done.14, bf16[32,32]{1,0:T(8,128)(2,1)S(1)} %copy-done.6, bf16[512,32]{1,0:T(8,128)(2,1)S(1)} %copy-done.9), custom_call_target="tpu_custom_call" | custom-call | flops 2147483648 | bytes 2147483 | tf_op jit(solution)/shard_map/pallas_call | solution.py:473
  65.6 0.0 copy-start.15
  65.6 1.1 %copy-done.15 = bf16[32,192,128]{2,1,0:T(8,128)(2,1)} copy-done((bf16[32,192,128]{2,1,0:T(8,128)(2,1)}, bf16[32,192,128]{2,1,0:T(8,128)(2,1)S(1)}, u32[]{:S(2)}) %copy-start.15) | copy-done | bytes 1572888
  66.7 4.9 %all-to-all-done.3.got_ref = f32[16,24,128]{2,1,0:T(8,128)S(1)} async-done(((f32[16,24,128]{2,1,0:T(8,128)}), f32[16,24,128]{2,1,0:T(8,128)S(1)}, u32[]{:S(2)}, u32[]{:S(2)}) %all-to-all-start.3) | async-done | bytes 196640 | tf_op jit(solution)/shard_map/all_to_all | solution.py:461
  71.6 0.0 collective-permute-start.6
  71.6 0.0 copy-start.16
  71.6 0.9 %shard_map.192 = f32[4,32,432]{2,1,0:T(8,128)} custom-call(f32[16,24,128]{2,1,0:T(8,128)S(1)} %all_to_all.20.got_ref, f32[16,24,128]{2,1,0:T(8,128)S(1)} %collective-permute-done.3.more_ref, f32[32,432]{1,0:T(8,128)S(1)} %bitcast.64), custom_call_target="tpu_custom_call" | custom-call | flops 2147483648 | bytes 2147483 | tf_op jit(solution)/shard_map/pallas_call | solution.py:479
  72.5 0.5 collective-permute-done.6.more_ref
  73.1 0.1 copy-done.16
  73.2 2.7 %shard_map.191 = (bf16[32,192,128]{2,1,0:T(8,128)(2,1)}, f32[4,32,432]{2,1,0:T(8,128)}) custom-call(f32[16,24,128]{2,1,0:T(8,128)S(1)} %all-to-all-done.3.got_ref, f32[16,24,128]{2,1,0:T(8,128)S(1)} %collective-permute-done.6.more_ref, bf16[32,192,128]{2,1,0:T(8,128)(2,1)S(1)} %copy-done.16, bf16[128,1024]{1,0:T(8,128)(2,1)S(1)} %copy-done.8, ...), custom_call_target="tpu_custom_call" | custom-call | flops 2147483648 | bytes 2147483 | tf_op jit(solution)/shard_map/pallas_call | solution.py:507
  (37 shorter events, 0.2 us)
Async XLA Ops:
  0.6 5.1 %copy-start = (bf16[1,32,12,16,128]{4,3,2,1,0:T(8,128)(2,1)S(1)}, bf16[1,32,12,16,128]{4,3,2,1,0:T(8,128)(2,1)}, u32[]{:S(2)}) copy-start(bf16[1,32,12,16,128]{4,3,2,1,0:T(8,128)(2,1)} %param.17) | copy-start | bytes 4718596
  0.6 5.1 %copy-start.7 = (bf16[384,512]{1,0:T(8,128)(2,1)S(1)}, bf16[384,512]{1,0:T(8,128)(2,1)}, u32[]{:S(2)}) copy-start(bf16[384,512]{1,0:T(8,128)(2,1)} %constant.27.order_ref) | copy-start | bytes 1179652
  0.7 5.0 %copy-start.8 = (bf16[128,1024]{1,0:T(8,128)(2,1)S(1)}, bf16[128,1024]{1,0:T(8,128)(2,1)}, u32[]{:S(2)}) copy-start(bf16[128,1024]{1,0:T(8,128)(2,1)} %constant.26.tz_ref) | copy-start | bytes 786436
  0.7 5.0 %copy-start.10 = (bf16[8,32,160]{2,1,0:T(8,128)(2,1)S(1)}, bf16[8,32,160]{2,1,0:T(8,128)(2,1)}, u32[]{:S(2)}) copy-start(bf16[8,32,160]{2,1,0:T(8,128)(2,1)} %constant.17.clone.ry_ref) | copy-start | bytes 245764
  0.7 5.0 %copy-start.11 = (bf16[8,24,160]{2,1,0:T(8,128)(2,1)S(1)}, bf16[8,24,160]{2,1,0:T(8,128)(2,1)}, u32[]{:S(2)}) copy-start(bf16[8,24,160]{2,1,0:T(8,128)(2,1)} %constant.16.clone.rx_ref) | copy-start | bytes 184324
  0.7 5.0 %copy-start.12 = (bf16[32,192]{1,0:T(8,128)(2,1)S(1)}, bf16[32,192]{1,0:T(8,128)(2,1)}, u32[]{:S(2)}) copy-start(bf16[32,192]{1,0:T(8,128)(2,1)} %constant.29.ey_ref) | copy-start | bytes 36868
  0.7 5.0 %copy-start.13 = (bf16[24,192]{1,0:T(8,128)(2,1)S(1)}, bf16[24,192]{1,0:T(8,128)(2,1)}, u32[]{:S(2)}) copy-start(bf16[24,192]{1,0:T(8,128)(2,1)} %constant.28.ex_ref) | copy-start | bytes 27652
  2.7 11.6 %collective-permute-start = (f32[2,2,2,4,16,128]{5,4,3,2,1,0:T(8,128)S(1)}, f32[2,2,2,4,16,128]{5,4,3,2,1,0:T(8,128)S(1)}, u32[]{:S(2)}, u32[]{:S(2)}) collective-permute-start(f32[2,2,2,4,16,128]{5,4,3,2,1,0:T(8,128)S(1)} %get-tuple-element.15), channel_id=1, source_target_pairs={{0,2},{1,3},{2,0},{3,1},{4,6},{5,7},{6,4},{7,5},{8,10},{9,11},{10,... | collective-permute-start | bytes 786440 | tf_op jit(solution)/shard_map/ppermute | solution.py:438
  9.3 15.5 %all-to-all-start = ((f32[32,16,128]{2,1,0:T(8,128)}), f32[32,16,128]{2,1,0:T(8,128)S(1)}, u32[]{:S(2)}, u32[]{:S(2)}) async-start(f32[32,16,128]{2,1,0:T(8,128)} %get-tuple-element.13), calls=%async_computation | async-start | bytes 524288 | tf_op jit(solution)/shard_map/all_to_all | solution.py:490
  14.3 7.7 %collective-permute-start.1 = (f32[2,2,4,16,128]{4,3,2,1,0:T(8,128)S(1)}, f32[2,2,4,16,128]{4,3,2,1,0:T(8,128)S(1)}, u32[]{:S(2)}, u32[]{:S(2)}) collective-permute-start(f32[2,2,4,16,128]{4,3,2,1,0:T(8,128)S(1)} %pad_maximum_fusion), channel_id=1, source_target_pairs={{0,4},{1,5},{2,6},{3,7},{4,0},{5,1},{6,2},{7,3},{8,12},{9,13},{10,... | collective-permute-start | bytes 393224 | tf_op jit(solution)/shard_map/ppermute | solution.py:438
  22.1 2.7 %collective-permute-start.2 = (f32[4,4,16,128]{3,2,1,0:T(8,128)S(1)}, f32[4,4,16,128]{3,2,1,0:T(8,128)S(1)}, u32[]{:S(2)}, u32[]{:S(2)}) collective-permute-start(f32[4,4,16,128]{3,2,1,0:T(8,128)S(1)} %pad_maximum_fusion.1), channel_id=1, source_target_pairs={{0,1},{1,0},{2,3},{3,2},{4,5},{5,4},{6,7},{7,6},{8,9},{9,8},{10,11... | collective-permute-start | bytes 393224 | tf_op jit(solution)/shard_map/ppermute | solution.py:455
  24.8 14.2 %copy-start.1 = (bf16[1,32,12,16,128]{4,3,2,1,0:T(8,128)(2,1)S(1)}, bf16[1,32,12,16,128]{4,3,2,1,0:T(8,128)(2,1)}, u32[]{:S(2)}) copy-start(bf16[1,32,12,16,128]{4,3,2,1,0:T(8,128)(2,1)} %param.18) | copy-start | bytes 4718596
  24.8 14.2 %copy-start.5 = (bf16[32,32]{1,0:T(8,128)(2,1)S(1)}, bf16[32,32]{1,0:T(8,128)(2,1)}, u32[]{:S(2)}) copy-start(bf16[32,32]{1,0:T(8,128)(2,1)} %refs_2_.1) | copy-start | bytes 6148
  24.8 14.2 %copy-start.9 = (bf16[512,32]{1,0:T(8,128)(2,1)S(1)}, bf16[512,32]{1,0:T(8,128)(2,1)}, u32[]{:S(2)}) copy-start(bf16[512,32]{1,0:T(8,128)(2,1)} %constant.30.refs_3_.refs_2_) | copy-start | bytes 98308
  39.0 2.2 %copy-start.2 = (bf16[1,32,12,16,128]{4,3,2,1,0:T(8,128)(2,1)S(1)}, bf16[1,32,12,16,128]{4,3,2,1,0:T(8,128)(2,1)}, u32[]{:S(2)}) copy-start(bf16[1,32,12,16,128]{4,3,2,1,0:T(8,128)(2,1)} %param.19) | copy-start | bytes 4718596
  39.0 2.2 %copy-start.17 = (bf16[320,192]{1,0:T(8,128)(2,1)S(1)}, bf16[320,192]{1,0:T(8,128)(2,1)}, u32[]{:S(2)}) copy-start(bf16[320,192]{1,0:T(8,128)(2,1)} %get-tuple-element.18.table_ref) | copy-start | bytes 368644
  39.0 2.2 %copy-start.18 = (bf16[192,160]{1,0:T(8,128)(2,1)S(1)}, bf16[192,160]{1,0:T(8,128)(2,1)}, u32[]{:S(2)}) copy-start(bf16[192,160]{1,0:T(8,128)(2,1)} %get-tuple-element.17.turned_ref) | copy-start | bytes 184324
  39.0 2.2 %collective-permute-start.3 = (f32[16,24,128]{2,1,0:T(8,128)S(1)}, f32[16,24,128]{2,1,0:T(8,128)S(1)}, u32[]{:S(2)}, u32[]{:S(2)}) collective-permute-start(f32[16,24,128]{2,1,0:T(8,128)S(1)} %all_to_all.20.got_ref), channel_id=1, source_target_pairs={{0,1},{1,0},{2,3},{3,2},{4,5},{5,4},{6,7},{7,6},{8,9},{9,8},{10,11... | collective-permute-start | bytes 589832 | tf_op jit(solution)/shard_map/ppermute | solution.py:464
  40.3 7.4 %collective-permute-start.4 = (f32[2,2,4,16,128]{4,3,2,1,0:T(8,128)S(1)}, f32[2,2,4,16,128]{4,3,2,1,0:T(8,128)S(1)}, u32[]{:S(2)}, u32[]{:S(2)}) collective-permute-start(f32[2,2,4,16,128]{4,3,2,1,0:T(8,128)S(1)} %pad_maximum_fusion.2), channel_id=1, source_target_pairs={{0,4},{1,5},{2,6},{3,7},{4,0},{5,1},{6,2},{7,3},{8,12},{9,13},{10,... | collective-permute-start | bytes 393224 | tf_op jit(solution)/shard_map/ppermute | solution.py:438
  41.2 6.5 %copy-start.19 = (f32[1,4,16,128]{3,2,1,0:T(8,128)S(1)}, f32[1,4,16,128]{3,2,1,0:T(8,128)}, u32[]{:S(2)}) copy-start(f32[1,4,16,128]{3,2,1,0:T(8,128)} %get-tuple-element.27) | copy-start | bytes 98308
  45.0 13.3 %all-to-all-start.2 = ((f32[32,16,128]{2,1,0:T(8,128)}), f32[32,16,128]{2,1,0:T(8,128)S(1)}, u32[]{:S(2)}, u32[]{:S(2)}) async-start(f32[32,16,128]{2,1,0:T(8,128)} %get-tuple-element.19), calls=%async_computation.2 | async-start | bytes 524288 | tf_op jit(solution)/shard_map/all_to_all | solution.py:501
  47.8 1.4 %collective-permute-start.5 = (f32[4,4,16,128]{3,2,1,0:T(8,128)S(1)}, f32[4,4,16,128]{3,2,1,0:T(8,128)S(1)}, u32[]{:S(2)}, u32[]{:S(2)}) collective-permute-start(f32[4,4,16,128]{3,2,1,0:T(8,128)S(1)} %pad_maximum_fusion.3), channel_id=1, source_target_pairs={{0,1},{1,0},{2,3},{3,2},{4,5},{5,4},{6,7},{7,6},{8,9},{9,8},{10,11... | collective-permute-start | bytes 393224 | tf_op jit(solution)/shard_map/ppermute | solution.py:455
  58.3 4.7 %copy-start.6 = (bf16[32,32]{1,0:T(8,128)(2,1)S(1)}, bf16[32,32]{1,0:T(8,128)(2,1)}, u32[]{:S(2)}) copy-start(bf16[32,32]{1,0:T(8,128)(2,1)} %refs_1_.1) | copy-start | bytes 6148
  59.4 12.2 %all-to-all-start.3 = ((f32[16,24,128]{2,1,0:T(8,128)}), f32[16,24,128]{2,1,0:T(8,128)S(1)}, u32[]{:S(2)}, u32[]{:S(2)}) async-start(f32[16,24,128]{2,1,0:T(8,128)} %shard_map.189), calls=%async_computation.3 | async-start | bytes 393216 | tf_op jit(solution)/shard_map/all_to_all | solution.py:461
  62.9 1.4 %copy-start.14 = (bf16[32,192,128]{2,1,0:T(8,128)(2,1)S(1)}, bf16[32,192,128]{2,1,0:T(8,128)(2,1)}, u32[]{:S(2)}) copy-start(bf16[32,192,128]{2,1,0:T(8,128)(2,1)} %get-tuple-element.20.refs_0_) | copy-start | bytes 4718596
  64.4 7.3 %copy-start.3 = (f32[1,432,32]{1,2,0:T(8,128)S(1)}, f32[1,432,32]{1,2,0:T(8,128)}, u32[]{:S(2)}) copy-start(f32[1,432,32]{1,2,0:T(8,128)} %param.24) | copy-start | bytes 165892
  65.6 1.1 %copy-start.15 = (bf16[32,192,128]{2,1,0:T(8,128)(2,1)}, bf16[32,192,128]{2,1,0:T(8,128)(2,1)S(1)}, u32[]{:S(2)}) copy-start(bf16[32,192,128]{2,1,0:T(8,128)(2,1)S(1)} %shard_map.190.point_ref) | copy-start | bytes 4718596
  71.6 1.4 %collective-permute-start.6 = (f32[16,24,128]{2,1,0:T(8,128)S(1)}, f32[16,24,128]{2,1,0:T(8,128)S(1)}, u32[]{:S(2)}, u32[]{:S(2)}) collective-permute-start(f32[16,24,128]{2,1,0:T(8,128)S(1)} %all-to-all-done.3.got_ref), channel_id=1, source_target_pairs={{0,1},{1,0},{2,3},{3,2},{4,5},{5,4},{6,7},{7,6},{8,9},{9,8},{10,11... | collective-permute-start | bytes 589832 | tf_op jit(solution)/shard_map/ppermute | solution.py:464
  71.6 1.4 %copy-start.4 = (f32[1,432,32]{1,2,0:T(8,128)S(1)}, f32[1,432,32]{1,2,0:T(8,128)}, u32[]{:S(2)}) copy-start(f32[1,432,32]{1,2,0:T(8,128)} %param.25) | copy-start | bytes 165892
  71.6 1.5 %copy-start.16 = (bf16[32,192,128]{2,1,0:T(8,128)(2,1)S(1)}, bf16[32,192,128]{2,1,0:T(8,128)(2,1)}, u32[]{:S(2)}) copy-start(bf16[32,192,128]{2,1,0:T(8,128)(2,1)} %copy-done.15) | copy-start | bytes 4718596

commit v5 on v4

--- a/solution.py
+++ b/solution.py
@@ -294,9 +294,10 @@
     p = plan
     place_ref = place_of(p)
     w_refs, cross_ref, out_ref, modes_ref = refs[: p.chips], *refs[p.chips :]
-    total = got_ref[0]
-    for d in range(1, p.devices):
-        total = total + got_ref[d]
+    sums = [got_ref[d] for d in range(p.devices)]
+    while len(sums) > 1:
+        sums = [sum(sums[n + 1 : n + 2], sums[n]) for n in range(0, len(sums), 2)]
+    total = sums[0]
     down = total.T
     ks = [down[k * p.c : (k + 1) * p.c, :] for k in range(p.per_row)]
     modes = jnp.concatenate(ks * p.fold, axis=1)

time: 76.3 us -> 76.3 us (level)
  no operation moved by 1% of the time
where the time goes in v5:
time: 76.3 us; the launch traced here: 75.8 us
  waiting for transfers between devices  23.5 us (31%)
  starting transfers between devices  17.3 us (23%)
  Pallas kernels  16.7 us (22%)
  blocking collectives  13.7 us (18%)
  local copies, waits for them, and re-layouts  3.45 us (5%)
  between operations  1.01 us (1%)
    all_to_all x1, blocking collectives, exchange(): return lax.all_to_all(parts, BOTH, 0, 0, tiled=True, axis_index_groups=same)  13.7 us
    all_to_all x1, waiting for transfers between devices, local(): got_one = lax.all_to_all(part_one, BOTH, 0, 0, tiled=True)  9.1 us
    ppermute x3, starting transfers between devices, swap(): lax.ppermute(blocks, 'tile', [(i, i ^ 2 * bit) for i in range(p.tiles)])  5.76 us
    ppermute x3, waiting for transfers between devices, swap(): lax.ppermute(blocks, 'tile', [(i, i ^ 2 * bit) for i in range(p.tiles)])  5.26 us
    all_to_all x1, starting transfers between devices, local(): got_two = lax.all_to_all(part_two, BOTH, 0, 0, tiled=True)  4.93 us
    all_to_all x1, waiting for transfers between devices, exchange(): return lax.all_to_all(parts, BOTH, 0, 0, tiled=True, axis_index_groups=same)  4.89 us
    pallas_call x1, Pallas kernels, local(): call(synth_analyse_body, p, [(field, BF16), (slots, F32)], [g_scr, s_scr,...  3.74 us
    all_to_all x1, starting transfers between devices, exchange(): return lax.all_to_all(parts, BOTH, 0, 0, tiled=True, axis_index_groups=same)  3.52 us
  transfers between devices with their start and end apart: 10, of which 6 were waited for; matrix products, arithmetic and copies ran while one was open for 1% of the time, Pallas kernels for 14%

profile of v5, /device:TPU:0, one launch (start us, length us, event | category | flops | bytes accessed | tf_op | source)
XLA Modules:
  0.0 75.8 jit_solution(193014668044014832)
XLA Ops:
  0.6 0.0 copy-start.7
  0.7 0.0 copy-start.8
  0.7 0.0 copy-start.10
  0.7 0.0 copy-start.11
  0.7 0.0 copy-start.12
  0.7 0.0 copy-start.13
  0.7 1.9 %shard_map.185 = (f32[2,2,2,4,16,128]{5,4,3,2,1,0:T(8,128)S(1)}, f32[2,2,4,16,128]{4,3,2,1,0:T(8,128)S(1)}, f32[2,2,4,16,128]{4,3,2,1,0:T(8,128)S(1)}) custom-call(f32[4,32,432]{2,1,0:T(8,128)} %bitcast.67, f32[4,32,432]{2,1,0:T(8,128)} %bitcast.68, s32[4,1,512]{2,1,0:T(1,128)} %constant.23.clone.target_hbm), custom_call_target="tpu_custom_call" | custom-call | flops 2147483648 | bytes 2147483 | tf_op jit(solution)/shard_map/pallas_call | solution.py:426
  2.7 3.0 %collective-permute-start = (f32[2,2,2,4,16,128]{5,4,3,2,1,0:T(8,128)S(1)}, f32[2,2,2,4,16,128]{5,4,3,2,1,0:T(8,128)S(1)}, u32[]{:S(2)}, u32[]{:S(2)}) collective-permute-start(f32[2,2,2,4,16,128]{5,4,3,2,1,0:T(8,128)S(1)} %get-tuple-element.15), channel_id=1, source_target_pairs={{0,2},{1,3},{2,0},{3,1},{4,6},{5,7},{6,4},{7,5},{8,10},{9,11},{10,... | collective-permute-start | bytes 786440 | tf_op jit(solution)/shard_map/ppermute | solution.py:439
  5.7 0.0 copy-done
  5.7 0.0 copy-done.11
  5.7 0.0 copy-done.12
  5.7 0.0 copy-done.13
  5.7 3.5 %shard_map.184 = (f32[32,16,128]{2,1,0:T(8,128)}, bf16[320,192]{1,0:T(8,128)(2,1)}, bf16[192,160]{1,0:T(8,128)(2,1)}) custom-call(bf16[32,192,128]{2,1,0:T(8,128)(2,1)S(1)} %bitcast.59, bf16[32,192,128]{2,1,0:T(8,128)(2,1)} %bitcast.61, bf16[128,1024]{1,0:T(8,128)(2,1)S(1)} %copy-done.8, bf16[384,512]{1,0:T(8,128)(2,1)S(1)} %copy-done.7, ...), custom_call_target="tpu_custom_call" | custom-call | flops 2147483648 | bytes 2147483 | tf_op jit(solution)/shard_map/pallas_call | solution.py:483
  9.3 4.9 %all-to-all-start = ((f32[32,16,128]{2,1,0:T(8,128)}), f32[32,16,128]{2,1,0:T(8,128)S(1)}, u32[]{:S(2)}, u32[]{:S(2)}) async-start(f32[32,16,128]{2,1,0:T(8,128)} %get-tuple-element.13), calls=%async_computation | async-start | bytes 524288 | tf_op jit(solution)/shard_map/all_to_all | solution.py:491
  14.2 0.0 collective-permute-done
  14.3 1.8 %collective-permute-start.1 = (f32[2,2,4,16,128]{4,3,2,1,0:T(8,128)S(1)}, f32[2,2,4,16,128]{4,3,2,1,0:T(8,128)S(1)}, u32[]{:S(2)}, u32[]{:S(2)}) collective-permute-start(f32[2,2,4,16,128]{4,3,2,1,0:T(8,128)S(1)} %pad_maximum_fusion), channel_id=1, source_target_pairs={{0,4},{1,5},{2,6},{3,7},{4,0},{5,1},{6,2},{7,3},{8,12},{9,13},{10,... | collective-permute-start | bytes 393224 | tf_op jit(solution)/shard_map/ppermute | solution.py:439
  16.2 0.6 slice_bitcast_fusion.15
  16.8 5.3 %collective-permute-done.1 = f32[2,2,4,16,128]{4,3,2,1,0:T(8,128)S(1)} collective-permute-done((f32[2,2,4,16,128]{4,3,2,1,0:T(8,128)S(1)}, f32[2,2,4,16,128]{4,3,2,1,0:T(8,128)S(1)}, u32[]{:S(2)}, u32[]{:S(2)}) %collective-permute-start.1) | collective-permute-done | bytes 131104 | tf_op jit(solution)/shard_map/ppermute | solution.py:439
  22.1 0.1 collective-permute-start.2
  22.2 2.6 %all-to-all-done.got_ref = f32[32,16,128]{2,1,0:T(8,128)S(1)} async-done(((f32[32,16,128]{2,1,0:T(8,128)}), f32[32,16,128]{2,1,0:T(8,128)S(1)}, u32[]{:S(2)}, u32[]{:S(2)}) %all-to-all-start) | async-done | bytes 262176 | tf_op jit(solution)/shard_map/all_to_all | solution.py:491
  24.8 0.0 collective-permute-done.2.refs_4_
  24.8 0.4 shard_map.186
  25.2 13.7 %all_to_all.20.got_ref = f32[16,24,128]{2,1,0:T(8,128)S(1)} all-to-all(f32[16,24,128]{2,1,0:T(8,128)S(1)} %shard_map.186), channel_id=1, replica_groups={{0,2,4,6,8,10,12,14,16,18,20,22,24,26,28,30},{1,3,5,7,9,11,13,15,17,19,..., dimensions={0} | all-to-all | bytes 393216 | tf_op jit(solution)/shard_map/all_to_all | solution.py:462
  39.0 0.0 collective-permute-start.3
  39.0 1.2 %shard_map.187.point_ref = bf16[32,192,128]{2,1,0:T(8,128)(2,1)S(1)} custom-call(bf16[32,192,128]{2,1,0:T(8,128)(2,1)S(1)} %bitcast.60, bf16[32,192,128]{2,1,0:T(8,128)(2,1)S(1)} %bitcast.62, bf16[32,32]{1,0:T(8,128)(2,1)S(1)} %copy-done.5, bf16[512,32]{1,0:T(8,128)(2,1)S(1)} %copy-done.9), custom_call_target="tpu_custom_call" | custom-call | flops 2147483648 | bytes 2147483 | tf_op jit(solution)/shard_map/pallas_call | solution.py:474
  40.3 0.9 %collective-permute-start.4 = (f32[2,2,4,16,128]{4,3,2,1,0:T(8,128)S(1)}, f32[2,2,4,16,128]{4,3,2,1,0:T(8,128)S(1)}, u32[]{:S(2)}, u32[]{:S(2)}) collective-permute-start(f32[2,2,4,16,128]{4,3,2,1,0:T(8,128)S(1)} %pad_maximum_fusion.2), channel_id=1, source_target_pairs={{0,4},{1,5},{2,6},{3,7},{4,0},{5,1},{6,2},{7,3},{8,12},{9,13},{10,... | collective-permute-start | bytes 393224 | tf_op jit(solution)/shard_map/ppermute | solution.py:439
  41.2 0.0 collective-permute-done.3.more_ref
  41.2 0.0 copy-done.2
  41.2 3.7 %shard_map.188 = (bf16[32,192,128]{2,1,0:T(8,128)(2,1)}, f32[32,16,128]{2,1,0:T(8,128)}) custom-call(f32[16,24,128]{2,1,0:T(8,128)S(1)} %all_to_all.20.got_ref, f32[16,24,128]{2,1,0:T(8,128)S(1)} %collective-permute-done.3.more_ref, bf16[32,192,128]{2,1,0:T(8,128)(2,1)S(1)} %shard_map.187.point_ref, bf16[32,192,128]{2,1,0:T(8,128)(2,1)S(1)} %bitcast.63, ...), custom_call_target="tpu_custom_call" | custom-call | flops 2147483648 | bytes 2147483 | tf_op jit(solution)/shard_map/pallas_call | solution.py:496
  45.0 2.7 %all-to-all-start.2 = ((f32[32,16,128]{2,1,0:T(8,128)}), f32[32,16,128]{2,1,0:T(8,128)S(1)}, u32[]{:S(2)}, u32[]{:S(2)}) async-start(f32[32,16,128]{2,1,0:T(8,128)} %get-tuple-element.19), calls=%async_computation.2 | async-start | bytes 524288 | tf_op jit(solution)/shard_map/all_to_all | solution.py:502
  47.7 0.0 collective-permute-done.4
  47.7 0.3 collective-permute-start.5
  48.1 1.1 %collective-permute-done.5.refs_4_ = f32[4,4,16,128]{3,2,1,0:T(8,128)S(1)} collective-permute-done((f32[4,4,16,128]{3,2,1,0:T(8,128)S(1)}, f32[4,4,16,128]{3,2,1,0:T(8,128)S(1)}, u32[]{:S(2)}, u32[]{:S(2)}) %collective-permute-start.5) | collective-permute-done | bytes 131104 | tf_op jit(solution)/shard_map/ppermute | solution.py:456
  49.2 9.1 %all-to-all-done.2.got_ref = f32[32,16,128]{2,1,0:T(8,128)S(1)} async-done(((f32[32,16,128]{2,1,0:T(8,128)}), f32[32,16,128]{2,1,0:T(8,128)S(1)}, u32[]{:S(2)}, u32[]{:S(2)}) %all-to-all-start.2) | async-done | bytes 262176 | tf_op jit(solution)/shard_map/all_to_all | solution.py:502
  58.3 1.1 %shard_map.189 = f32[16,24,128]{2,1,0:T(8,128)} custom-call(f32[32,16,128]{2,1,0:T(8,128)S(1)} %all-to-all-done.2.got_ref, f32[2,4,16,128]{3,2,1,0:T(8,128)S(1)} %get-tuple-element.39.refs_0_, f32[2,4,16,128]{3,2,1,0:T(8,128)S(1)} %get-tuple-element.37.refs_1_, f32[2,4,16,128]{3,2,1,0:T(8,128)S(1)} %get-tuple-element.32.refs_2_, ...), custom_call_target="tpu_custom_call" | custom-call | flops 2147483648 | bytes 2147483 | tf_op jit(solution)/shard_map/pallas_call | solution.py:468
  59.4 3.5 %all-to-all-start.3 = ((f32[16,24,128]{2,1,0:T(8,128)}), f32[16,24,128]{2,1,0:T(8,128)S(1)}, u32[]{:S(2)}, u32[]{:S(2)}) async-start(f32[16,24,128]{2,1,0:T(8,128)} %shard_map.189), calls=%async_computation.3 | async-start | bytes 393216 | tf_op jit(solution)/shard_map/all_to_all | solution.py:462
  62.9 0.0 copy-start.14
  62.9 1.4 %copy-done.14 = bf16[32,192,128]{2,1,0:T(8,128)(2,1)S(1)} copy-done((bf16[32,192,128]{2,1,0:T(8,128)(2,1)S(1)}, bf16[32,192,128]{2,1,0:T(8,128)(2,1)}, u32[]{:S(2)}) %copy-start.14) | copy-done | bytes 1572888
  64.3 1.2 %shard_map.190.point_ref = bf16[32,192,128]{2,1,0:T(8,128)(2,1)S(1)} custom-call(bf16[32,192,128]{2,1,0:T(8,128)(2,1)S(1)} %copy-done.14, bf16[32,32]{1,0:T(8,128)(2,1)S(1)} %copy-done.6, bf16[512,32]{1,0:T(8,128)(2,1)S(1)} %copy-done.9), custom_call_target="tpu_custom_call" | custom-call | flops 2147483648 | bytes 2147483 | tf_op jit(solution)/shard_map/pallas_call | solution.py:474
  65.5 0.0 copy-start.15
  65.5 1.1 %copy-done.15 = bf16[32,192,128]{2,1,0:T(8,128)(2,1)} copy-done((bf16[32,192,128]{2,1,0:T(8,128)(2,1)}, bf16[32,192,128]{2,1,0:T(8,128)(2,1)S(1)}, u32[]{:S(2)}) %copy-start.15) | copy-done | bytes 1572888
  66.7 4.9 %all-to-all-done.3.got_ref = f32[16,24,128]{2,1,0:T(8,128)S(1)} async-done(((f32[16,24,128]{2,1,0:T(8,128)}), f32[16,24,128]{2,1,0:T(8,128)S(1)}, u32[]{:S(2)}, u32[]{:S(2)}) %all-to-all-start.3) | async-done | bytes 196640 | tf_op jit(solution)/shard_map/all_to_all | solution.py:462
  71.6 0.0 collective-permute-start.6
  71.6 0.0 copy-start.16
  71.6 0.9 %shard_map.192 = f32[4,32,432]{2,1,0:T(8,128)} custom-call(f32[16,24,128]{2,1,0:T(8,128)S(1)} %all_to_all.20.got_ref, f32[16,24,128]{2,1,0:T(8,128)S(1)} %collective-permute-done.3.more_ref, f32[32,432]{1,0:T(8,128)S(1)} %bitcast.64), custom_call_target="tpu_custom_call" | custom-call | flops 2147483648 | bytes 2147483 | tf_op jit(solution)/shard_map/pallas_call | solution.py:480
  72.5 0.5 collective-permute-done.6.more_ref
  73.0 0.1 copy-done.16
  73.1 2.7 %shard_map.191 = (bf16[32,192,128]{2,1,0:T(8,128)(2,1)}, f32[4,32,432]{2,1,0:T(8,128)}) custom-call(f32[16,24,128]{2,1,0:T(8,128)S(1)} %all-to-all-done.3.got_ref, f32[16,24,128]{2,1,0:T(8,128)S(1)} %collective-permute-done.6.more_ref, bf16[32,192,128]{2,1,0:T(8,128)(2,1)S(1)} %copy-done.16, bf16[128,1024]{1,0:T(8,128)(2,1)S(1)} %copy-done.8, ...), custom_call_target="tpu_custom_call" | custom-call | flops 2147483648 | bytes 2147483 | tf_op jit(solution)/shard_map/pallas_call | solution.py:508
  (37 shorter events, 0.2 us)
Async XLA Ops:
  0.6 5.1 %copy-start = (bf16[1,32,12,16,128]{4,3,2,1,0:T(8,128)(2,1)S(1)}, bf16[1,32,12,16,128]{4,3,2,1,0:T(8,128)(2,1)}, u32[]{:S(2)}) copy-start(bf16[1,32,12,16,128]{4,3,2,1,0:T(8,128)(2,1)} %param.17) | copy-start | bytes 4718596
  0.6 5.1 %copy-start.7 = (bf16[384,512]{1,0:T(8,128)(2,1)S(1)}, bf16[384,512]{1,0:T(8,128)(2,1)}, u32[]{:S(2)}) copy-start(bf16[384,512]{1,0:T(8,128)(2,1)} %constant.27.order_ref) | copy-start | bytes 1179652
  0.7 5.0 %copy-start.8 = (bf16[128,1024]{1,0:T(8,128)(2,1)S(1)}, bf16[128,1024]{1,0:T(8,128)(2,1)}, u32[]{:S(2)}) copy-start(bf16[128,1024]{1,0:T(8,128)(2,1)} %constant.26.tz_ref) | copy-start | bytes 786436
  0.7 5.0 %copy-start.10 = (bf16[8,32,160]{2,1,0:T(8,128)(2,1)S(1)}, bf16[8,32,160]{2,1,0:T(8,128)(2,1)}, u32[]{:S(2)}) copy-start(bf16[8,32,160]{2,1,0:T(8,128)(2,1)} %constant.17.clone.ry_ref) | copy-start | bytes 245764
  0.7 5.0 %copy-start.11 = (bf16[8,24,160]{2,1,0:T(8,128)(2,1)S(1)}, bf16[8,24,160]{2,1,0:T(8,128)(2,1)}, u32[]{:S(2)}) copy-start(bf16[8,24,160]{2,1,0:T(8,128)(2,1)} %constant.16.clone.rx_ref) | copy-start | bytes 184324
  0.7 5.0 %copy-start.12 = (bf16[32,192]{1,0:T(8,128)(2,1)S(1)}, bf16[32,192]{1,0:T(8,128)(2,1)}, u32[]{:S(2)}) copy-start(bf16[32,192]{1,0:T(8,128)(2,1)} %constant.29.ey_ref) | copy-start | bytes 36868
  0.7 5.0 %copy-start.13 = (bf16[24,192]{1,0:T(8,128)(2,1)S(1)}, bf16[24,192]{1,0:T(8,128)(2,1)}, u32[]{:S(2)}) copy-start(bf16[24,192]{1,0:T(8,128)(2,1)} %constant.28.ex_ref) | copy-start | bytes 27652
  2.7 11.6 %collective-permute-start = (f32[2,2,2,4,16,128]{5,4,3,2,1,0:T(8,128)S(1)}, f32[2,2,2,4,16,128]{5,4,3,2,1,0:T(8,128)S(1)}, u32[]{:S(2)}, u32[]{:S(2)}) collective-permute-start(f32[2,2,2,4,16,128]{5,4,3,2,1,0:T(8,128)S(1)} %get-tuple-element.15), channel_id=1, source_target_pairs={{0,2},{1,3},{2,0},{3,1},{4,6},{5,7},{6,4},{7,5},{8,10},{9,11},{10,... | collective-permute-start | bytes 786440 | tf_op jit(solution)/shard_map/ppermute | solution.py:439
  9.3 15.5 %all-to-all-start = ((f32[32,16,128]{2,1,0:T(8,128)}), f32[32,16,128]{2,1,0:T(8,128)S(1)}, u32[]{:S(2)}, u32[]{:S(2)}) async-start(f32[32,16,128]{2,1,0:T(8,128)} %get-tuple-element.13), calls=%async_computation | async-start | bytes 524288 | tf_op jit(solution)/shard_map/all_to_all | solution.py:491
  14.3 7.7 %collective-permute-start.1 = (f32[2,2,4,16,128]{4,3,2,1,0:T(8,128)S(1)}, f32[2,2,4,16,128]{4,3,2,1,0:T(8,128)S(1)}, u32[]{:S(2)}, u32[]{:S(2)}) collective-permute-start(f32[2,2,4,16,128]{4,3,2,1,0:T(8,128)S(1)} %pad_maximum_fusion), channel_id=1, source_target_pairs={{0,4},{1,5},{2,6},{3,7},{4,0},{5,1},{6,2},{7,3},{8,12},{9,13},{10,... | collective-permute-start | bytes 393224 | tf_op jit(solution)/shard_map/ppermute | solution.py:439
  22.1 2.7 %collective-permute-start.2 = (f32[4,4,16,128]{3,2,1,0:T(8,128)S(1)}, f32[4,4,16,128]{3,2,1,0:T(8,128)S(1)}, u32[]{:S(2)}, u32[]{:S(2)}) collective-permute-start(f32[4,4,16,128]{3,2,1,0:T(8,128)S(1)} %pad_maximum_fusion.1), channel_id=1, source_target_pairs={{0,1},{1,0},{2,3},{3,2},{4,5},{5,4},{6,7},{7,6},{8,9},{9,8},{10,11... | collective-permute-start | bytes 393224 | tf_op jit(solution)/shard_map/ppermute | solution.py:456
  24.8 14.2 %copy-start.1 = (bf16[1,32,12,16,128]{4,3,2,1,0:T(8,128)(2,1)S(1)}, bf16[1,32,12,16,128]{4,3,2,1,0:T(8,128)(2,1)}, u32[]{:S(2)}) copy-start(bf16[1,32,12,16,128]{4,3,2,1,0:T(8,128)(2,1)} %param.18) | copy-start | bytes 4718596
  24.8 14.2 %copy-start.5 = (bf16[32,32]{1,0:T(8,128)(2,1)S(1)}, bf16[32,32]{1,0:T(8,128)(2,1)}, u32[]{:S(2)}) copy-start(bf16[32,32]{1,0:T(8,128)(2,1)} %refs_2_.1) | copy-start | bytes 6148
  24.8 14.2 %copy-start.9 = (bf16[512,32]{1,0:T(8,128)(2,1)S(1)}, bf16[512,32]{1,0:T(8,128)(2,1)}, u32[]{:S(2)}) copy-start(bf16[512,32]{1,0:T(8,128)(2,1)} %constant.30.refs_3_.refs_2_) | copy-start | bytes 98308
  39.0 2.2 %copy-start.2 = (bf16[1,32,12,16,128]{4,3,2,1,0:T(8,128)(2,1)S(1)}, bf16[1,32,12,16,128]{4,3,2,1,0:T(8,128)(2,1)}, u32[]{:S(2)}) copy-start(bf16[1,32,12,16,128]{4,3,2,1,0:T(8,128)(2,1)} %param.19) | copy-start | bytes 4718596
  39.0 2.2 %copy-start.17 = (bf16[320,192]{1,0:T(8,128)(2,1)S(1)}, bf16[320,192]{1,0:T(8,128)(2,1)}, u32[]{:S(2)}) copy-start(bf16[320,192]{1,0:T(8,128)(2,1)} %get-tuple-element.18.table_ref) | copy-start | bytes 368644
  39.0 2.2 %copy-start.18 = (bf16[192,160]{1,0:T(8,128)(2,1)S(1)}, bf16[192,160]{1,0:T(8,128)(2,1)}, u32[]{:S(2)}) copy-start(bf16[192,160]{1,0:T(8,128)(2,1)} %get-tuple-element.17.turned_ref) | copy-start | bytes 184324
  39.0 2.2 %collective-permute-start.3 = (f32[16,24,128]{2,1,0:T(8,128)S(1)}, f32[16,24,128]{2,1,0:T(8,128)S(1)}, u32[]{:S(2)}, u32[]{:S(2)}) collective-permute-start(f32[16,24,128]{2,1,0:T(8,128)S(1)} %all_to_all.20.got_ref), channel_id=1, source_target_pairs={{0,1},{1,0},{2,3},{3,2},{4,5},{5,4},{6,7},{7,6},{8,9},{9,8},{10,11... | collective-permute-start | bytes 589832 | tf_op jit(solution)/shard_map/ppermute | solution.py:465
  40.3 7.4 %collective-permute-start.4 = (f32[2,2,4,16,128]{4,3,2,1,0:T(8,128)S(1)}, f32[2,2,4,16,128]{4,3,2,1,0:T(8,128)S(1)}, u32[]{:S(2)}, u32[]{:S(2)}) collective-permute-start(f32[2,2,4,16,128]{4,3,2,1,0:T(8,128)S(1)} %pad_maximum_fusion.2), channel_id=1, source_target_pairs={{0,4},{1,5},{2,6},{3,7},{4,0},{5,1},{6,2},{7,3},{8,12},{9,13},{10,... | collective-permute-start | bytes 393224 | tf_op jit(solution)/shard_map/ppermute | solution.py:439
  41.2 6.5 %copy-start.19 = (f32[1,4,16,128]{3,2,1,0:T(8,128)S(1)}, f32[1,4,16,128]{3,2,1,0:T(8,128)}, u32[]{:S(2)}) copy-start(f32[1,4,16,128]{3,2,1,0:T(8,128)} %get-tuple-element.27) | copy-start | bytes 98308
  45.0 13.3 %all-to-all-start.2 = ((f32[32,16,128]{2,1,0:T(8,128)}), f32[32,16,128]{2,1,0:T(8,128)S(1)}, u32[]{:S(2)}, u32[]{:S(2)}) async-start(f32[32,16,128]{2,1,0:T(8,128)} %get-tuple-element.19), calls=%async_computation.2 | async-start | bytes 524288 | tf_op jit(solution)/shard_map/all_to_all | solution.py:502
  47.7 1.4 %collective-permute-start.5 = (f32[4,4,16,128]{3,2,1,0:T(8,128)S(1)}, f32[4,4,16,128]{3,2,1,0:T(8,128)S(1)}, u32[]{:S(2)}, u32[]{:S(2)}) collective-permute-start(f32[4,4,16,128]{3,2,1,0:T(8,128)S(1)} %pad_maximum_fusion.3), channel_id=1, source_target_pairs={{0,1},{1,0},{2,3},{3,2},{4,5},{5,4},{6,7},{7,6},{8,9},{9,8},{10,11... | collective-permute-start | bytes 393224 | tf_op jit(solution)/shard_map/ppermute | solution.py:456
  58.3 4.6 %copy-start.6 = (bf16[32,32]{1,0:T(8,128)(2,1)S(1)}, bf16[32,32]{1,0:T(8,128)(2,1)}, u32[]{:S(2)}) copy-start(bf16[32,32]{1,0:T(8,128)(2,1)} %refs_1_.1) | copy-start | bytes 6148
  59.4 12.2 %all-to-all-start.3 = ((f32[16,24,128]{2,1,0:T(8,128)}), f32[16,24,128]{2,1,0:T(8,128)S(1)}, u32[]{:S(2)}, u32[]{:S(2)}) async-start(f32[16,24,128]{2,1,0:T(8,128)} %shard_map.189), calls=%async_computation.3 | async-start | bytes 393216 | tf_op jit(solution)/shard_map/all_to_all | solution.py:462
  62.9 1.4 %copy-start.14 = (bf16[32,192,128]{2,1,0:T(8,128)(2,1)S(1)}, bf16[32,192,128]{2,1,0:T(8,128)(2,1)}, u32[]{:S(2)}) copy-start(bf16[32,192,128]{2,1,0:T(8,128)(2,1)} %get-tuple-element.20.refs_0_) | copy-start | bytes 4718596
  64.3 7.3 %copy-start.3 = (f32[1,432,32]{1,2,0:T(8,128)S(1)}, f32[1,432,32]{1,2,0:T(8,128)}, u32[]{:S(2)}) copy-start(f32[1,432,32]{1,2,0:T(8,128)} %param.24) | copy-start | bytes 165892
  65.5 1.1 %copy-start.15 = (bf16[32,192,128]{2,1,0:T(8,128)(2,1)}, bf16[32,192,128]{2,1,0:T(8,128)(2,1)S(1)}, u32[]{:S(2)}) copy-start(bf16[32,192,128]{2,1,0:T(8,128)(2,1)S(1)} %shard_map.190.point_ref) | copy-start | bytes 4718596
  71.6 1.4 %collective-permute-start.6 = (f32[16,24,128]{2,1,0:T(8,128)S(1)}, f32[16,24,128]{2,1,0:T(8,128)S(1)}, u32[]{:S(2)}, u32[]{:S(2)}) collective-permute-start(f32[16,24,128]{2,1,0:T(8,128)S(1)} %all-to-all-done.3.got_ref), channel_id=1, source_target_pairs={{0,1},{1,0},{2,3},{3,2},{4,5},{5,4},{6,7},{7,6},{8,9},{9,8},{10,11... | collective-permute-start | bytes 589832 | tf_op jit(solution)/shard_map/ppermute | solution.py:465
  71.6 1.4 %copy-start.4 = (f32[1,432,32]{1,2,0:T(8,128)S(1)}, f32[1,432,32]{1,2,0:T(8,128)}, u32[]{:S(2)}) copy-start(f32[1,432,32]{1,2,0:T(8,128)} %param.25) | copy-start | bytes 165892
  71.6 1.5 %copy-start.16 = (bf16[32,192,128]{2,1,0:T(8,128)(2,1)S(1)}, bf16[32,192,128]{2,1,0:T(8,128)(2,1)}, u32[]{:S(2)}) copy-start(bf16[32,192,128]{2,1,0:T(8,128)(2,1)} %copy-done.15) | copy-start | bytes 4718596
